TPU v7x, 256 devices: a whole 4x4x8 slice. The times are simulated.
256 devices in a mesh: firm: 16 (over y_lo, z), tm: 16 (over x, y_hi, core).
Axes of the slice: x: 4, y: 4 (y_hi: 2, y_lo: 2; y = y_hi * 2 + y_lo), z: 8, core: 2. Of those that a mesh axis runs over, the one named last changes fastest.
Arguments:
- features: bfloat16 [8192, 32, 128], P('firm', 'tm'), may hold values from -6 to 6
- cotangent: bfloat16 [8192, 32, 128], P('firm', 'tm'), may hold values from -6 to 6
- tiles: bfloat16 [64, 64, 128, 128], P('firm'), may hold values from -0.125 to 0.125
- mask: int32 [64, 64], P('firm'), may hold values 0 or 1
- w_prev: bfloat16 [2, 128, 256], replicated, may hold values from -0.375 to 0.375
- w_cur: bfloat16 [2, 128, 256], replicated, may hold values from -0.375 to 0.375
- w_self: bfloat16 [2, 128, 128], replicated, may hold values from -0.5 to 0.5
- w_nbr: bfloat16 [2, 128, 128], replicated, may hold values from -0.5 to 0.5
- dilations: int32 [2], replicated, may hold values from 1 to 2, as said below
Outputs:
- grad_features: float32 [8192, 32, 128], P('firm', 'tm')
- grad_prev: float32 [2, 128, 256], replicated
- grad_cur: float32 [2, 128, 256], replicated
- grad_self: float32 [2, 128, 128], replicated
- grad_nbr: float32 [2, 128, 128], replicated
Inputs may be any that keep to these rules, and one draw needn't show every extreme that they name: `dilations`: each layer's dilation lies between 1 and 2; some layer has dilation 1 and some layer has dilation 2.
All inputs are finite; a program needn't handle non-finite values. No bound on the sum of `mask` on one device may be relied on, other than what follows from the above.
Results may differ from a plain program's by a relative error of at most 0.007.
Values may be sent and summed in bfloat16 or wider, within the bound.
No kernel may reach another device: no remote copies, remote signals or barrier semaphores. Data moves between devices by JAX's collectives and lax.ppermute only.
A program may use at most 128 MiB of HBM per device.

v0:
```python
import jax
import jax.numpy as jnp
from jax import lax
from jax.sharding import PartitionSpec as P

L = 2


def shifted(array, axis, by):
    peers = lax.axis_size(axis)
    pairs = [(i, i + by) for i in range(peers) if 0 <= i + by < peers]
    return lax.ppermute(array, axis, pairs)


def earlier_time_days(hidden_state, dilation_factor):
    time_days = hidden_state.shape[1]
    prior = shifted(hidden_state, "tm", 1)
    paired_terms = jnp.concatenate([prior, hidden_state], axis=1)
    return lax.dynamic_slice_in_dim(paired_terms, time_days - dilation_factor, time_days, 1)


def later_time_days(reverse_flow, dilation_factor):
    time_days = reverse_flow.shape[1]
    following = shifted(reverse_flow, "tm", -1)
    paired_terms = jnp.concatenate([reverse_flow, following], axis=1)
    return lax.dynamic_slice_in_dim(paired_terms, dilation_factor, time_days, 1)


def folder(matrix, piece):
    return jnp.dot(matrix, piece, preferred_element_type=jnp.float32)


def per_device(features, cotangent, tiles, mask, w_prev, w_cur, w_self, w_nbr, dilations):
    rows, time_days, width = features.shape
    blocks_local, blocks_all, block_size, _ = tiles.shape
    all_firms = blocks_all * block_size
    masked = tiles * mask.astype(tiles.dtype)[:, :, None, None]
    row_matrix = masked.transpose(0, 2, 1, 3).reshape(rows, all_firms)
    saved = []
    hidden_state = features
    for layer_index in range(L):
        dilation_factor = dilations[layer_index]
        previous_state = earlier_time_days(hidden_state, dilation_factor)
        pre = jnp.dot(
            previous_state.reshape(-1, width),
            w_prev[layer_index],
            preferred_element_type=jnp.float32,
        )
        pre = pre + jnp.dot(
            hidden_state.reshape(-1, width), w_cur[layer_index], preferred_element_type=jnp.float32
        )
        filt = pre[:, :width]
        gate = pre[:, width:]
        gated = (jnp.tanh(filt) * jax.nn.sigmoid(gate)).astype(jnp.bfloat16)
        diffused = folder(
            row_matrix,
            lax.all_gather(gated.reshape(rows, time_days * width), "firm", axis=0, tiled=True),
        ).astype(jnp.bfloat16)
        mixed = jnp.dot(gated, w_self[layer_index], preferred_element_type=jnp.float32)
        mixed = mixed + jnp.dot(
            diffused.reshape(-1, width), w_nbr[layer_index], preferred_element_type=jnp.float32
        )
        saved.append((hidden_state, previous_state, filt, gate, gated, diffused))
        hidden_state = (
            hidden_state.astype(jnp.float32) + mixed.reshape(rows, time_days, width)
        ).astype(jnp.bfloat16)
    gradient_value = cotangent.astype(jnp.float32)
    outs_prev, outs_cur, outs_self, outs_nbr = ([], [], [], [])
    for layer_index in reversed(range(L)):
        hidden_state, previous_state, filt, gate, gated, diffused = saved[layer_index]
        dilation_factor = dilations[layer_index]
        gzb = gradient_value.astype(jnp.bfloat16).reshape(-1, width)
        outs_self.append(jnp.dot(gated.T, gzb, preferred_element_type=jnp.float32))
        outs_nbr.append(
            jnp.dot(diffused.reshape(-1, width).T, gzb, preferred_element_type=jnp.float32)
        )
        gdiff = jnp.dot(gzb, w_nbr[layer_index].T, preferred_element_type=jnp.float32).astype(
            jnp.bfloat16
        )
        gdiff_rows = gdiff.reshape(rows, time_days * width)
        spread = lax.psum_scatter(
            lax.dot_general(
                row_matrix, gdiff_rows, (((0,), (0,)), ((), ())), preferred_element_type=jnp.float32
            ),
            "firm",
            scatter_dimension=0,
            tiled=True,
        )
        ggated = jnp.dot(
            gzb, w_self[layer_index].T, preferred_element_type=jnp.float32
        ) + spread.reshape(-1, width)
        tanh_filt = jnp.tanh(filt)
        sig_gate = jax.nn.sigmoid(gate)
        gpre = jnp.concatenate(
            [
                ggated * sig_gate * (1.0 - tanh_filt * tanh_filt),
                ggated * tanh_filt * sig_gate * (1.0 - sig_gate),
            ],
            axis=1,
        ).astype(jnp.bfloat16)
        outs_cur.append(
            jnp.dot(hidden_state.reshape(-1, width).T, gpre, preferred_element_type=jnp.float32)
        )
        outs_prev.append(
            jnp.dot(previous_state.reshape(-1, width).T, gpre, preferred_element_type=jnp.float32)
        )
        reverse_flow = jnp.dot(
            gpre, w_prev[layer_index].T, preferred_element_type=jnp.float32
        ).reshape(rows, time_days, width)
        direct_path = jnp.dot(
            gpre, w_cur[layer_index].T, preferred_element_type=jnp.float32
        ).reshape(rows, time_days, width)
        gradient_value = (
            gradient_value + direct_path + later_time_days(reverse_flow, dilation_factor)
        )
    sums = lax.psum(
        (
            jnp.stack(outs_prev[::-1]),
            jnp.stack(outs_cur[::-1]),
            jnp.stack(outs_self[::-1]),
            jnp.stack(outs_nbr[::-1]),
        ),
        ("firm", "tm"),
    )
    factor = 1.0 / jnp.sqrt(jnp.float32(all_firms * time_days * lax.axis_size("tm")))
    return (gradient_value, sums[0] * factor, sums[1] * factor, sums[2] * factor, sums[3] * factor)


def solution(mesh):
    in_specs = (
        P("firm", "tm", None),
        P("firm", "tm", None),
        P("firm", None, None, None),
        P("firm", None),
        P(),
        P(),
        P(),
        P(),
        P(),
    )
    out_specs = (P("firm", "tm", None), P(), P(), P(), P())
    return jax.shard_map(
        per_device, mesh=mesh, in_specs=in_specs, out_specs=out_specs, check_vma=False
    )
```

profile of v0, /device:TPU:97, one launch (start us, length us, event | category | flops | bytes accessed | tf_op | source)
XLA Modules:
  0.0 658.3 jit_solution(12701526937728373321)
XLA Ops:
  7.2 5.4 collective-permute-start
  12.6 1.3 fusion.67
  15.2 1.2 fusion.39
  16.4 1.9 fusion.29
  18.4 1.2 convolution_add_fusion.1
  21.3 7.2 %multiply_bitcast_fusion = bf16[4,128,64,128]{3,1,2,0:T(8,128)(2,1)} fusion(bf16[4,64,128,128]{3,2,1,0:T(8,128)(2,1)} %param.11, bf16[4,64]{1,0:T(4,128)(2,1)S(1)} %convert_element_type.41), kind=kLoop, calls=%fused_computation.8 | loop fusion | flops 4194304 | bytes 16777728 | tf_op jit(solution)/shard_map/transpose | solution.py:38
  28.6 12.1 %copy.22 = bf16[4,128,64,128]{3,2,1,0:T(8,128)(2,1)} copy(bf16[4,128,64,128]{3,1,2,0:T(8,128)(2,1)} %multiply_bitcast_fusion) | data formatting | bytes 16777216 | tf_op jit(solution)/shard_map/transpose | solution.py:38
  41.0 24.6 %fusion.6 = f32[8192,256]{1,0:T(8,128)} fusion(bf16[512,256]{1,0:T(8,128)(2,1)S(1)} %reshape.86, bf16[64,8,64,128]{3,2,1,0:T(8,128)(2,1)} %bitcast.124), kind=kOutput, calls=%fused_computation.6 | convolution fusion | flops 2147483648 | bytes 17039360 | tf_op jit(solution)/shard_map/dot_general | solution.py:82
  66.7 19.3 %all-gather.3.cloned.1.call-done = bf16[8192,256]{1,0:T(8,128)(2,1)} async-done(((bf16[512,256]{1,0:T(8,128)(2,1)}), bf16[8192,256]{1,0:T(8,128)(2,1)}) %all-gather.3.cloned.1.call-update) | async-done | bytes 4194320 | tf_op jit(solution)/shard_map/all_gather | solution.py:57
  86.1 9.3 %fusion.13 = bf16[512,256]{1,0:T(8,128)(2,1)S(1)} fusion(bf16[8192,256]{1,0:T(8,128)(2,1)} %all-gather.3.cloned.1.call-done, bf16[64,8,64,128]{3,2,1,0:T(8,128)(2,1)} %bitcast.125), kind=kOutput, calls=%fused_computation.23 | convolution fusion | flops 2147614720 | bytes 12845056 | tf_op jit(solution)/shard_map/dot_general | solution.py:30
  95.9 14.7 %collective-permute-start.1 = (bf16[512,2,128]{2,1,0:T(2,128)(2,1)S(1)}, bf16[512,2,128]{2,1,0:T(2,128)(2,1)S(1)}, u32[]{:S(2)}, u32[]{:S(2)}) collective-permute-start(bf16[512,2,128]{2,1,0:T(2,128)(2,1)S(1)} %add_convert_fusion), channel_id=1, source_target_pairs={{0,1},{1,2},{2,3},{3,4},{4,5},{5,6},{6,7},{7,8},{8,9},{9,10},{10,1... | collective-permute-start | bytes 786440 | tf_op jit(solution)/shard_map/ppermute | solution.py:12
  112.3 1.7 collective-permute-done.1
  116.0 82.7 %reduce-scatter.3.cloned.1.call-done = f32[512,256]{1,0:T(8,128)} async-done(((f32[8192,256]{1,0:T(8,128)}), f32[512,256]{1,0:T(8,128)}) %reduce-scatter.3.cloned.1.call-update) | async-done | bytes 524304 | tf_op jit(solution)/shard_map/reduce_scatter | solution.py:81
  198.7 1.9 reshape.87
  200.6 2.4 multiply_convert_fusion.3
  202.9 1.8 reshape.98
  207.1 2.8 collective-permute-start.2
  211.9 7.5 %collective-permute-done.2 = f32[512,2,128]{2,0,1:T(8,128)} collective-permute-done((f32[512,2,128]{2,0,1:T(8,128)S(1)}, f32[512,2,128]{2,0,1:T(8,128)}, u32[]{:S(2)}, u32[]{:S(2)}) %collective-permute-start.2) | collective-permute-done | bytes 524320 | tf_op jit(solution)/shard_map/ppermute | solution.py:12
  219.3 2.1 fusion.68
  222.8 24.2 %fusion.2 = f32[8192,256]{1,0:T(8,128)} fusion(bf16[512,256]{1,0:T(8,128)(2,1)S(1)} %reshape.96, bf16[64,8,64,128]{3,2,1,0:T(8,128)(2,1)} %bitcast.126), kind=kOutput, calls=%fused_computation.2 | convolution fusion | flops 2147483648 | bytes 17039360 | tf_op jit(solution)/shard_map/dot_general | solution.py:82
  248.2 1.9 convolution_bitcast_fusion
  250.1 1.9 convolution_bitcast_fusion.2
  253.2 16.6 %all-gather.5.cloned.1.call-done = bf16[8192,256]{1,0:T(8,128)(2,1)} async-done(((bf16[512,256]{1,0:T(8,128)(2,1)}), bf16[8192,256]{1,0:T(8,128)(2,1)}) %all-gather.5.cloned.1.call-update) | async-done | bytes 4194320 | tf_op jit(solution)/shard_map/all_gather | solution.py:57
  269.9 9.3 %fusion.16 = bf16[512,256]{1,0:T(8,128)(2,1)S(1)} fusion(bf16[8192,256]{1,0:T(8,128)(2,1)} %all-gather.5.cloned.1.call-done, bf16[64,8,64,128]{3,2,1,0:T(8,128)(2,1)} %bitcast.127), kind=kOutput, calls=%fused_computation.24 | convolution fusion | flops 2147614720 | bytes 12845056 | tf_op jit(solution)/shard_map/dot_general | solution.py:30
  280.2 101.3 %reduce-scatter.5.cloned.1.call-done = f32[512,256]{1,0:T(8,128)} async-done(((f32[8192,256]{1,0:T(8,128)}), f32[512,256]{1,0:T(8,128)}) %reduce-scatter.5.cloned.1.call-update) | async-done | bytes 524304 | tf_op jit(solution)/shard_map/reduce_scatter | solution.py:81
  382.6 1.2 multiply_convert_fusion.1
  384.4 1.6 pad_maximum_fusion.7
  387.1 2.6 collective-permute-start.3
  391.7 254.6 %all-reduce.3.cloned.1.call-done = (f32[2,128,256]{2,1,0:T(8,128)}, f32[2,128,256]{2,1,0:T(8,128)}, f32[2,128,128]{2,1,0:T(8,128)}, f32[2,128,128]{2,1,0:T(8,128)}) async-done(((f32[2,128,256]{2,1,0:T(8,128)}, f32[2,128,256]{2,1,0:T(8,128)}, f32[2,128,128]{2,1,0:T(8,128)}, f32[2,128,128]{2,1,0:T(8,128)}), (f32[2,128,256]{2,1,0:T(8,128)}, f32[2,128,256]{2,1,0:T(8,128)}, f32[2,128,128]{2,1,0:T(8,128)}, ...) | async-done | bytes 786448 | tf_op jit(solution)/shard_map/psum | solution.py:116
  646.3 1.7 broadcast_multiply_fusion.2
  648.0 1.9 broadcast_multiply_fusion
  650.1 1.2 copy.29
  (75 shorter events, 16.2 us)
Async XLA Ops:
  7.2 78.9 %all-gather.3.cloned.1.call-start = ((), (), s32[]{:S(2)}) async-start(), calls=%async_computation.3 | async-start | bytes 4456448 | tf_op jit(solution)/shard_map/all_gather | solution.py:57
  7.2 9.2 %collective-permute-start = (bf16[512,2,128]{2,1,0:T(2,128)(2,1)}, bf16[512,2,128]{2,1,0:T(2,128)(2,1)S(1)}, u32[]{:S(2)}, u32[]{:S(2)}) collective-permute-start(bf16[512,2,128]{2,1,0:T(2,128)(2,1)} %param.9), channel_id=1, source_target_pairs={{0,1},{1,2},{2,3},{3,4},{4,5},{5,6},{6,7},{7,8},{8,9},{9,10},{10,1... | collective-permute-start | bytes 786440 | tf_op jit(solution)/shard_map/ppermute | solution.py:12
  18.4 1.2 copy-start.3
  20.6 178.1 %reduce-scatter.3.cloned.1.call-start = ((), (), s32[]{:S(2)}) async-start(), calls=%async_computation.2 | async-start | bytes 8912896 | tf_op jit(solution)/shard_map/reduce_scatter | solution.py:81
  28.6 12.1 %copy-start = (bf16[512,2,128]{2,1,0:T(2,128)(2,1)S(1)}, bf16[512,2,128]{2,1,0:T(2,128)(2,1)}, u32[]{:S(2)}) copy-start(bf16[512,2,128]{2,1,0:T(2,128)(2,1)} %param.10) | copy-start | bytes 786436
  28.6 12.1 %copy-start.12 = (bf16[2,128,128]{2,1,0:T(8,128)(2,1)S(1)}, bf16[2,128,128]{2,1,0:T(8,128)(2,1)}, u32[]{:S(2)}) copy-start(bf16[2,128,128]{2,1,0:T(8,128)(2,1)} %param.16) | copy-start | bytes 196612
  65.6 0.8 copy-start.14
  65.7 204.2 %all-gather.5.cloned.1.call-start = ((), (), s32[]{:S(2)}) async-start(), calls=%async_computation.5 | async-start | bytes 4456448 | tf_op jit(solution)/shard_map/all_gather | solution.py:57
  66.7 29.0 %copy-start.1 = (bf16[512,2,128]{2,1,0:T(2,128)(2,1)S(1)}, bf16[512,2,128]{2,1,0:T(2,128)(2,1)}, u32[]{:S(2)}) copy-start(bf16[512,2,128]{2,1,0:T(2,128)(2,1)} %param.9) | copy-start | bytes 786436
  66.7 45.3 %copy-start.9 = (bf16[2,128,256]{2,1,0:T(8,128)(2,1)S(1)}, bf16[2,128,256]{2,1,0:T(8,128)(2,1)}, u32[]{:S(2)}) copy-start(bf16[2,128,256]{2,1,0:T(8,128)(2,1)} %param.14) | copy-start | bytes 393220
  66.7 49.0 %copy-start.8 = (bf16[2,128,256]{2,1,0:T(8,128)(2,1)S(1)}, bf16[2,128,256]{2,1,0:T(8,128)(2,1)}, u32[]{:S(2)}) copy-start(bf16[2,128,256]{2,1,0:T(8,128)(2,1)} %param.13) | copy-start | bytes 393220
  95.9 18.0 %collective-permute-start.1 = (bf16[512,2,128]{2,1,0:T(2,128)(2,1)S(1)}, bf16[512,2,128]{2,1,0:T(2,128)(2,1)S(1)}, u32[]{:S(2)}, u32[]{:S(2)}) collective-permute-start(bf16[512,2,128]{2,1,0:T(2,128)(2,1)S(1)} %add_convert_fusion), channel_id=1, source_target_pairs={{0,1},{1,2},{2,3},{3,4},{4,5},{5,6},{6,7},{7,8},{8,9},{9,10},{10,1... | collective-permute-start | bytes 786440 | tf_op jit(solution)/shard_map/ppermute | solution.py:12
  115.0 0.7 copy-start.5
  204.7 176.8 %reduce-scatter.5.cloned.1.call-start = ((), (), s32[]{:S(2)}) async-start(), calls=%async_computation.4 | async-start | bytes 8912896 | tf_op jit(solution)/shard_map/reduce_scatter | solution.py:81
  207.1 12.2 %collective-permute-start.2 = (f32[512,2,128]{2,0,1:T(8,128)S(1)}, f32[512,2,128]{2,0,1:T(8,128)}, u32[]{:S(2)}, u32[]{:S(2)}) collective-permute-start(f32[512,2,128]{2,0,1:T(8,128)S(1)} %fusion.33), channel_id=1, source_target_pairs={{1,0},{2,1},{3,2},{4,3},{5,4},{6,5},{7,6},{8,7},{9,8},{10,9},{11,1... | collective-permute-start | bytes 1572872 | tf_op jit(solution)/shard_map/ppermute | solution.py:12
  247.0 1.0 copy-start.7
  247.0 1.2 copy-start.11
  247.0 3.1 copy-start.6
  247.0 399.3 %all-reduce.3.cloned.1.call-start = ((), (), s32[]{:S(2)}) async-start(), calls=%async_computation.6 | async-start | bytes 1572864 | tf_op jit(solution)/shard_map/psum | solution.py:116
  253.2 130.8 %copy-start.4 = (bf16[512,2,128]{2,1,0:T(2,128)(2,1)S(1)}, bf16[512,2,128]{2,1,0:T(2,128)(2,1)}, u32[]{:S(2)}) copy-start(bf16[512,2,128]{2,1,0:T(2,128)(2,1)} %copy-done.3) | copy-start | bytes 786436
  279.2 370.7 %copy-start.2 = (f32[512,2,128]{2,0,1:T(8,128)S(1)}, f32[512,2,128]{2,0,1:T(8,128)}, u32[]{:S(2)}) copy-start(f32[512,2,128]{2,0,1:T(8,128)} %get-tuple-element.27) | copy-start | bytes 1572868
  279.2 370.7 %copy-start.10 = (bf16[2,128,256]{2,1,0:T(8,128)(2,1)S(1)}, bf16[2,128,256]{2,1,0:T(8,128)(2,1)}, u32[]{:S(2)}) copy-start(bf16[2,128,256]{2,1,0:T(8,128)(2,1)} %param.14) | copy-start | bytes 393220
  280.2 105.8 %copy-start.13 = (f32[1,128,256]{2,1,0:T(8,128)S(1)}, f32[1,128,256]{2,1,0:T(8,128)}, u32[]{:S(2)}) copy-start(f32[1,128,256]{2,1,0:T(8,128)} %convolution_bitcast_fusion.2) | copy-start | bytes 393220
  387.1 262.7 %collective-permute-start.3 = (f32[512,2,128]{2,0,1:T(8,128)S(1)}, f32[512,2,128]{2,0,1:T(8,128)S(1)}, u32[]{:S(2)}, u32[]{:S(2)}) collective-permute-start(f32[512,2,128]{2,0,1:T(8,128)S(1)} %fusion.30), channel_id=1, source_target_pairs={{1,0},{2,1},{3,2},{4,3},{5,4},{6,5},{7,6},{8,7},{9,8},{10,9},{11,1... | collective-permute-start | bytes 1572872 | tf_op jit(solution)/shard_map/ppermute | solution.py:12
Sparse Core Ops, SparseCore 0:
  20.7 65.2 all-gather.2
  88.6 110.0 reduce-scatter.2
  204.8 64.9 all-gather.4
  272.3 109.1 reduce-scatter.4
  387.8 258.4 all-reduce.2
where the time goes:
time: 669 us; the launch traced here: 658 us
  waiting for transfers between devices  484 us (72%)
  matrix products  83.8 us (13%)
  starting transfers between devices  26.1 us (4%)
  local copies, waits for them, and re-layouts  25.1 us (4%)
  between operations  21 us (3%)
  other arithmetic  18.5 us (3%)
    psum x1, waiting for transfers between devices, per_device(): lax.psum((jnp.stack(outs_prev[::-1]), jnp.stack(outs_cur[::-1]), jnp.stac...  255 us
    reduce_scatter x2, waiting for transfers between devices, per_device(): lax.psum_scatter(lax.dot_general(row_matrix, gdiff_rows, (((0,), (0,)), (...  184 us
    dot_general x2, matrix products, per_device(): lax.dot_general(row_matrix, gdiff_rows, (((0,), (0,)), ((), ())), preferr...  48.8 us
    all_gather x2, waiting for transfers between devices, per_device(): lax.all_gather(gated.reshape(rows, time_days * width), 'firm', axis=0, ti...  36 us
    ppermute x4, starting transfers between devices, shifted(): return lax.ppermute(array, axis, pairs)  25.6 us
    dot_general x2, matrix products, folder(): return jnp.dot(matrix, piece, preferred_element_type=jnp.float32)  18.6 us
  transfers between devices with their start and end apart: 9, of which 7 were waited for; matrix products, arithmetic and copies ran while one was open for 16% of the time, Pallas kernels for 0%

commit v1 on v0

v1 whole, which is shorter than its diff:
```python
import jax
import jax.numpy as jnp
from jax import lax
from jax.experimental import pallas as pl
from jax.experimental.pallas import tpu as pltpu
from jax.sharding import PartitionSpec as P


L = 2
NZ = 8
BF = jnp.bfloat16
F32 = jnp.float32

FIRMS = 16
TMS = 16
ANY = pl.BlockSpec(memory_space=pltpu.HBM)


def along_z(array, by):
    pairs = [(y * NZ + z, y * NZ + (z + by) % NZ) for y in range(2) for z in range(NZ)]
    return lax.ppermute(array, "firm", pairs)


def firm_xor(array, k):
    return lax.ppermute(array, "firm", [(i, i ^ k) for i in range(FIRMS)])


def tm_xor(array, k):
    return lax.ppermute(array, "tm", [(i, i ^ k) for i in range(TMS)])


def along_x(array, by):
    pairs = [(i, ((i // 4 + by) % 4) * 4 + i % 4) for i in range(TMS)]
    return lax.ppermute(array, "tm", pairs)


def along_tm(array, by):
    pairs = [(i, i + by) for i in range(TMS) if 0 <= i + by < TMS]
    return lax.ppermute(array, "tm", pairs)


def mm(a, b, ca=1, cb=0):
    return lax.dot_general(a, b, (((ca,), (cb,)), ((), ())), preferred_element_type=F32)


VMEM_WHOLE = pl.BlockSpec(memory_space=pltpu.VMEM)
SMEM_WHOLE = pl.BlockSpec(memory_space=pltpu.SMEM)


def whole_call(kernel, outs, ins, flops=0, bytes_accessed=1 << 20, scratch=(), grant=16 << 20):
    return pl.pallas_call(
        kernel,
        in_specs=[spec for _, spec in ins],
        out_specs=[VMEM_WHOLE for _ in outs],
        out_shape=[jax.ShapeDtypeStruct(shape, dtype) for shape, dtype in outs],
        scratch_shapes=list(scratch),
        cost_estimate=cost(flops, bytes_accessed),
        compiler_params=pltpu.CompilerParams(vmem_limit_bytes=grant),
    )(*[array for array, _ in ins])


def behind(array, *earlier):
    return lax.optimization_barrier((array,) + earlier)[0]


def cost(flops, bytes_accessed):
    return pl.CostEstimate(flops=flops, bytes_accessed=bytes_accessed, transcendentals=0)


def seat(pos):
    return pos // 128, (pos // 16) % 8, (pos // 4) % 4, pos % 2


def fetch(mask_ref, tiles_ref, target, sems, slot, block_column):
    copies = []
    for i in range(4):
        for j in range(4):
            copies.append(
                pltpu.make_async_copy(
                    tiles_ref.at[i, block_column * 4 + j],
                    target.at[i * 128 : (i + 1) * 128, j * 128 : (j + 1) * 128],
                    sems.at[slot, i * 4 + j],
                )
            )

    def finish():
        for copy in copies:
            copy.wait()
        for i in range(4):
            for j in range(4):

                @pl.when(mask_ref[i, block_column * 4 + j] == 0)
                def _():
                    target[i * 128 : (i + 1) * 128, j * 128 : (j + 1) * 128] = jnp.zeros((128, 128), BF)

    return copies, finish


def lend_kernel(pos_ref, mask_ref, tiles_ref, out_ref, sems):
    y, _, x, core = seat(pos_ref[0])
    copies, finish = fetch(mask_ref, tiles_ref, out_ref, sems, 0, (1 - y) * NZ + x * 2 + core)
    for copy in copies:
        copy.start()
    finish()


def lend(pos, mask, tiles):
    return whole_call(
        lend_kernel,
        [((512, 512), BF)],
        [(pos, SMEM_WHOLE), (mask, SMEM_WHOLE), (tiles, ANY)],
        scratch=[pltpu.SemaphoreType.DMA((1, 16))],
        grant=53 << 20,
    )[0]


def prepare_kernel(pos_ref, mask_ref, cot_ref, tiles_ref, out_ref, turned_ref, sems):
    width = cot_ref.shape[1] // 2
    base = seat(pos_ref[0])[0] * NZ

    def start(q, carry):
        for copy in fetch(mask_ref, tiles_ref, out_ref.at[q], sems, q, base + q)[0]:
            copy.start()
        return carry

    def finish(q, carry):
        fetch(mask_ref, tiles_ref, out_ref.at[q], sems, q, base + q)[1]()
        return carry

    lax.fori_loop(0, NZ, start, 0)
    for t in range(2):
        lanes = slice(t * width, (t + 1) * width)
        turned_ref[lanes, :] = jnp.transpose(cot_ref[:, lanes].astype(F32)).astype(BF)
    lax.fori_loop(0, NZ, finish, 0)


def prepare(pos, mask, tiles, cot):
    rows, columns = cot.shape
    return whole_call(
        prepare_kernel,
        [((NZ, 512, 512), BF), ((columns, rows), BF)],
        [(pos, SMEM_WHOLE), (mask, SMEM_WHOLE), (cot, VMEM_WHOLE), (tiles, ANY)],
        bytes_accessed=9 << 20,
        scratch=[pltpu.SemaphoreType.DMA((NZ, 16))],
        grant=53 << 20,
    )


def previous_days(near, x, prior):
    width = x.shape[1] // 2
    first = jnp.where(near, prior[:, width:], prior[:, :width])
    second = jnp.where(near, x[:, :width], prior[:, width:])
    return first, second


def halves(array):
    width = array.shape[1] // 2
    return array[:, :width], array[:, width:]


BLOCK = 256


def by_blocks(rows, body):
    def step(s, carry):
        body(pl.ds(pl.multiple_of(s * BLOCK, BLOCK), BLOCK))
        return carry

    lax.fori_loop(0, rows // BLOCK, step, 0)


def gate_kernel(dil_ref, x_ref, prior_ref, wp_ref, wc_ref, gated_ref):
    width = wp_ref.shape[1]
    near = dil_ref[0] == 1

    def body(rows):
        x = x_ref[rows, :]
        prevs = previous_days(near, x, prior_ref[rows, :])
        for t in range(2):
            lanes = slice(t * width, (t + 1) * width)
            pre = mm(prevs[t], wp_ref[0]) + mm(x[:, lanes], wc_ref[0])
            gated_ref[rows, lanes] = (jnp.tanh(pre[:, :width]) * jax.nn.sigmoid(pre[:, width:])).astype(BF)

    by_blocks(x_ref.shape[0], body)


def gate(dil, x, prior, wp, wc):
    return whole_call(
        gate_kernel,
        [(x.shape, BF)],
        [(dil, SMEM_WHOLE), (x, VMEM_WHOLE), (prior, VMEM_WHOLE), (wp, VMEM_WHOLE), (wc, VMEM_WHOLE)],
        flops=2 * 512 * 256 * 512,
    )[0]


def gather_kernel(pos_ref, first_ref, sides_ref, far0_ref, far1_ref, other_ref, other_sides_ref, other_far_ref, out_ref):
    _, _, x, core = seat(pos_ref[0])

    def column(step, sibling):
        return ((x + step) % 4) * 2 + (core if not sibling else 1 - core)

    out_ref[column(0, False)] = first_ref[...]
    out_ref[column(1, False)] = sides_ref[:512]
    out_ref[column(3, False)] = sides_ref[512:]
    out_ref[column(2, False), :256] = far0_ref[...]
    out_ref[column(2, False), 256:] = far1_ref[...]
    out_ref[column(0, True)] = other_ref[...]
    out_ref[column(1, True)] = other_sides_ref[:512]
    out_ref[column(3, True)] = other_sides_ref[512:]
    out_ref[column(2, True)] = other_far_ref[...]


def gather_pieces(pos, pieces):
    return whole_call(
        gather_kernel,
        [((NZ, 512, 512), BF)],
        [(pos, SMEM_WHOLE)] + [(piece, VMEM_WHOLE) for piece in pieces],
        bytes_accessed=8 << 20,
    )[0]


def spread_rows(pos_ref, own_ref, peer_ref, *refs):
    pieces, (out_own_ref, out_peer_ref, acc_ref, gathered) = refs[:9], refs[9:]
    z = seat(pos_ref[0])[1]
    for slot, ref in zip((0, 1, 2, 3, None, None, 5, 6, 7), pieces):
        if slot is not None:
            gathered[slot] = ref[...]
    gathered[4, :, :128] = pieces[4][...]
    gathered[4, :, 128:] = pieces[5][...]
    out_own_ref[...] = jnp.zeros_like(out_own_ref)
    acc_ref[...] = jnp.zeros_like(acc_ref)

    def step(q, carry):
        piece = gathered[(q - z + NZ) % NZ]
        out_own_ref[...] += mm(own_ref[q], piece)
        acc_ref[...] += mm(peer_ref[q], piece)
        return carry

    lax.fori_loop(0, NZ, step, 0)
    out_peer_ref[...] = acc_ref[...].astype(BF)


def spread_forward(pos, own, peer, pieces):
    shape = pieces[0].shape
    return whole_call(
        spread_rows,
        [(shape, F32), (shape, BF)],
        [(pos, SMEM_WHOLE), (own, VMEM_WHOLE), (peer, VMEM_WHOLE)] + [(piece, VMEM_WHOLE) for piece in pieces],
        flops=2 * 1024 * 4096 * 256,
        scratch=[pltpu.VMEM(shape, F32), pltpu.VMEM((NZ,) + shape, BF)],
    )


def ring_column(s, z):
    return (z + jnp.where(s % 2 == 1, (7 - s) // 2, s // 2 - 4) + NZ) % NZ


def spread_columns(pos_ref, own_ref, peer_ref, mine_ref, theirs_ref, first_ref, out_ref, last_ref):
    z = seat(pos_ref[0])[1]

    def step(s, carry):
        q = ring_column(s, z)
        total = mm(mine_ref[...], own_ref[q]) + mm(theirs_ref[...], peer_ref[q])

        @pl.when(s == 0)
        def _():
            first_ref[...] = total.astype(BF)

        @pl.when((s > 0) & (s < NZ - 1))
        def _():
            out_ref[jnp.clip(s - 1, 0, NZ - 3)] = total

        @pl.when(s == NZ - 1)
        def _():
            last_ref[...] = total

        return carry

    lax.fori_loop(0, NZ, step, 0)


def spread_backward(pos, own, peer, mine, theirs):
    shape = mine.shape
    return whole_call(
        spread_columns,
        [(shape, BF), ((NZ - 2,) + shape, F32), (shape, F32)],
        [(pos, SMEM_WHOLE), (own, VMEM_WHOLE), (peer, VMEM_WHOLE), (mine, VMEM_WHOLE), (theirs, VMEM_WHOLE)],
        flops=2 * 1024 * 4096 * 256,
    )


def mix_kernel(x_ref, gated_ref, own_ref, other_ref, ws_ref, wn_ref, out_ref):
    width = ws_ref.shape[1]

    def body(rows):
        diffused = (own_ref[rows, :] + other_ref[rows, :].astype(F32)).astype(BF)
        for t in range(2):
            lanes = slice(t * width, (t + 1) * width)
            mixed = mm(gated_ref[rows, lanes], ws_ref[0]) + mm(diffused[:, lanes], wn_ref[0])
            out_ref[rows, lanes] = (x_ref[rows, lanes].astype(F32) + mixed).astype(BF)

    by_blocks(x_ref.shape[0], body)


def mix(*arrays):
    return whole_call(
        mix_kernel, [(arrays[0].shape, BF)], [(array, VMEM_WHOLE) for array in arrays], flops=2 * 512 * 256 * 256
    )[0]


def layer_back_kernel(
    layer, dil_ref, x_ref, prior_ref, gz_ref, p_ref, f_ref, b_ref, wp_ref, wc_ref, ws_ref, wn_ref, *refs
):
    if layer:
        gx_ref, back_ref, gw_ref = refs
    else:
        upper_ref, gx_ref, back_ref, sent_ref, gw_ref = refs
    width = ws_ref.shape[1]
    near = dil_ref[layer] == 1
    wp, wc, ws, wn = wp_ref.at[layer], wc_ref.at[layer], ws_ref.at[layer], wn_ref.at[layer]
    gw_ref[...] = jnp.zeros_like(gw_ref)

    def body(rows):
        prevs = previous_days(near, x_ref[rows, :], prior_ref[rows, :])
        backs = []
        for t in range(2):
            lanes = slice(t * width, (t + 1) * width)
            x, prev = x_ref[rows, lanes], prevs[t]
            pre = mm(prev, wp[...]) + mm(x, wc[...])
            th = jnp.tanh(pre[:, :width])
            sg = jax.nn.sigmoid(pre[:, width:])
            gated = (th * sg).astype(BF)
            gz = gz_ref[rows, lanes]
            gzb = gz.astype(BF)
            spread = p_ref[lanes, rows] + f_ref[lanes, rows].astype(F32) + b_ref[lanes, rows].astype(F32)
            spread = jnp.transpose(spread).astype(BF)
            ggated = mm(gzb, ws[...], 1, 1) + mm(spread, wn[...], 1, 1)
            gpre = jnp.concatenate(
                [ggated * sg * (1.0 - th * th), ggated * th * sg * (1.0 - sg)], axis=1
            ).astype(BF)
            gw_ref[0:128, :] += mm(gated, gzb, 0, 0)
            gw_ref[128:256, :] += mm(gated, spread, 0, 0)
            gcur = mm(x, gpre, 0, 0)
            gw_ref[256:384, :] += gcur[:, :width]
            gw_ref[384:512, :] += gcur[:, width:]
            gprev = mm(prev, gpre, 0, 0)
            gw_ref[512:640, :] += gprev[:, :width]
            gw_ref[640:768, :] += gprev[:, width:]
            back = mm(gpre, wp[...], 1, 1)
            backs.append(back)
            back_ref[rows, lanes] = back.astype(BF)
            gx_ref[rows, lanes] = gz.astype(F32) + mm(gpre, wc[...], 1, 1)
        gx_ref[rows, :width] += jnp.where(near, backs[1], jnp.zeros_like(backs[1]))

    by_blocks(x_ref.shape[0], body)
    if not layer:
        for k in range(8):
            sent_ref[k] = gw_ref[96 * k : 96 * (k + 1), :].astype(BF)
            sent_ref[8 + k] = upper_ref[96 * k : 96 * (k + 1), :].astype(BF)


def layer_back(layer, dil, arrays, upper=None):
    shape = arrays[0].shape
    outs = [(shape, F32), (shape, BF), ((768, 128), F32)]
    if not layer:
        outs[2] = ((TMS, 96, 128), BF)
        arrays = arrays + [upper]
    return whole_call(
        lambda *refs: layer_back_kernel(layer, *refs),
        outs,
        [(dil, SMEM_WHOLE)] + [(array, VMEM_WHOLE) for array in arrays],
        flops=2 * 512 * 256 * 2048,
        bytes_accessed=4 << 20,
        scratch=[] if layer else [pltpu.VMEM((768, 128), F32)],
    )


def joined(near, gx, later):
    (gx_first, gx_second), (first, second) = halves(gx), halves(later)
    first, second = first.astype(F32), second.astype(F32)
    shift_first = jnp.where(near, jnp.zeros_like(first), first)
    shift_second = jnp.where(near, first, second)
    return gx_first.astype(F32) + shift_first, gx_second.astype(F32) + shift_second


def join_kernel(dil_ref, gx_ref, later_ref, gx_pair_ref, later_pair_ref, gz_ref, turned_ref, turned_pair_ref):
    near = dil_ref[1] == 1
    width = gx_ref.shape[1] // 2
    days = joined(near, gx_ref[...], later_ref[...])
    for t in range(2):
        lanes = slice(t * width, (t + 1) * width)
        gz_ref[:, lanes] = days[t]
        turned_ref[lanes, :] = jnp.transpose(days[t]).astype(BF)
    days = joined(near, gx_pair_ref[...], later_pair_ref[...])
    for t in range(2):
        turned_pair_ref[t * width : (t + 1) * width, :] = jnp.transpose(days[t]).astype(BF)


def join(dil, *arrays):
    rows, columns = arrays[0].shape
    return whole_call(
        join_kernel,
        [((rows, columns), F32), ((columns, rows), BF), ((columns, rows), BF)],
        [(dil, SMEM_WHOLE)] + [(array, VMEM_WHOLE) for array in arrays],
    )


def ring_sum(send, parts, second=None, third=None):
    half = send.shape[0] // 2
    f, b = along_z(send[:half], 1), along_z(send[half:], -1)
    f, b = lax.optimization_barrier((f, b))
    ahead = jnp.concatenate([parts[0, :half] + f.astype(F32), parts[0, half:]], axis=0).astype(BF)
    aback = jnp.concatenate([parts[1, :half], parts[1, half:] + b.astype(F32)], axis=0).astype(BF)
    for s, wait in ((2, second), (4, third)):
        if wait is not None:
            ahead, aback, _ = lax.optimization_barrier((ahead, aback, wait))
        f, b = lax.optimization_barrier((along_z(ahead, 1), along_z(aback, -1)))
        ahead = (parts[s] + f.astype(F32)).astype(BF)
        aback = (parts[s + 1] + b.astype(F32)).astype(BF)
    return along_z(ahead, 1), along_z(aback, -1)


def exchanged(chunks, axis):
    return lax.all_to_all(chunks, axis, 0, 0).astype(F32)


def sum_everywhere(chunks):
    mine = jnp.sum(exchanged(chunks, "tm"), axis=0).astype(BF)
    mine = jnp.sum(exchanged(jnp.broadcast_to(mine, (FIRMS,) + mine.shape), "firm"), axis=0).astype(BF)
    return exchanged(jnp.broadcast_to(mine, chunks.shape), "tm")


def from_pair_later(array):
    pairs = [((i ^ NZ) * TMS + t, i * TMS + t - 1) for i in range(FIRMS) for t in range(1, TMS)]
    return lax.ppermute(array, ("firm", "tm"), pairs)


def per_device(features, cotangent, tiles, mask, w_prev, w_cur, w_self, w_nbr, dilations):
    rows, days, width = features.shape
    firm, tm = lax.axis_index("firm"), lax.axis_index("tm")
    pos = (firm * TMS + tm).astype(jnp.int32).reshape(1)
    weights = [w_prev, w_cur, w_self, w_nbr]

    state = features.reshape(rows, days * width)
    cot = cotangent.reshape(rows, days * width)
    prior = along_tm(state, 1)
    lent = firm_xor(lend(pos, mask, tiles), NZ)
    gated = gate(dilations, state, prior, w_prev, w_cur)

    half = width
    f1, b1 = along_z(gated, 1), along_z(gated, -1)
    own, cot_turned = prepare(behind(pos, gated), mask, tiles, cot)
    f1, b1, own = lax.optimization_barrier((f1, b1, own))
    f2, b2 = along_z(f1, 1), along_z(b1, -1)
    cot_pair = firm_xor(cot_turned, NZ)
    first = behind(lent, f1)
    before, after = along_x(first, 1), along_x(first, -1)
    other_first = tm_xor(first, 1)
    f2, b2, cot_pair = lax.optimization_barrier((f2, b2, cot_pair))
    f3, b3 = along_z(f2, 1), along_z(b2, -1)
    before, after = behind(before, f3, b3), behind(after, f3, b3)
    f4, b4 = along_z(f3[:, :half], 1), along_z(b3[:, half:], -1)
    far = [along_x(before[:256], 1), along_x(after[256:], -1)]
    sides = jnp.concatenate([after, before], axis=0)
    other_sides = tm_xor(sides, 1)
    other_far = tm_xor(jnp.concatenate(far, axis=0), 1)
    peer = gather_pieces(pos, [first, sides] + far + [other_first, other_sides, other_far])
    pieces = [gated, b1, b2, b3, f4, b4, f3, f2, f1]

    send, parts, last = spread_backward(pos, own, peer, cot_turned, cot_pair)
    mixed, other = spread_forward(behind(pos, send), own, peer, pieces)
    next_state = mix(state, gated, mixed, firm_xor(other, NZ), w_self, w_nbr)
    next_prior = along_tm(next_state, 1)
    f, b = ring_sum(send, parts, mixed, next_state)
    gx, back, upper = layer_back(1, dilations, [next_state, next_prior, cot, last, f, b] + weights)

    gx_pair = firm_xor(gx.astype(BF), NZ)
    gz, gz_turned, gz_pair = join(dilations, gx, along_tm(back, -1), gx_pair, from_pair_later(back))
    send, parts, last = spread_backward(pos, own, peer, gz_turned, gz_pair)
    f, b = ring_sum(send, parts)
    gx, back, sent = layer_back(0, dilations, [state, prior, gz, last, f, b] + weights, upper)
    grad = jnp.stack(joined(dilations[0] == 1, gx, along_tm(back, -1)), axis=1)

    factor = 1.0 / jnp.sqrt(jnp.float32(rows * FIRMS * days * TMS))
    sums = sum_everywhere(sent).reshape(L, 768, width) * factor
    g_self, g_nbr = sums[:, 0:128], sums[:, 128:256]
    g_cur = jnp.concatenate([sums[:, 256:384], sums[:, 384:512]], axis=2)
    g_prev = jnp.concatenate([sums[:, 512:640], sums[:, 640:768]], axis=2)
    return grad, g_prev, g_cur, g_self, g_nbr


def solution(mesh):
    in_specs = (
        P("firm", "tm", None),
        P("firm", "tm", None),
        P("firm", None, None, None),
        P("firm", None),
        P(),
        P(),
        P(),
        P(),
        P(),
    )
    out_specs = (P("firm", "tm", None), P(), P(), P(), P())
    return jax.shard_map(per_device, mesh=mesh, in_specs=in_specs, out_specs=out_specs, check_vma=False)
```

time: 669 us -> 216 us (0.32); the launches traced: 658 us -> 212 us
  waiting for transfers between devices: 484 us -> 81 us
  matrix products: 83.8 us -> 0 us
  starting transfers between devices: 26.1 us -> 69.1 us
  Pallas kernels: 0 us -> 27.5 us
  blocking collectives: 0 us -> 23.3 us
  between operations: 21 us -> 1.1 us
  local copies, waits for them, and re-layouts: 25.1 us -> 7.23 us
  other arithmetic: 18.5 us -> 3.18 us
    psum x1 -> x0, waiting for transfers between devices: 255 us -> none  [per_device(): lax.psum((jnp.stack(outs_prev[::-1]), jnp.stack(outs_cur[::-1]), jnp.stac...]
    reduce_scatter x2 -> x0, waiting for transfers between devices: 184 us -> none  [per_device(): lax.psum_scatter(lax.dot_general(row_matrix, gdiff_rows, (((0,), (0,)), (...]
    dot_general x26 -> x0, matrix products: 83.8 us -> none  [the longest x2 48.8 us: per_device(): lax.dot_general(row_matrix, gdiff_rows, (((0,), (0,)), ((), ())), preferr...]
    ppermute x4 -> x40, waiting for transfers between devices: 9.19 us -> 63.9 us  [the longest x24 44 us: along_z(): return lax.ppermute(array, 'firm', pairs)]
    all_gather x2 -> x0, waiting for transfers between devices: 36 us -> none  [per_device(): lax.all_gather(gated.reshape(rows, time_days * width), 'firm', axis=0, ti...]
    ppermute x4 -> x40, starting transfers between devices: 25.6 us -> 57.2 us  [the longest x24 22.5 us: along_z(): return lax.ppermute(array, 'firm', pairs)]
    pallas_call x0 -> x11, Pallas kernels: none -> 27.5 us  [whole_call(): pl.pallas_call(kernel, in_specs=[spec for _, spec in ins], out_specs=[VME...]
    all_to_all x0 -> x1, blocking collectives: none -> 23.3 us  [exchanged(): return lax.all_to_all(chunks, axis, 0, 0).astype(F32)]
  transfers between devices with their start and end apart: 9 -> 42, of which waited for: 7 -> 28; matrix products, arithmetic and copies ran while one was open for 16% -> 1% of each run, Pallas kernels for 0% -> 6%
where the time goes in v1:
time: 216 us; the launch traced here: 212 us
  waiting for transfers between devices  81 us (38%)
  starting transfers between devices  69.1 us (32%)
  Pallas kernels  27.5 us (13%)
  blocking collectives  23.3 us (11%)
  local copies, waits for them, and re-layouts  7.23 us (3%)
  other arithmetic  3.18 us (1%)
    ppermute x24, waiting for transfers between devices, along_z(): return lax.ppermute(array, 'firm', pairs)  44 us
    pallas_call x11, Pallas kernels, whole_call(): pl.pallas_call(kernel, in_specs=[spec for _, spec in ins], out_specs=[VME...  27.5 us
    all_to_all x1, blocking collectives, exchanged(): return lax.all_to_all(chunks, axis, 0, 0).astype(F32)  23.3 us
    ppermute x24, starting transfers between devices, along_z(): return lax.ppermute(array, 'firm', pairs)  22.5 us
    ppermute x4, starting transfers between devices, along_tm(): return lax.ppermute(array, 'tm', pairs)  19.3 us
    all_to_all x2, waiting for transfers between devices, exchanged(): return lax.all_to_all(chunks, axis, 0, 0).astype(F32)  17.1 us
    all_to_all x2, starting transfers between devices, exchanged(): return lax.all_to_all(chunks, axis, 0, 0).astype(F32)  11.9 us
    ppermute x4, waiting for transfers between devices, along_x(): return lax.ppermute(array, 'tm', pairs)  8.63 us
  transfers between devices with their start and end apart: 42, of which 28 were waited for; matrix products, arithmetic and copies ran while one was open for 1% of the time, Pallas kernels for 6%

profile of v1, /device:TPU:97, one launch (start us, length us, event | category | flops | bytes accessed | tf_op | source)
XLA Modules:
  0.0 212.4 jit_solution(13820390004286476234)
XLA Ops:
  1.6 5.4 %collective-permute-start = (bf16[512,256]{1,0:T(8,128)(2,1)S(1)}, bf16[512,256]{1,0:T(8,128)(2,1)S(1)}, u32[]{:S(2)}, u32[]{:S(2)}) collective-permute-start(bf16[512,256]{1,0:T(8,128)(2,1)S(1)} %bitcast.72), channel_id=1, source_target_pairs={{0,1},{1,2},{2,3},{3,4},{4,5},{5,6},{6,7},{7,8},{8,9},{9,10},{10,1... | collective-permute-start | bytes 786440 | tf_op jit(solution)/shard_map/ppermute | solution.py:39
  12.8 2.9 %collective-permute-start.1 = (bf16[512,256]{1,0:T(8,128)(2,1)S(1)}, bf16[512,256]{1,0:T(8,128)(2,1)S(1)}, u32[]{:S(2)}, u32[]{:S(2)}) collective-permute-start(bf16[512,256]{1,0:T(8,128)(2,1)S(1)} %shard_map.128.refs_0_.gated_ref), channel_id=1, source_target_pairs={{0,16},{16,32},{32,48},{48,64},{64,80},{80,96},{96,112},{112,0},{1... | collective-permute-start | bytes 786440 | tf_op jit(solution)/shard_map/ppermute | solution.py:21
  15.7 6.1 %shard_map.129 = (bf16[8,512,512]{2,1,0:T(8,128)(2,1)}, bf16[256,512]{1,0:T(8,128)(2,1)S(1)}) custom-call(s32[1]{0:T(128)} %bitcast.pos_ref, s32[4,64]{1,0:T(4,128)S(1)} %copy-done.6, bf16[512,256]{1,0:T(8,128)(2,1)S(1)} %bitcast.76, bf16[4,64,128,128]{3,2,1,0:T(8,128)(2,1)} %tiles_ref.3), custom_call_target="tpu_custom_call" | custom-call | bytes 9437184 | tf_op jit(solution)/shard_map/pallas_call | solution.py:51
  22.5 2.7 %collective-permute-start.5 = (bf16[512,256]{1,0:T(8,128)(2,1)S(1)}, bf16[512,256]{1,0:T(8,128)(2,1)S(1)}, u32[]{:S(2)}, u32[]{:S(2)}) collective-permute-start(bf16[512,256]{1,0:T(8,128)(2,1)S(1)} %collective-permute-done.1.refs_8_), channel_id=1, source_target_pairs={{0,16},{16,32},{32,48},{48,64},{64,80},{80,96},{96,112},{112,0},{1... | collective-permute-start | bytes 786440 | tf_op jit(solution)/shard_map/ppermute | solution.py:21
  29.3 3.0 %collective-permute-done.6.refs_2_ = bf16[512,256]{1,0:T(8,128)(2,1)S(1)} collective-permute-done((bf16[512,256]{1,0:T(8,128)(2,1)S(1)}, bf16[512,256]{1,0:T(8,128)(2,1)S(1)}, u32[]{:S(2)}, u32[]{:S(2)}) %collective-permute-start.6) | collective-permute-done | bytes 262176 | tf_op jit(solution)/shard_map/ppermute | solution.py:21
  33.7 2.8 %collective-permute-done.4 = bf16[512,512]{1,0:T(8,128)(2,1)S(1)} collective-permute-done((bf16[512,512]{1,0:T(8,128)(2,1)S(1)}, bf16[512,512]{1,0:T(8,128)(2,1)S(1)}, u32[]{:S(2)}, u32[]{:S(2)}) %collective-permute-start.4) | collective-permute-done | bytes 524320 | tf_op jit(solution)/shard_map/ppermute | solution.py:34
  36.6 3.0 %collective-permute-done.8.refs_6_ = bf16[512,256]{1,0:T(8,128)(2,1)S(1)} collective-permute-done((bf16[512,256]{1,0:T(8,128)(2,1)S(1)}, bf16[512,256]{1,0:T(8,128)(2,1)S(1)}, u32[]{:S(2)}, u32[]{:S(2)}) %collective-permute-start.8) | collective-permute-done | bytes 262176 | tf_op jit(solution)/shard_map/ppermute | solution.py:21
  39.7 3.5 %collective-permute-start.14 = (bf16[1024,512]{1,0:T(8,128)(2,1)S(1)}, bf16[1024,512]{1,0:T(8,128)(2,1)S(1)}, u32[]{:S(2)}, u32[]{:S(2)}) collective-permute-start(bf16[1024,512]{1,0:T(8,128)(2,1)S(1)} %constant_dynamic-update-slice_fusion.sides_ref), channel_id=1, source_target_pairs={{0,1},{1,0},{2,3},{3,2},{4,5},{5,4},{6,7},{7,6},{8,9},{9,8},{10,11... | collective-permute-start | bytes 3145736 | tf_op jit(solution)/shard_map/ppermute | solution.py:29
  46.6 5.8 %collective-permute-done.11.far0_ref = bf16[256,512]{1,0:T(8,128)(2,1)S(1)} collective-permute-done((bf16[256,512]{1,0:T(8,128)(2,1)S(1)}, bf16[256,512]{1,0:T(8,128)(2,1)S(1)}, u32[]{:S(2)}, u32[]{:S(2)}) %collective-permute-start.11) | collective-permute-done | bytes 262176 | tf_op jit(solution)/shard_map/ppermute | solution.py:34
  53.4 2.9 %collective-permute-start.16 = (bf16[512,128]{1,0:T(8,128)(2,1)S(1)}, bf16[512,128]{1,0:T(8,128)(2,1)S(1)}, u32[]{:S(2)}, u32[]{:S(2)}) collective-permute-start(bf16[512,128]{1,0:T(8,128)(2,1)S(1)} %slice.144), channel_id=1, source_target_pairs={{0,16},{16,32},{32,48},{48,64},{64,80},{80,96},{96,112},{112,0},{1... | collective-permute-start | bytes 393224 | tf_op jit(solution)/shard_map/ppermute | solution.py:21
  58.5 3.9 %shard_map.132 = (bf16[256,512]{1,0:T(8,128)(2,1)S(1)}, f32[6,256,512]{2,1,0:T(8,128)S(1)}, f32[256,512]{1,0:T(8,128)S(1)}) custom-call(s32[1]{0:T(128)} %bitcast.pos_ref, bf16[8,512,512]{2,1,0:T(8,128)(2,1)S(1)} %copy-done, bf16[8,512,512]{2,1,0:T(8,128)(2,1)S(1)} %shard_map.131.peer_ref, bf16[256,512]{1,0:T(8,128)(2,1)S(1)} %get-tuple-element.57.mine_ref, ...), custom_call_target="tpu_custom_call" | custom-call | flops 2147483648 | bytes 1048576 | tf_op jit(solution)/shard_map/pallas_call | solution.py:51
  62.5 3.8 %shard_map.133 = (f32[512,256]{1,0:T(8,128)S(1)}, bf16[512,256]{1,0:T(8,128)(2,1)S(1)}) custom-call(s32[1]{0:T(128)} %bitcast.pos_ref, bf16[8,512,512]{2,1,0:T(8,128)(2,1)S(1)} %copy-done, bf16[8,512,512]{2,1,0:T(8,128)(2,1)S(1)} %shard_map.131.peer_ref, bf16[512,256]{1,0:T(8,128)(2,1)S(1)} %shard_map.128.refs_0_.gated_ref, ...), custom_call_target="tpu_custom_call" | custom-call | flops 2147483648 | bytes 1048576 | tf_op jit(solution)/shard_map/pallas_call | solution.py:51
  69.0 2.6 %collective-permute-done.20 = bf16[128,512]{1,0:T(8,128)(2,1)S(1)} collective-permute-done((bf16[128,512]{1,0:T(8,128)(2,1)S(1)}, bf16[128,512]{1,0:T(8,128)(2,1)S(1)}, u32[]{:S(2)}, u32[]{:S(2)}) %collective-permute-start.20) | collective-permute-done | bytes 131104 | tf_op jit(solution)/shard_map/ppermute | solution.py:21
  75.7 3.7 %collective-permute-done.22 = bf16[256,512]{1,0:T(8,128)(2,1)S(1)} collective-permute-done((bf16[256,512]{1,0:T(8,128)(2,1)S(1)}, bf16[256,512]{1,0:T(8,128)(2,1)S(1)}, u32[]{:S(2)}, u32[]{:S(2)}) %collective-permute-start.22) | collective-permute-done | bytes 262176 | tf_op jit(solution)/shard_map/ppermute | solution.py:21
  82.9 7.4 %collective-permute-start.19 = (bf16[512,256]{1,0:T(8,128)(2,1)S(1)}, bf16[512,256]{1,0:T(8,128)(2,1)S(1)}, u32[]{:S(2)}, u32[]{:S(2)}) collective-permute-start(bf16[512,256]{1,0:T(8,128)(2,1)S(1)} %shard_map.134.refs_1_), channel_id=1, source_target_pairs={{0,1},{1,2},{2,3},{3,4},{4,5},{5,6},{6,7},{7,8},{8,9},{9,10},{10,1... | collective-permute-start | bytes 786440 | tf_op jit(solution)/shard_map/ppermute | solution.py:39
  93.6 3.5 %collective-permute-done.26.refs_5_ = bf16[256,512]{1,0:T(8,128)(2,1)S(1)} collective-permute-done((bf16[256,512]{1,0:T(8,128)(2,1)S(1)}, bf16[256,512]{1,0:T(8,128)(2,1)S(1)}, u32[]{:S(2)}, u32[]{:S(2)}) %collective-permute-start.26) | collective-permute-done | bytes 262176 | tf_op jit(solution)/shard_map/ppermute | solution.py:21
  97.1 3.0 %collective-permute-done.27.refs_6_ = bf16[256,512]{1,0:T(8,128)(2,1)S(1)} collective-permute-done((bf16[256,512]{1,0:T(8,128)(2,1)S(1)}, bf16[256,512]{1,0:T(8,128)(2,1)S(1)}, u32[]{:S(2)}, u32[]{:S(2)}) %collective-permute-start.27) | collective-permute-done | bytes 262176 | tf_op jit(solution)/shard_map/ppermute | solution.py:21
  100.2 2.6 %shard_map.135 = (f32[512,256]{1,0:T(8,128)S(1)}, bf16[512,256]{1,0:T(8,128)(2,1)S(1)}, f32[768,128]{1,0:T(8,128)S(1)}) custom-call(s32[2]{0:T(128)S(1)} %copy-done.7, bf16[512,256]{1,0:T(8,128)(2,1)S(1)} %shard_map.134.refs_1_, bf16[512,256]{1,0:T(8,128)(2,1)S(1)} %collective-permute-done.19.refs_2_, bf16[512,256]{1,0:T(8,128)(2,1)S(1)} %bitcast.77, ...), custom_call_target="tpu_custom_call" | custom-call | flops 536870912 | bytes 4194304 | tf_op jit(solution)/shard_map/pallas_call | solution.py:51
  102.8 3.5 %collective-permute-start.28 = (bf16[512,256]{1,0:T(8,128)(2,1)S(1)}, bf16[512,256]{1,0:T(8,128)(2,1)S(1)}, u32[]{:S(2)}, u32[]{:S(2)}) collective-permute-start(bf16[512,256]{1,0:T(8,128)(2,1)S(1)} %get-tuple-element.80), channel_id=1, source_target_pairs={{1,0},{2,1},{3,2},{4,3},{5,4},{6,5},{7,6},{8,7},{9,8},{10,9},{11,1... | collective-permute-start | bytes 786440 | tf_op jit(solution)/shard_map/ppermute | solution.py:39
  107.1 2.5 %collective-permute-start.30 = (bf16[512,256]{1,0:T(8,128)(2,1)S(1)}, bf16[512,256]{1,0:T(8,128)(2,1)S(1)}, u32[]{:S(2)}, u32[]{:S(2)}) collective-permute-start(bf16[512,256]{1,0:T(8,128)(2,1)S(1)} %get-tuple-element.80), channel_id=1, source_target_pairs={{129,0},{130,1},{131,2},{132,3},{133,4},{134,5},{135,6},{136,7},{1... | collective-permute-start | bytes 786440 | tf_op jit(solution)/shard_map/ppermute | solution.py:435
  109.5 5.2 %collective-permute-done.28.later_ref = bf16[512,256]{1,0:T(8,128)(2,1)S(1)} collective-permute-done((bf16[512,256]{1,0:T(8,128)(2,1)S(1)}, bf16[512,256]{1,0:T(8,128)(2,1)S(1)}, u32[]{:S(2)}, u32[]{:S(2)}) %collective-permute-start.28) | collective-permute-done | bytes 262176 | tf_op jit(solution)/shard_map/ppermute | solution.py:39
  117.8 4.0 %shard_map.137 = (bf16[256,512]{1,0:T(8,128)(2,1)S(1)}, f32[6,256,512]{2,1,0:T(8,128)S(1)}, f32[256,512]{1,0:T(8,128)S(1)}) custom-call(s32[1]{0:T(128)} %bitcast.pos_ref, bf16[8,512,512]{2,1,0:T(8,128)(2,1)S(1)} %copy-done, bf16[8,512,512]{2,1,0:T(8,128)(2,1)S(1)} %shard_map.131.peer_ref, bf16[256,512]{1,0:T(8,128)(2,1)S(1)} %get-tuple-element.82.mine_ref, ...), custom_call_target="tpu_custom_call" | custom-call | flops 2147483648 | bytes 1048576 | tf_op jit(solution)/shard_map/pallas_call | solution.py:51
  128.9 3.7 %collective-permute-done.33 = bf16[256,512]{1,0:T(8,128)(2,1)S(1)} collective-permute-done((bf16[256,512]{1,0:T(8,128)(2,1)S(1)}, bf16[256,512]{1,0:T(8,128)(2,1)S(1)}, u32[]{:S(2)}, u32[]{:S(2)}) %collective-permute-start.33) | collective-permute-done | bytes 262176 | tf_op jit(solution)/shard_map/ppermute | solution.py:21
  135.7 3.9 %collective-permute-done.35 = bf16[256,512]{1,0:T(8,128)(2,1)S(1)} collective-permute-done((bf16[256,512]{1,0:T(8,128)(2,1)S(1)}, bf16[256,512]{1,0:T(8,128)(2,1)S(1)}, u32[]{:S(2)}, u32[]{:S(2)}) %collective-permute-start.35) | collective-permute-done | bytes 262176 | tf_op jit(solution)/shard_map/ppermute | solution.py:21
  142.8 5.0 %collective-permute-done.37.refs_5_ = bf16[256,512]{1,0:T(8,128)(2,1)S(1)} collective-permute-done((bf16[256,512]{1,0:T(8,128)(2,1)S(1)}, bf16[256,512]{1,0:T(8,128)(2,1)S(1)}, u32[]{:S(2)}, u32[]{:S(2)}) %collective-permute-start.37) | collective-permute-done | bytes 262176 | tf_op jit(solution)/shard_map/ppermute | solution.py:21
  149.1 2.6 %shard_map.138 = (f32[512,256]{1,0:T(8,128)S(1)}, bf16[512,256]{1,0:T(8,128)(2,1)S(1)}, bf16[16,96,128]{2,1,0:T(8,128)(2,1)S(1)}) custom-call(s32[2]{0:T(128)S(1)} %copy-done.7, bf16[512,256]{1,0:T(8,128)(2,1)S(1)} %bitcast.75, bf16[512,256]{1,0:T(8,128)(2,1)S(1)} %collective-permute-done.prior_ref.refs_2_, f32[512,256]{1,0:T(8,128)S(1)} %get-tuple-element.81.refs_3_, ...), custom_call_target="tpu_custom_call" | custom-call | flops 536870912 | bytes 4194304 | tf_op jit(solution)/shard_map/pallas_call | solution.py:51
  151.8 23.3 %all_to_all.15 = bf16[16,96,128]{2,1,0:T(8,128)(2,1)S(1)} all-to-all(bf16[16,96,128]{2,1,0:T(8,128)(2,1)S(1)} %get-tuple-element.96), channel_id=1, replica_groups=mesh['firm'=16,'tm'=16] {'tm'}, dimensions={0} | all-to-all | bytes 786432 | tf_op jit(solution)/shard_map/all_to_all | solution.py:424
  176.0 7.0 %all-to-all-start.1 = ((bf16[16,96,128]{2,1,0:T(8,128)(2,1)}), bf16[16,96,128]{2,1,0:T(8,128)(2,1)S(1)}, u32[]{:S(2)}, u32[]{:S(2)}) async-start(bf16[16,96,128]{2,1,0:T(8,128)(2,1)} %broadcast_in_dim.10), calls=%async_computation.1 | async-start | bytes 786432 | tf_op jit(solution)/shard_map/all_to_all | solution.py:424
  183.0 3.0 %collective-permute-start.39 = (bf16[512,256]{1,0:T(8,128)(2,1)S(1)}, bf16[512,256]{1,0:T(8,128)(2,1)S(1)}, u32[]{:S(2)}, u32[]{:S(2)}) collective-permute-start(bf16[512,256]{1,0:T(8,128)(2,1)S(1)} %get-tuple-element.95), channel_id=1, source_target_pairs={{1,0},{2,1},{3,2},{4,3},{5,4},{6,5},{7,6},{8,7},{9,8},{10,9},{11,1... | collective-permute-start | bytes 786440 | tf_op jit(solution)/shard_map/ppermute | solution.py:39
  186.0 8.3 %all-to-all-done.1 = bf16[16,96,128]{2,1,0:T(8,128)(2,1)S(1)} async-done(((bf16[16,96,128]{2,1,0:T(8,128)(2,1)}), bf16[16,96,128]{2,1,0:T(8,128)(2,1)S(1)}, u32[]{:S(2)}, u32[]{:S(2)}) %all-to-all-start.1) | async-done | bytes 393248 | tf_op jit(solution)/shard_map/all_to_all | solution.py:424
  195.2 4.9 %all-to-all-start.2 = ((bf16[16,96,128]{2,1,0:T(8,128)(2,1)}), bf16[16,96,128]{2,1,0:T(8,128)(2,1)S(1)}, u32[]{:S(2)}, u32[]{:S(2)}) async-start(bf16[16,96,128]{2,1,0:T(8,128)(2,1)} %broadcast_in_dim.11), calls=%async_computation.2 | async-start | bytes 786432 | tf_op jit(solution)/shard_map/all_to_all | solution.py:424
  201.4 8.8 %all-to-all-done.2 = bf16[16,96,128]{2,1,0:T(8,128)(2,1)S(1)} async-done(((bf16[16,96,128]{2,1,0:T(8,128)(2,1)}), bf16[16,96,128]{2,1,0:T(8,128)(2,1)S(1)}, u32[]{:S(2)}, u32[]{:S(2)}) %all-to-all-start.2) | async-done | bytes 393248 | tf_op jit(solution)/shard_map/all_to_all | solution.py:424
  (118 shorter events, 57.2 us)
Async XLA Ops:
  1.6 10.0 %collective-permute-start = (bf16[512,256]{1,0:T(8,128)(2,1)S(1)}, bf16[512,256]{1,0:T(8,128)(2,1)S(1)}, u32[]{:S(2)}, u32[]{:S(2)}) collective-permute-start(bf16[512,256]{1,0:T(8,128)(2,1)S(1)} %bitcast.72), channel_id=1, source_target_pairs={{0,1},{1,2},{2,3},{3,4},{4,5},{5,6},{6,7},{7,8},{8,9},{9,10},{10,1... | collective-permute-start | bytes 786440 | tf_op jit(solution)/shard_map/ppermute | solution.py:39
  9.6 15.6 %collective-permute-start.3 = (bf16[512,512]{1,0:T(8,128)(2,1)S(1)}, bf16[512,512]{1,0:T(8,128)(2,1)S(1)}, u32[]{:S(2)}, u32[]{:S(2)}) collective-permute-start(bf16[512,512]{1,0:T(8,128)(2,1)S(1)} %shard_map.130), channel_id=1, source_target_pairs={{0,128},{16,144},{32,160},{48,176},{64,192},{80,208},{96,224},{112... | collective-permute-start | bytes 1572872 | tf_op jit(solution)/shard_map/ppermute | solution.py:25
  12.8 9.8 %collective-permute-start.1 = (bf16[512,256]{1,0:T(8,128)(2,1)S(1)}, bf16[512,256]{1,0:T(8,128)(2,1)S(1)}, u32[]{:S(2)}, u32[]{:S(2)}) collective-permute-start(bf16[512,256]{1,0:T(8,128)(2,1)S(1)} %shard_map.128.refs_0_.gated_ref), channel_id=1, source_target_pairs={{0,16},{16,32},{32,48},{48,64},{64,80},{80,96},{96,112},{112,0},{1... | collective-permute-start | bytes 786440 | tf_op jit(solution)/shard_map/ppermute | solution.py:21
  15.7 6.8 %collective-permute-start.2 = (bf16[512,256]{1,0:T(8,128)(2,1)S(1)}, bf16[512,256]{1,0:T(8,128)(2,1)S(1)}, u32[]{:S(2)}, u32[]{:S(2)}) collective-permute-start(bf16[512,256]{1,0:T(8,128)(2,1)S(1)} %shard_map.128.refs_0_.gated_ref), channel_id=1, source_target_pairs={{0,112},{16,0},{32,16},{48,32},{64,48},{80,64},{96,80},{112,96},{1... | collective-permute-start | bytes 786440 | tf_op jit(solution)/shard_map/ppermute | solution.py:21
  21.8 6.5 %collective-permute-start.7 = (bf16[256,512]{1,0:T(8,128)(2,1)S(1)}, bf16[256,512]{1,0:T(8,128)(2,1)S(1)}, u32[]{:S(2)}, u32[]{:S(2)}) collective-permute-start(bf16[256,512]{1,0:T(8,128)(2,1)S(1)} %get-tuple-element.57.mine_ref), channel_id=1, source_target_pairs={{0,128},{16,144},{32,160},{48,176},{64,192},{80,208},{96,224},{112... | collective-permute-start | bytes 786440 | tf_op jit(solution)/shard_map/ppermute | solution.py:25
  22.5 6.8 %collective-permute-start.5 = (bf16[512,256]{1,0:T(8,128)(2,1)S(1)}, bf16[512,256]{1,0:T(8,128)(2,1)S(1)}, u32[]{:S(2)}, u32[]{:S(2)}) collective-permute-start(bf16[512,256]{1,0:T(8,128)(2,1)S(1)} %collective-permute-done.1.refs_8_), channel_id=1, source_target_pairs={{0,16},{16,32},{32,48},{48,64},{64,80},{80,96},{96,112},{112,0},{1... | collective-permute-start | bytes 786440 | tf_op jit(solution)/shard_map/ppermute | solution.py:21
  25.2 7.1 %collective-permute-start.6 = (bf16[512,256]{1,0:T(8,128)(2,1)S(1)}, bf16[512,256]{1,0:T(8,128)(2,1)S(1)}, u32[]{:S(2)}, u32[]{:S(2)}) collective-permute-start(bf16[512,256]{1,0:T(8,128)(2,1)S(1)} %collective-permute-done.2.refs_1_), channel_id=1, source_target_pairs={{0,112},{16,0},{32,16},{48,32},{64,48},{80,64},{96,80},{112,96},{1... | collective-permute-start | bytes 786440 | tf_op jit(solution)/shard_map/ppermute | solution.py:21
  25.2 11.3 %collective-permute-start.4 = (bf16[512,512]{1,0:T(8,128)(2,1)S(1)}, bf16[512,512]{1,0:T(8,128)(2,1)S(1)}, u32[]{:S(2)}, u32[]{:S(2)}) collective-permute-start(bf16[512,512]{1,0:T(8,128)(2,1)S(1)} %collective-permute-done.3.first_ref), channel_id=1, source_target_pairs={{0,12},{1,13},{2,14},{3,15},{4,0},{5,1},{6,2},{7,3},{8,4},{9,5},{1... | collective-permute-start | bytes 1572872 | tf_op jit(solution)/shard_map/ppermute | solution.py:34
  27.5 12.2 %collective-permute-start.10 = (bf16[512,512]{1,0:T(8,128)(2,1)S(1)}, bf16[512,512]{1,0:T(8,128)(2,1)S(1)}, u32[]{:S(2)}, u32[]{:S(2)}) collective-permute-start(bf16[512,512]{1,0:T(8,128)(2,1)S(1)} %collective-permute-done.3.first_ref), channel_id=1, source_target_pairs={{0,4},{1,5},{2,6},{3,7},{4,8},{5,9},{6,10},{7,11},{8,12},{9,13},{1... | collective-permute-start | bytes 1572872 | tf_op jit(solution)/shard_map/ppermute | solution.py:34
  32.3 7.3 %collective-permute-start.8 = (bf16[512,256]{1,0:T(8,128)(2,1)S(1)}, bf16[512,256]{1,0:T(8,128)(2,1)S(1)}, u32[]{:S(2)}, u32[]{:S(2)}) collective-permute-start(bf16[512,256]{1,0:T(8,128)(2,1)S(1)} %collective-permute-done.5.refs_7_), channel_id=1, source_target_pairs={{0,16},{16,32},{32,48},{48,64},{64,80},{80,96},{96,112},{112,0},{1... | collective-permute-start | bytes 786440 | tf_op jit(solution)/shard_map/ppermute | solution.py:21
  32.3 7.4 %collective-permute-start.9 = (bf16[512,256]{1,0:T(8,128)(2,1)S(1)}, bf16[512,256]{1,0:T(8,128)(2,1)S(1)}, u32[]{:S(2)}, u32[]{:S(2)}) collective-permute-start(bf16[512,256]{1,0:T(8,128)(2,1)S(1)} %collective-permute-done.6.refs_2_), channel_id=1, source_target_pairs={{0,112},{16,0},{32,16},{48,32},{64,48},{80,64},{96,80},{112,96},{1... | collective-permute-start | bytes 786440 | tf_op jit(solution)/shard_map/ppermute | solution.py:21
  39.7 16.7 %collective-permute-start.14 = (bf16[1024,512]{1,0:T(8,128)(2,1)S(1)}, bf16[1024,512]{1,0:T(8,128)(2,1)S(1)}, u32[]{:S(2)}, u32[]{:S(2)}) collective-permute-start(bf16[1024,512]{1,0:T(8,128)(2,1)S(1)} %constant_dynamic-update-slice_fusion.sides_ref), channel_id=1, source_target_pairs={{0,1},{1,0},{2,3},{3,2},{4,5},{5,4},{6,7},{7,6},{8,9},{9,8},{10,11... | collective-permute-start | bytes 3145736 | tf_op jit(solution)/shard_map/ppermute | solution.py:29
  43.2 9.1 %collective-permute-start.11 = (bf16[256,512]{1,0:T(8,128)(2,1)S(1)}, bf16[256,512]{1,0:T(8,128)(2,1)S(1)}, u32[]{:S(2)}, u32[]{:S(2)}) collective-permute-start(bf16[256,512]{1,0:T(8,128)(2,1)S(1)} %slice.109), channel_id=1, source_target_pairs={{0,4},{1,5},{2,6},{3,7},{4,8},{5,9},{6,10},{7,11},{8,12},{9,13},{1... | collective-permute-start | bytes 786440 | tf_op jit(solution)/shard_map/ppermute | solution.py:34
  44.6 7.8 %collective-permute-start.12 = (bf16[256,512]{1,0:T(8,128)(2,1)S(1)}, bf16[256,512]{1,0:T(8,128)(2,1)S(1)}, u32[]{:S(2)}, u32[]{:S(2)}) collective-permute-start(bf16[256,512]{1,0:T(8,128)(2,1)S(1)} %slice.110), channel_id=1, source_target_pairs={{0,12},{1,13},{2,14},{3,15},{4,0},{5,1},{6,2},{7,3},{8,4},{9,5},{1... | collective-permute-start | bytes 786440 | tf_op jit(solution)/shard_map/ppermute | solution.py:34
  46.0 10.4 %collective-permute-start.13 = (bf16[512,512]{1,0:T(8,128)(2,1)S(1)}, bf16[512,512]{1,0:T(8,128)(2,1)S(1)}, u32[]{:S(2)}, u32[]{:S(2)}) collective-permute-start(bf16[512,512]{1,0:T(8,128)(2,1)S(1)} %collective-permute-done.3.first_ref), channel_id=1, source_target_pairs={{0,1},{1,0},{2,3},{3,2},{4,5},{5,4},{6,7},{7,6},{8,9},{9,8},{10,11... | collective-permute-start | bytes 1572872 | tf_op jit(solution)/shard_map/ppermute | solution.py:29
  53.4 9.1 %collective-permute-start.16 = (bf16[512,128]{1,0:T(8,128)(2,1)S(1)}, bf16[512,128]{1,0:T(8,128)(2,1)S(1)}, u32[]{:S(2)}, u32[]{:S(2)}) collective-permute-start(bf16[512,128]{1,0:T(8,128)(2,1)S(1)} %slice.144), channel_id=1, source_target_pairs={{0,16},{16,32},{32,48},{48,64},{64,80},{80,96},{96,112},{112,0},{1... | collective-permute-start | bytes 393224 | tf_op jit(solution)/shard_map/ppermute | solution.py:21
  66.3 8.9 %collective-permute-start.18 = (bf16[512,256]{1,0:T(8,128)(2,1)S(1)}, bf16[512,256]{1,0:T(8,128)(2,1)S(1)}, u32[]{:S(2)}, u32[]{:S(2)}) collective-permute-start(bf16[512,256]{1,0:T(8,128)(2,1)S(1)} %get-tuple-element.66), channel_id=1, source_target_pairs={{0,128},{16,144},{32,160},{48,176},{64,192},{80,208},{96,224},{112... | collective-permute-start | bytes 786440 | tf_op jit(solution)/shard_map/ppermute | solution.py:25
  74.1 7.1 %collective-permute-start.23 = (bf16[256,512]{1,0:T(8,128)(2,1)S(1)}, bf16[256,512]{1,0:T(8,128)(2,1)S(1)}, u32[]{:S(2)}, u32[]{:S(2)}) collective-permute-start(bf16[256,512]{1,0:T(8,128)(2,1)S(1)} %get-tuple-element.72), channel_id=1, source_target_pairs={{0,112},{16,0},{32,16},{48,32},{64,48},{80,64},{96,80},{112,96},{1... | collective-permute-start | bytes 786440 | tf_op jit(solution)/shard_map/ppermute | solution.py:21
  81.4 8.9 %collective-permute-start.24 = (bf16[256,512]{1,0:T(8,128)(2,1)S(1)}, bf16[256,512]{1,0:T(8,128)(2,1)S(1)}, u32[]{:S(2)}, u32[]{:S(2)}) collective-permute-start(bf16[256,512]{1,0:T(8,128)(2,1)S(1)} %get-tuple-element.75), channel_id=1, source_target_pairs={{0,16},{16,32},{32,48},{48,64},{64,80},{80,96},{96,112},{112,0},{1... | collective-permute-start | bytes 786440 | tf_op jit(solution)/shard_map/ppermute | solution.py:21
  81.7 8.6 %collective-permute-start.25 = (bf16[256,512]{1,0:T(8,128)(2,1)S(1)}, bf16[256,512]{1,0:T(8,128)(2,1)S(1)}, u32[]{:S(2)}, u32[]{:S(2)}) collective-permute-start(bf16[256,512]{1,0:T(8,128)(2,1)S(1)} %get-tuple-element.76), channel_id=1, source_target_pairs={{0,112},{16,0},{32,16},{48,32},{64,48},{80,64},{96,80},{112,96},{1... | collective-permute-start | bytes 786440 | tf_op jit(solution)/shard_map/ppermute | solution.py:21
  82.9 10.7 %collective-permute-start.19 = (bf16[512,256]{1,0:T(8,128)(2,1)S(1)}, bf16[512,256]{1,0:T(8,128)(2,1)S(1)}, u32[]{:S(2)}, u32[]{:S(2)}) collective-permute-start(bf16[512,256]{1,0:T(8,128)(2,1)S(1)} %shard_map.134.refs_1_), channel_id=1, source_target_pairs={{0,1},{1,2},{2,3},{3,4},{4,5},{5,6},{6,7},{7,8},{8,9},{9,10},{10,1... | collective-permute-start | bytes 786440 | tf_op jit(solution)/shard_map/ppermute | solution.py:39
  90.5 6.6 %collective-permute-start.26 = (bf16[256,512]{1,0:T(8,128)(2,1)S(1)}, bf16[256,512]{1,0:T(8,128)(2,1)S(1)}, u32[]{:S(2)}, u32[]{:S(2)}) collective-permute-start(bf16[256,512]{1,0:T(8,128)(2,1)S(1)} %get-tuple-element.114), channel_id=1, source_target_pairs={{0,16},{16,32},{32,48},{48,64},{64,80},{80,96},{96,112},{112,0},{1... | collective-permute-start | bytes 786440 | tf_op jit(solution)/shard_map/ppermute | solution.py:21
  91.8 8.4 %collective-permute-start.27 = (bf16[256,512]{1,0:T(8,128)(2,1)S(1)}, bf16[256,512]{1,0:T(8,128)(2,1)S(1)}, u32[]{:S(2)}, u32[]{:S(2)}) collective-permute-start(bf16[256,512]{1,0:T(8,128)(2,1)S(1)} %get-tuple-element.113), channel_id=1, source_target_pairs={{0,112},{16,0},{32,16},{48,32},{64,48},{80,64},{96,80},{112,96},{1... | collective-permute-start | bytes 786440 | tf_op jit(solution)/shard_map/ppermute | solution.py:21
  102.8 12.0 %collective-permute-start.28 = (bf16[512,256]{1,0:T(8,128)(2,1)S(1)}, bf16[512,256]{1,0:T(8,128)(2,1)S(1)}, u32[]{:S(2)}, u32[]{:S(2)}) collective-permute-start(bf16[512,256]{1,0:T(8,128)(2,1)S(1)} %get-tuple-element.80), channel_id=1, source_target_pairs={{1,0},{2,1},{3,2},{4,3},{5,4},{6,5},{7,6},{8,7},{9,8},{10,9},{11,1... | collective-permute-start | bytes 786440 | tf_op jit(solution)/shard_map/ppermute | solution.py:39
  106.3 9.1 %collective-permute-start.29 = (bf16[512,256]{1,0:T(8,128)(2,1)S(1)}, bf16[512,256]{1,0:T(8,128)(2,1)S(1)}, u32[]{:S(2)}, u32[]{:S(2)}) collective-permute-start(bf16[512,256]{1,0:T(8,128)(2,1)S(1)} %convert_element_type.90), channel_id=1, source_target_pairs={{0,128},{16,144},{32,160},{48,176},{64,192},{80,208},{96,224},{112... | collective-permute-start | bytes 786440 | tf_op jit(solution)/shard_map/ppermute | solution.py:25
  107.1 9.9 %collective-permute-start.30 = (bf16[512,256]{1,0:T(8,128)(2,1)S(1)}, bf16[512,256]{1,0:T(8,128)(2,1)S(1)}, u32[]{:S(2)}, u32[]{:S(2)}) collective-permute-start(bf16[512,256]{1,0:T(8,128)(2,1)S(1)} %get-tuple-element.80), channel_id=1, source_target_pairs={{129,0},{130,1},{131,2},{132,3},{133,4},{134,5},{135,6},{136,7},{1... | collective-permute-start | bytes 786440 | tf_op jit(solution)/shard_map/ppermute | solution.py:435
  127.4 6.5 %collective-permute-start.34 = (bf16[256,512]{1,0:T(8,128)(2,1)S(1)}, bf16[256,512]{1,0:T(8,128)(2,1)S(1)}, u32[]{:S(2)}, u32[]{:S(2)}) collective-permute-start(bf16[256,512]{1,0:T(8,128)(2,1)S(1)} %pad_maximum_fusion.5), channel_id=1, source_target_pairs={{0,112},{16,0},{32,16},{48,32},{64,48},{80,64},{96,80},{112,96},{1... | collective-permute-start | bytes 786440 | tf_op jit(solution)/shard_map/ppermute | solution.py:21
  141.3 6.5 %collective-permute-start.37 = (bf16[256,512]{1,0:T(8,128)(2,1)S(1)}, bf16[256,512]{1,0:T(8,128)(2,1)S(1)}, u32[]{:S(2)}, u32[]{:S(2)}) collective-permute-start(bf16[256,512]{1,0:T(8,128)(2,1)S(1)} %get-tuple-element.108), channel_id=1, source_target_pairs={{0,16},{16,32},{32,48},{48,64},{64,80},{80,96},{96,112},{112,0},{1... | collective-permute-start | bytes 786440 | tf_op jit(solution)/shard_map/ppermute | solution.py:21
  141.5 7.7 %collective-permute-start.38 = (bf16[256,512]{1,0:T(8,128)(2,1)S(1)}, bf16[256,512]{1,0:T(8,128)(2,1)S(1)}, u32[]{:S(2)}, u32[]{:S(2)}) collective-permute-start(bf16[256,512]{1,0:T(8,128)(2,1)S(1)} %get-tuple-element.107), channel_id=1, source_target_pairs={{0,112},{16,0},{32,16},{48,32},{64,48},{80,64},{96,80},{112,96},{1... | collective-permute-start | bytes 786440 | tf_op jit(solution)/shard_map/ppermute | solution.py:21
  176.0 18.4 %all-to-all-start.1 = ((bf16[16,96,128]{2,1,0:T(8,128)(2,1)}), bf16[16,96,128]{2,1,0:T(8,128)(2,1)S(1)}, u32[]{:S(2)}, u32[]{:S(2)}) async-start(bf16[16,96,128]{2,1,0:T(8,128)(2,1)} %broadcast_in_dim.10), calls=%async_computation.1 | async-start | bytes 786432 | tf_op jit(solution)/shard_map/all_to_all | solution.py:424
  183.0 17.1 %collective-permute-start.39 = (bf16[512,256]{1,0:T(8,128)(2,1)S(1)}, bf16[512,256]{1,0:T(8,128)(2,1)S(1)}, u32[]{:S(2)}, u32[]{:S(2)}) collective-permute-start(bf16[512,256]{1,0:T(8,128)(2,1)S(1)} %get-tuple-element.95), channel_id=1, source_target_pairs={{1,0},{2,1},{3,2},{4,3},{5,4},{6,5},{7,6},{8,7},{9,8},{10,9},{11,1... | collective-permute-start | bytes 786440 | tf_op jit(solution)/shard_map/ppermute | solution.py:39
  195.2 15.0 %all-to-all-start.2 = ((bf16[16,96,128]{2,1,0:T(8,128)(2,1)}), bf16[16,96,128]{2,1,0:T(8,128)(2,1)S(1)}, u32[]{:S(2)}, u32[]{:S(2)}) async-start(bf16[16,96,128]{2,1,0:T(8,128)(2,1)} %broadcast_in_dim.11), calls=%async_computation.2 | async-start | bytes 786432 | tf_op jit(solution)/shard_map/all_to_all | solution.py:424
  (19 other events, 97.8 us)

commit v2 on v1

--- a/solution.py
+++ b/solution.py
@@ -110,7 +110,7 @@
         [((512, 512), BF)],
         [(pos, SMEM_WHOLE), (mask, SMEM_WHOLE), (tiles, ANY)],
         scratch=[pltpu.SemaphoreType.DMA((1, 16))],
-        grant=53 << 20,
+        grant=49 << 20,
     )[0]
 
 
@@ -142,7 +142,7 @@
         [(pos, SMEM_WHOLE), (mask, SMEM_WHOLE), (cot, VMEM_WHOLE), (tiles, ANY)],
         bytes_accessed=9 << 20,
         scratch=[pltpu.SemaphoreType.DMA((NZ, 16))],
-        grant=53 << 20,
+        grant=49 << 20,
     )
 
 
@@ -255,20 +255,21 @@
     return (z + jnp.where(s % 2 == 1, (7 - s) // 2, s // 2 - 4) + NZ) % NZ
 
 
-def spread_columns(pos_ref, own_ref, peer_ref, mine_ref, theirs_ref, first_ref, out_ref, last_ref):
+def spread_first(pos_ref, own_ref, peer_ref, mine_ref, theirs_ref, first_ref):
+    q = ring_column(0, seat(pos_ref[0])[1])
+    first_ref[...] = (mm(mine_ref[...], own_ref[q]) + mm(theirs_ref[...], peer_ref[q])).astype(BF)
+
+
+def spread_columns(pos_ref, own_ref, peer_ref, mine_ref, theirs_ref, out_ref, last_ref):
     z = seat(pos_ref[0])[1]
 
     def step(s, carry):
         q = ring_column(s, z)
         total = mm(mine_ref[...], own_ref[q]) + mm(theirs_ref[...], peer_ref[q])
 
-        @pl.when(s == 0)
+        @pl.when(s < NZ - 1)
         def _():
-            first_ref[...] = total.astype(BF)
-
-        @pl.when((s > 0) & (s < NZ - 1))
-        def _():
-            out_ref[jnp.clip(s - 1, 0, NZ - 3)] = total
+            out_ref[jnp.minimum(s - 1, NZ - 3)] = total
 
         @pl.when(s == NZ - 1)
         def _():
@@ -276,17 +277,17 @@
 
         return carry
 
-    lax.fori_loop(0, NZ, step, 0)
+    lax.fori_loop(1, NZ, step, 0)
 
 
 def spread_backward(pos, own, peer, mine, theirs):
     shape = mine.shape
-    return whole_call(
-        spread_columns,
-        [(shape, BF), ((NZ - 2,) + shape, F32), (shape, F32)],
-        [(pos, SMEM_WHOLE), (own, VMEM_WHOLE), (peer, VMEM_WHOLE), (mine, VMEM_WHOLE), (theirs, VMEM_WHOLE)],
-        flops=2 * 1024 * 4096 * 256,
-    )
+    ins = [(pos, SMEM_WHOLE), (own, VMEM_WHOLE), (peer, VMEM_WHOLE), (mine, VMEM_WHOLE), (theirs, VMEM_WHOLE)]
+    send = whole_call(spread_first, [(shape, BF)], ins, flops=2 * 1024 * 512 * 256)[0]
+    ins[0] = (behind(pos, send), SMEM_WHOLE)
+    outs = [((NZ - 2,) + shape, F32), (shape, F32)]
+    parts, last = whole_call(spread_columns, outs, ins, flops=2 * 1024 * 3584 * 256)
+    return send, parts, last
 
 
 def mix_kernel(x_ref, gated_ref, own_ref, other_ref, ws_ref, wn_ref, out_ref):
@@ -405,19 +406,21 @@
     )
 
 
-def ring_sum(send, parts, second=None, third=None):
+def ring_step(ahead, aback):
+    f, b = along_z(ahead, 1), along_z(aback, -1)
+    return lax.optimization_barrier((f, b))
+
+
+def ring_sum(send, parts):
     half = send.shape[0] // 2
-    f, b = along_z(send[:half], 1), along_z(send[half:], -1)
-    f, b = lax.optimization_barrier((f, b))
+    f, b = ring_step(send[:half], send[half:])
     ahead = jnp.concatenate([parts[0, :half] + f.astype(F32), parts[0, half:]], axis=0).astype(BF)
     aback = jnp.concatenate([parts[1, :half], parts[1, half:] + b.astype(F32)], axis=0).astype(BF)
-    for s, wait in ((2, second), (4, third)):
-        if wait is not None:
-            ahead, aback, _ = lax.optimization_barrier((ahead, aback, wait))
-        f, b = lax.optimization_barrier((along_z(ahead, 1), along_z(aback, -1)))
+    for s in (2, 4):
+        f, b = ring_step(ahead, aback)
         ahead = (parts[s] + f.astype(F32)).astype(BF)
         aback = (parts[s + 1] + b.astype(F32)).astype(BF)
-    return along_z(ahead, 1), along_z(aback, -1)
+    return ring_step(ahead, aback)
 
 
 def exchanged(chunks, axis):
@@ -435,43 +438,47 @@
     return lax.ppermute(array, ("firm", "tm"), pairs)
 
 
-def per_device(features, cotangent, tiles, mask, w_prev, w_cur, w_self, w_nbr, dilations):
+def both_layers(features, cotangent, tiles, mask, w_prev, w_cur, w_self, w_nbr, dilations):
     rows, days, width = features.shape
     firm, tm = lax.axis_index("firm"), lax.axis_index("tm")
     pos = (firm * TMS + tm).astype(jnp.int32).reshape(1)
     weights = [w_prev, w_cur, w_self, w_nbr]
 
+    piece = lend(pos, mask, tiles)
     state = features.reshape(rows, days * width)
     cot = cotangent.reshape(rows, days * width)
-    prior = along_tm(state, 1)
-    lent = firm_xor(lend(pos, mask, tiles), NZ)
+    lent = firm_xor(piece, NZ)
+    prior = along_tm(behind(state, piece), 1)
     gated = gate(dilations, state, prior, w_prev, w_cur)
 
     half = width
-    f1, b1 = along_z(gated, 1), along_z(gated, -1)
-    own, cot_turned = prepare(behind(pos, gated), mask, tiles, cot)
-    f1, b1, own = lax.optimization_barrier((f1, b1, own))
-    f2, b2 = along_z(f1, 1), along_z(b1, -1)
-    cot_pair = firm_xor(cot_turned, NZ)
-    first = behind(lent, f1)
+    first = behind(lent, gated)
     before, after = along_x(first, 1), along_x(first, -1)
     other_first = tm_xor(first, 1)
-    f2, b2, cot_pair = lax.optimization_barrier((f2, b2, cot_pair))
-    f3, b3 = along_z(f2, 1), along_z(b2, -1)
-    before, after = behind(before, f3, b3), behind(after, f3, b3)
-    f4, b4 = along_z(f3[:, :half], 1), along_z(b3[:, half:], -1)
+    f1, b1 = along_z(gated, 1), along_z(gated, -1)
+    pos_then = behind(pos, gated)
+    own, cot_turned = prepare(pos_then, mask, tiles, cot)
+    cot_pair = firm_xor(cot_turned, NZ)
+    before, after, own, f1, b1 = lax.optimization_barrier((before, after, own, f1, b1))
     far = [along_x(before[:256], 1), along_x(after[256:], -1)]
+    f2, b2 = along_z(f1, 1), along_z(b1, -1)
     sides = jnp.concatenate([after, before], axis=0)
     other_sides = tm_xor(sides, 1)
+    f2, b2, cot_pair, far[0], far[1] = lax.optimization_barrier((f2, b2, cot_pair, far[0], far[1]))
     other_far = tm_xor(jnp.concatenate(far, axis=0), 1)
+    f3, b3 = along_z(f2, 1), along_z(b2, -1)
     peer = gather_pieces(pos, [first, sides] + far + [other_first, other_sides, other_far])
+    send, parts, last = spread_backward(pos, own, peer, cot_turned, cot_pair)
+    f3, b3 = lax.optimization_barrier((f3, b3))
+    f4, b4 = along_z(f3[:, :half], 1), along_z(b3[:, half:], -1)
+    f4, b4 = lax.optimization_barrier((f4, b4))
     pieces = [gated, b1, b2, b3, f4, b4, f3, f2, f1]
 
-    send, parts, last = spread_backward(pos, own, peer, cot_turned, cot_pair)
-    mixed, other = spread_forward(behind(pos, send), own, peer, pieces)
+    pos_then = behind(pos, send)
+    mixed, other = spread_forward(pos_then, own, peer, pieces)
     next_state = mix(state, gated, mixed, firm_xor(other, NZ), w_self, w_nbr)
     next_prior = along_tm(next_state, 1)
-    f, b = ring_sum(send, parts, mixed, next_state)
+    f, b = ring_sum(send, parts)
     gx, back, upper = layer_back(1, dilations, [next_state, next_prior, cot, last, f, b] + weights)
 
     gx_pair = firm_xor(gx.astype(BF), NZ)
@@ -502,4 +509,4 @@
         P(),
     )
     out_specs = (P("firm", "tm", None), P(), P(), P(), P())
-    return jax.shard_map(per_device, mesh=mesh, in_specs=in_specs, out_specs=out_specs, check_vma=False)
+    return jax.shard_map(both_layers, mesh=mesh, in_specs=in_specs, out_specs=out_specs, check_vma=False)

time: 216 us -> 211 us (0.977)
  waiting for transfers between devices: 81 us -> 84 us
  local copies, waits for them, and re-layouts: 7.23 us -> 4.53 us
    ppermute x4, waiting for transfers between devices: 8.36 us -> 19.6 us  [along_tm(): return lax.ppermute(array, 'tm', pairs)]
    ppermute x4, waiting for transfers between devices: 8.63 us -> 0.01 us  [along_x(): return lax.ppermute(array, 'tm', pairs)]
    unnamed x22 -> x20, local copies, waits for them, and re-layouts: 4.71 us -> 2.01 us
    pallas_call x11 -> x13, Pallas kernels: 27.5 us -> 25.5 us  [whole_call(): pl.pallas_call(kernel, in_specs=[spec for _, spec in ins], out_specs=[VME...]
  transfers between devices with their start and end apart: 42 -> 42, of which waited for: 28 -> 24; matrix products, arithmetic and copies ran while one was open for 1% -> 2% of each run, Pallas kernels for 6% -> 7%
where the time goes in v2:
time: 211 us; the launch traced here: 207 us
  waiting for transfers between devices  84 us (40%)
  starting transfers between devices  67 us (32%)
  Pallas kernels  25.5 us (12%)
  blocking collectives  22.6 us (11%)
  local copies, waits for them, and re-layouts  4.53 us (2%)
  other arithmetic  2.61 us (1%)
    ppermute x24, waiting for transfers between devices, along_z(): return lax.ppermute(array, 'firm', pairs)  43.3 us
    pallas_call x13, Pallas kernels, whole_call(): pl.pallas_call(kernel, in_specs=[spec for _, spec in ins], out_specs=[VME...  25.5 us
    ppermute x24, starting transfers between devices, along_z(): return lax.ppermute(array, 'firm', pairs)  23.3 us
    all_to_all x1, blocking collectives, exchanged(): return lax.all_to_all(chunks, axis, 0, 0).astype(F32)  22.6 us
    ppermute x4, waiting for transfers between devices, along_tm(): return lax.ppermute(array, 'tm', pairs)  19.6 us
    ppermute x4, starting transfers between devices, along_tm(): return lax.ppermute(array, 'tm', pairs)  19.2 us
    all_to_all x2, waiting for transfers between devices, exchanged(): return lax.all_to_all(chunks, axis, 0, 0).astype(F32)  17.2 us
    all_to_all x2, starting transfers between devices, exchanged(): return lax.all_to_all(chunks, axis, 0, 0).astype(F32)  9.98 us
  transfers between devices with their start and end apart: 42, of which 24 were waited for; matrix products, arithmetic and copies ran while one was open for 2% of the time, Pallas kernels for 7%

profile of v2, /device:TPU:97, one launch (start us, length us, event | category | flops | bytes accessed | tf_op | source)
XLA Modules:
  0.0 207.3 jit_solution(17309330159849849780)
XLA Ops:
  4.6 5.4 %collective-permute-start = (bf16[512,256]{1,0:T(8,128)(2,1)S(1)}, bf16[512,256]{1,0:T(8,128)(2,1)S(1)}, u32[]{:S(2)}, u32[]{:S(2)}) collective-permute-start(bf16[512,256]{1,0:T(8,128)(2,1)S(1)} %bitcast.72), channel_id=1, source_target_pairs={{0,1},{1,2},{2,3},{3,4},{4,5},{5,6},{6,7},{7,8},{8,9},{9,10},{10,1... | collective-permute-start | bytes 786440 | tf_op jit(solution)/shard_map/ppermute | solution.py:39
  10.0 9.1 %collective-permute-done.prior_ref.refs_2_ = bf16[512,256]{1,0:T(8,128)(2,1)S(1)} collective-permute-done((bf16[512,256]{1,0:T(8,128)(2,1)S(1)}, bf16[512,256]{1,0:T(8,128)(2,1)S(1)}, u32[]{:S(2)}, u32[]{:S(2)}) %collective-permute-start) | collective-permute-done | bytes 262176 | tf_op jit(solution)/shard_map/ppermute | solution.py:39
  23.0 2.9 %collective-permute-start.4 = (bf16[512,256]{1,0:T(8,128)(2,1)S(1)}, bf16[512,256]{1,0:T(8,128)(2,1)S(1)}, u32[]{:S(2)}, u32[]{:S(2)}) collective-permute-start(bf16[512,256]{1,0:T(8,128)(2,1)S(1)} %shard_map.129.refs_0_.gated_ref), channel_id=1, source_target_pairs={{0,16},{16,32},{32,48},{48,64},{64,80},{80,96},{96,112},{112,0},{1... | collective-permute-start | bytes 786440 | tf_op jit(solution)/shard_map/ppermute | solution.py:21
  26.0 4.1 %shard_map.130 = (bf16[8,512,512]{2,1,0:T(8,128)(2,1)S(1)}, bf16[256,512]{1,0:T(8,128)(2,1)S(1)}) custom-call(s32[1]{0:T(128)} %bitcast.pos_ref, s32[4,64]{1,0:T(4,128)S(1)} %copy-done.4, bf16[512,256]{1,0:T(8,128)(2,1)S(1)} %bitcast.76, bf16[4,64,128,128]{3,2,1,0:T(8,128)(2,1)} %tiles_ref.3), custom_call_target="tpu_custom_call" | custom-call | bytes 9437184 | tf_op jit(solution)/shard_map/pallas_call | solution.py:51
  31.4 3.4 %collective-permute-done.5.refs_1_ = bf16[512,256]{1,0:T(8,128)(2,1)S(1)} collective-permute-done((bf16[512,256]{1,0:T(8,128)(2,1)S(1)}, bf16[512,256]{1,0:T(8,128)(2,1)S(1)}, u32[]{:S(2)}, u32[]{:S(2)}) %collective-permute-start.5) | collective-permute-done | bytes 262176 | tf_op jit(solution)/shard_map/ppermute | solution.py:21
  35.4 2.4 %collective-permute-start.6 = (bf16[512,256]{1,0:T(8,128)(2,1)S(1)}, bf16[512,256]{1,0:T(8,128)(2,1)S(1)}, u32[]{:S(2)}, u32[]{:S(2)}) collective-permute-start(bf16[512,256]{1,0:T(8,128)(2,1)S(1)} %collective-permute-done.4.refs_8_), channel_id=1, source_target_pairs={{0,16},{16,32},{32,48},{48,64},{64,80},{80,96},{96,112},{112,0},{1... | collective-permute-start | bytes 786440 | tf_op jit(solution)/shard_map/ppermute | solution.py:21
  40.5 2.7 %collective-permute-done.6.refs_7_ = bf16[512,256]{1,0:T(8,128)(2,1)S(1)} collective-permute-done((bf16[512,256]{1,0:T(8,128)(2,1)S(1)}, bf16[512,256]{1,0:T(8,128)(2,1)S(1)}, u32[]{:S(2)}, u32[]{:S(2)}) %collective-permute-start.6) | collective-permute-done | bytes 262176 | tf_op jit(solution)/shard_map/ppermute | solution.py:21
  47.9 2.7 %collective-permute-start.14 = (bf16[512,256]{1,0:T(8,128)(2,1)S(1)}, bf16[512,256]{1,0:T(8,128)(2,1)S(1)}, u32[]{:S(2)}, u32[]{:S(2)}) collective-permute-start(bf16[512,256]{1,0:T(8,128)(2,1)S(1)} %collective-permute-done.6.refs_7_), channel_id=1, source_target_pairs={{0,16},{16,32},{32,48},{48,64},{64,80},{80,96},{96,112},{112,0},{1... | collective-permute-start | bytes 786440 | tf_op jit(solution)/shard_map/ppermute | solution.py:21
  51.4 3.5 %shard_map.135 = (f32[6,256,512]{2,1,0:T(8,128)S(1)}, f32[256,512]{1,0:T(8,128)S(1)}) custom-call(s32[1]{0:T(128)} %bitcast.pos_ref, bf16[8,512,512]{2,1,0:T(8,128)(2,1)S(1)} %get-tuple-element.61.own_ref, bf16[8,512,512]{2,1,0:T(8,128)(2,1)S(1)} %shard_map.131.peer_ref, bf16[256,512]{1,0:T(8,128)(2,1)S(1)} %get-tuple-element.66.mine_ref, ...), custom_call_target="tpu_custom_call" | custom-call | flops 1879048192 | bytes 1048576 | tf_op jit(solution)/shard_map/pallas_call | solution.py:51
  55.1 2.7 %collective-permute-start.20 = (bf16[128,512]{1,0:T(8,128)(2,1)S(1)}, bf16[128,512]{1,0:T(8,128)(2,1)S(1)}, u32[]{:S(2)}, u32[]{:S(2)}) collective-permute-start(bf16[128,512]{1,0:T(8,128)(2,1)S(1)} %get-tuple-element.146), channel_id=1, source_target_pairs={{0,16},{16,32},{32,48},{48,64},{64,80},{80,96},{96,112},{112,0},{1... | collective-permute-start | bytes 393224 | tf_op jit(solution)/shard_map/ppermute | solution.py:21
  57.8 2.2 %collective-permute-done.20 = bf16[128,512]{1,0:T(8,128)(2,1)S(1)} collective-permute-done((bf16[128,512]{1,0:T(8,128)(2,1)S(1)}, bf16[128,512]{1,0:T(8,128)(2,1)S(1)}, u32[]{:S(2)}, u32[]{:S(2)}) %collective-permute-start.20) | collective-permute-done | bytes 131104 | tf_op jit(solution)/shard_map/ppermute | solution.py:21
  60.0 3.1 %collective-permute-done.21 = bf16[128,512]{1,0:T(8,128)(2,1)S(1)} collective-permute-done((bf16[128,512]{1,0:T(8,128)(2,1)S(1)}, bf16[128,512]{1,0:T(8,128)(2,1)S(1)}, u32[]{:S(2)}, u32[]{:S(2)}) %collective-permute-start.21) | collective-permute-done | bytes 131104 | tf_op jit(solution)/shard_map/ppermute | solution.py:21
  66.6 2.8 %collective-permute-done.22 = bf16[256,512]{1,0:T(8,128)(2,1)S(1)} collective-permute-done((bf16[256,512]{1,0:T(8,128)(2,1)S(1)}, bf16[256,512]{1,0:T(8,128)(2,1)S(1)}, u32[]{:S(2)}, u32[]{:S(2)}) %collective-permute-start.22) | collective-permute-done | bytes 262176 | tf_op jit(solution)/shard_map/ppermute | solution.py:21
  73.8 3.8 %shard_map.133 = (f32[512,256]{1,0:T(8,128)S(1)}, bf16[512,256]{1,0:T(8,128)(2,1)S(1)}) custom-call(s32[1]{0:T(128)} %bitcast.pos_ref, bf16[8,512,512]{2,1,0:T(8,128)(2,1)S(1)} %get-tuple-element.61.own_ref, bf16[8,512,512]{2,1,0:T(8,128)(2,1)S(1)} %shard_map.131.peer_ref, bf16[512,256]{1,0:T(8,128)(2,1)S(1)} %shard_map.129.refs_0_.gated_ref, ...), custom_call_target="tpu_custom_call" | custom-call | flops 2147483648 | bytes 1048576 | tf_op jit(solution)/shard_map/pallas_call | solution.py:51
  83.4 9.2 %collective-permute-start.19 = (bf16[512,256]{1,0:T(8,128)(2,1)S(1)}, bf16[512,256]{1,0:T(8,128)(2,1)S(1)}, u32[]{:S(2)}, u32[]{:S(2)}) collective-permute-start(bf16[512,256]{1,0:T(8,128)(2,1)S(1)} %shard_map.134.refs_1_), channel_id=1, source_target_pairs={{0,1},{1,2},{2,3},{3,4},{4,5},{5,6},{6,7},{7,8},{8,9},{9,10},{10,1... | collective-permute-start | bytes 786440 | tf_op jit(solution)/shard_map/ppermute | solution.py:39
  92.6 3.3 %collective-permute-done.19.refs_2_ = bf16[512,256]{1,0:T(8,128)(2,1)S(1)} collective-permute-done((bf16[512,256]{1,0:T(8,128)(2,1)S(1)}, bf16[512,256]{1,0:T(8,128)(2,1)S(1)}, u32[]{:S(2)}, u32[]{:S(2)}) %collective-permute-start.19) | collective-permute-done | bytes 262176 | tf_op jit(solution)/shard_map/ppermute | solution.py:39
  95.9 2.6 %shard_map.136 = (f32[512,256]{1,0:T(8,128)S(1)}, bf16[512,256]{1,0:T(8,128)(2,1)S(1)}, f32[768,128]{1,0:T(8,128)S(1)}) custom-call(s32[2]{0:T(128)S(1)} %copy-done.5, bf16[512,256]{1,0:T(8,128)(2,1)S(1)} %shard_map.134.refs_1_, bf16[512,256]{1,0:T(8,128)(2,1)S(1)} %collective-permute-done.19.refs_2_, bf16[512,256]{1,0:T(8,128)(2,1)S(1)} %bitcast.77, ...), custom_call_target="tpu_custom_call" | custom-call | flops 536870912 | bytes 4194304 | tf_op jit(solution)/shard_map/pallas_call | solution.py:51
  101.0 2.1 %collective-permute-start.30 = (bf16[512,256]{1,0:T(8,128)(2,1)S(1)}, bf16[512,256]{1,0:T(8,128)(2,1)S(1)}, u32[]{:S(2)}, u32[]{:S(2)}) collective-permute-start(bf16[512,256]{1,0:T(8,128)(2,1)S(1)} %get-tuple-element.90), channel_id=1, source_target_pairs={{129,0},{130,1},{131,2},{132,3},{133,4},{134,5},{135,6},{136,7},{1... | collective-permute-start | bytes 786440 | tf_op jit(solution)/shard_map/ppermute | solution.py:438
  103.1 7.2 %collective-permute-done.28.later_ref = bf16[512,256]{1,0:T(8,128)(2,1)S(1)} collective-permute-done((bf16[512,256]{1,0:T(8,128)(2,1)S(1)}, bf16[512,256]{1,0:T(8,128)(2,1)S(1)}, u32[]{:S(2)}, u32[]{:S(2)}) %collective-permute-start.28) | collective-permute-done | bytes 262176 | tf_op jit(solution)/shard_map/ppermute | solution.py:39
  113.4 3.5 %shard_map.139 = (f32[6,256,512]{2,1,0:T(8,128)S(1)}, f32[256,512]{1,0:T(8,128)S(1)}) custom-call(s32[1]{0:T(128)} %bitcast.pos_ref, bf16[8,512,512]{2,1,0:T(8,128)(2,1)S(1)} %get-tuple-element.61.own_ref, bf16[8,512,512]{2,1,0:T(8,128)(2,1)S(1)} %shard_map.131.peer_ref, bf16[256,512]{1,0:T(8,128)(2,1)S(1)} %get-tuple-element.92.mine_ref, ...), custom_call_target="tpu_custom_call" | custom-call | flops 1879048192 | bytes 1048576 | tf_op jit(solution)/shard_map/pallas_call | solution.py:51
  118.6 3.5 %collective-permute-done.31 = bf16[128,512]{1,0:T(8,128)(2,1)S(1)} collective-permute-done((bf16[128,512]{1,0:T(8,128)(2,1)S(1)}, bf16[128,512]{1,0:T(8,128)(2,1)S(1)}, u32[]{:S(2)}, u32[]{:S(2)}) %collective-permute-start.31) | collective-permute-done | bytes 131104 | tf_op jit(solution)/shard_map/ppermute | solution.py:21
  122.2 2.1 %collective-permute-done.32 = bf16[128,512]{1,0:T(8,128)(2,1)S(1)} collective-permute-done((bf16[128,512]{1,0:T(8,128)(2,1)S(1)}, bf16[128,512]{1,0:T(8,128)(2,1)S(1)}, u32[]{:S(2)}, u32[]{:S(2)}) %collective-permute-start.32) | collective-permute-done | bytes 131104 | tf_op jit(solution)/shard_map/ppermute | solution.py:21
  126.0 5.2 %collective-permute-done.33 = bf16[256,512]{1,0:T(8,128)(2,1)S(1)} collective-permute-done((bf16[256,512]{1,0:T(8,128)(2,1)S(1)}, bf16[256,512]{1,0:T(8,128)(2,1)S(1)}, u32[]{:S(2)}, u32[]{:S(2)}) %collective-permute-start.33) | collective-permute-done | bytes 262176 | tf_op jit(solution)/shard_map/ppermute | solution.py:21
  134.5 4.4 %collective-permute-done.35 = bf16[256,512]{1,0:T(8,128)(2,1)S(1)} collective-permute-done((bf16[256,512]{1,0:T(8,128)(2,1)S(1)}, bf16[256,512]{1,0:T(8,128)(2,1)S(1)}, u32[]{:S(2)}, u32[]{:S(2)}) %collective-permute-start.35) | collective-permute-done | bytes 262176 | tf_op jit(solution)/shard_map/ppermute | solution.py:21
  142.1 3.8 %collective-permute-done.37.refs_5_ = bf16[256,512]{1,0:T(8,128)(2,1)S(1)} collective-permute-done((bf16[256,512]{1,0:T(8,128)(2,1)S(1)}, bf16[256,512]{1,0:T(8,128)(2,1)S(1)}, u32[]{:S(2)}, u32[]{:S(2)}) %collective-permute-start.37) | collective-permute-done | bytes 262176 | tf_op jit(solution)/shard_map/ppermute | solution.py:21
  147.3 2.6 %shard_map.140 = (f32[512,256]{1,0:T(8,128)S(1)}, bf16[512,256]{1,0:T(8,128)(2,1)S(1)}, bf16[16,96,128]{2,1,0:T(8,128)(2,1)S(1)}) custom-call(s32[2]{0:T(128)S(1)} %copy-done.5, bf16[512,256]{1,0:T(8,128)(2,1)S(1)} %bitcast.75, bf16[512,256]{1,0:T(8,128)(2,1)S(1)} %collective-permute-done.prior_ref.refs_2_, f32[512,256]{1,0:T(8,128)S(1)} %get-tuple-element.91.refs_3_, ...), custom_call_target="tpu_custom_call" | custom-call | flops 536870912 | bytes 4194304 | tf_op jit(solution)/shard_map/pallas_call | solution.py:51
  150.0 22.6 %all_to_all.15 = bf16[16,96,128]{2,1,0:T(8,128)(2,1)S(1)} all-to-all(bf16[16,96,128]{2,1,0:T(8,128)(2,1)S(1)} %get-tuple-element.108), channel_id=1, replica_groups=mesh['firm'=16,'tm'=16] {'tm'}, dimensions={0} | all-to-all | bytes 786432 | tf_op jit(solution)/shard_map/all_to_all | solution.py:427
  173.5 5.2 %all-to-all-start.1 = ((bf16[16,96,128]{2,1,0:T(8,128)(2,1)}), bf16[16,96,128]{2,1,0:T(8,128)(2,1)S(1)}, u32[]{:S(2)}, u32[]{:S(2)}) async-start(bf16[16,96,128]{2,1,0:T(8,128)(2,1)} %broadcast_in_dim.10), calls=%async_computation.1 | async-start | bytes 786432 | tf_op jit(solution)/shard_map/all_to_all | solution.py:427
  178.6 2.8 %collective-permute-start.39 = (bf16[512,256]{1,0:T(8,128)(2,1)S(1)}, bf16[512,256]{1,0:T(8,128)(2,1)S(1)}, u32[]{:S(2)}, u32[]{:S(2)}) collective-permute-start(bf16[512,256]{1,0:T(8,128)(2,1)S(1)} %get-tuple-element.107), channel_id=1, source_target_pairs={{1,0},{2,1},{3,2},{4,3},{5,4},{6,5},{7,6},{8,7},{9,8},{10,9},{11,1... | collective-permute-start | bytes 786440 | tf_op jit(solution)/shard_map/ppermute | solution.py:39
  181.4 8.4 %all-to-all-done.1 = bf16[16,96,128]{2,1,0:T(8,128)(2,1)S(1)} async-done(((bf16[16,96,128]{2,1,0:T(8,128)(2,1)}), bf16[16,96,128]{2,1,0:T(8,128)(2,1)S(1)}, u32[]{:S(2)}, u32[]{:S(2)}) %all-to-all-start.1) | async-done | bytes 393248 | tf_op jit(solution)/shard_map/all_to_all | solution.py:427
  190.7 4.8 %all-to-all-start.2 = ((bf16[16,96,128]{2,1,0:T(8,128)(2,1)}), bf16[16,96,128]{2,1,0:T(8,128)(2,1)S(1)}, u32[]{:S(2)}, u32[]{:S(2)}) async-start(bf16[16,96,128]{2,1,0:T(8,128)(2,1)} %broadcast_in_dim.11), calls=%async_computation.2 | async-start | bytes 786432 | tf_op jit(solution)/shard_map/all_to_all | solution.py:427
  196.9 8.8 %all-to-all-done.2 = bf16[16,96,128]{2,1,0:T(8,128)(2,1)S(1)} async-done(((bf16[16,96,128]{2,1,0:T(8,128)(2,1)}), bf16[16,96,128]{2,1,0:T(8,128)(2,1)S(1)}, u32[]{:S(2)}, u32[]{:S(2)}) %all-to-all-start.2) | async-done | bytes 393248 | tf_op jit(solution)/shard_map/all_to_all | solution.py:427
  (118 shorter events, 53.4 us)
Async XLA Ops:
  3.2 17.1 %collective-permute-start.1 = (bf16[512,512]{1,0:T(8,128)(2,1)S(1)}, bf16[512,512]{1,0:T(8,128)(2,1)S(1)}, u32[]{:S(2)}, u32[]{:S(2)}) collective-permute-start(bf16[512,512]{1,0:T(8,128)(2,1)S(1)} %shard_map.128), channel_id=1, source_target_pairs={{0,128},{16,144},{32,160},{48,176},{64,192},{80,208},{96,224},{112... | collective-permute-start | bytes 1572872 | tf_op jit(solution)/shard_map/ppermute | solution.py:25
  4.6 14.5 %collective-permute-start = (bf16[512,256]{1,0:T(8,128)(2,1)S(1)}, bf16[512,256]{1,0:T(8,128)(2,1)S(1)}, u32[]{:S(2)}, u32[]{:S(2)}) collective-permute-start(bf16[512,256]{1,0:T(8,128)(2,1)S(1)} %bitcast.72), channel_id=1, source_target_pairs={{0,1},{1,2},{2,3},{3,4},{4,5},{5,6},{6,7},{7,8},{8,9},{9,10},{10,1... | collective-permute-start | bytes 786440 | tf_op jit(solution)/shard_map/ppermute | solution.py:39
  20.3 14.5 %collective-permute-start.2 = (bf16[512,512]{1,0:T(8,128)(2,1)S(1)}, bf16[512,512]{1,0:T(8,128)(2,1)S(1)}, u32[]{:S(2)}, u32[]{:S(2)}) collective-permute-start(bf16[512,512]{1,0:T(8,128)(2,1)S(1)} %collective-permute-done.1.first_ref), channel_id=1, source_target_pairs={{0,4},{1,5},{2,6},{3,7},{4,8},{5,9},{6,10},{7,11},{8,12},{9,13},{1... | collective-permute-start | bytes 1572872 | tf_op jit(solution)/shard_map/ppermute | solution.py:34
  21.6 13.3 %collective-permute-start.3 = (bf16[512,512]{1,0:T(8,128)(2,1)S(1)}, bf16[512,512]{1,0:T(8,128)(2,1)S(1)}, u32[]{:S(2)}, u32[]{:S(2)}) collective-permute-start(bf16[512,512]{1,0:T(8,128)(2,1)S(1)} %collective-permute-done.1.first_ref), channel_id=1, source_target_pairs={{0,12},{1,13},{2,14},{3,15},{4,0},{5,1},{6,2},{7,3},{8,4},{9,5},{1... | collective-permute-start | bytes 1572872 | tf_op jit(solution)/shard_map/ppermute | solution.py:34
  23.0 8.4 %collective-permute-start.4 = (bf16[512,256]{1,0:T(8,128)(2,1)S(1)}, bf16[512,256]{1,0:T(8,128)(2,1)S(1)}, u32[]{:S(2)}, u32[]{:S(2)}) collective-permute-start(bf16[512,256]{1,0:T(8,128)(2,1)S(1)} %shard_map.129.refs_0_.gated_ref), channel_id=1, source_target_pairs={{0,16},{16,32},{32,48},{48,64},{64,80},{80,96},{96,112},{112,0},{1... | collective-permute-start | bytes 786440 | tf_op jit(solution)/shard_map/ppermute | solution.py:21
  25.9 8.9 %collective-permute-start.5 = (bf16[512,256]{1,0:T(8,128)(2,1)S(1)}, bf16[512,256]{1,0:T(8,128)(2,1)S(1)}, u32[]{:S(2)}, u32[]{:S(2)}) collective-permute-start(bf16[512,256]{1,0:T(8,128)(2,1)S(1)} %shard_map.129.refs_0_.gated_ref), channel_id=1, source_target_pairs={{0,112},{16,0},{32,16},{48,32},{64,48},{80,64},{96,80},{112,96},{1... | collective-permute-start | bytes 786440 | tf_op jit(solution)/shard_map/ppermute | solution.py:21
  30.0 9.0 %collective-permute-start.8 = (bf16[256,512]{1,0:T(8,128)(2,1)S(1)}, bf16[256,512]{1,0:T(8,128)(2,1)S(1)}, u32[]{:S(2)}, u32[]{:S(2)}) collective-permute-start(bf16[256,512]{1,0:T(8,128)(2,1)S(1)} %get-tuple-element.66.mine_ref), channel_id=1, source_target_pairs={{0,128},{16,144},{32,160},{48,176},{64,192},{80,208},{96,224},{112... | collective-permute-start | bytes 786440 | tf_op jit(solution)/shard_map/ppermute | solution.py:25
  34.9 15.7 %collective-permute-start.12 = (bf16[1024,512]{1,0:T(8,128)(2,1)S(1)}, bf16[1024,512]{1,0:T(8,128)(2,1)S(1)}, u32[]{:S(2)}, u32[]{:S(2)}) collective-permute-start(bf16[1024,512]{1,0:T(8,128)(2,1)S(1)} %constant_dynamic-update-slice_fusion.sides_ref), channel_id=1, source_target_pairs={{0,1},{1,0},{2,3},{3,2},{4,5},{5,4},{6,7},{7,6},{8,9},{9,8},{10,11... | collective-permute-start | bytes 3145736 | tf_op jit(solution)/shard_map/ppermute | solution.py:29
  35.4 7.8 %collective-permute-start.6 = (bf16[512,256]{1,0:T(8,128)(2,1)S(1)}, bf16[512,256]{1,0:T(8,128)(2,1)S(1)}, u32[]{:S(2)}, u32[]{:S(2)}) collective-permute-start(bf16[512,256]{1,0:T(8,128)(2,1)S(1)} %collective-permute-done.4.refs_8_), channel_id=1, source_target_pairs={{0,16},{16,32},{32,48},{48,64},{64,80},{80,96},{96,112},{112,0},{1... | collective-permute-start | bytes 786440 | tf_op jit(solution)/shard_map/ppermute | solution.py:21
  37.8 8.3 %collective-permute-start.7 = (bf16[512,256]{1,0:T(8,128)(2,1)S(1)}, bf16[512,256]{1,0:T(8,128)(2,1)S(1)}, u32[]{:S(2)}, u32[]{:S(2)}) collective-permute-start(bf16[512,256]{1,0:T(8,128)(2,1)S(1)} %collective-permute-done.5.refs_1_), channel_id=1, source_target_pairs={{0,112},{16,0},{32,16},{48,32},{64,48},{80,64},{96,80},{112,96},{1... | collective-permute-start | bytes 786440 | tf_op jit(solution)/shard_map/ppermute | solution.py:21
  37.8 8.3 %collective-permute-start.9 = (bf16[256,512]{1,0:T(8,128)(2,1)S(1)}, bf16[256,512]{1,0:T(8,128)(2,1)S(1)}, u32[]{:S(2)}, u32[]{:S(2)}) collective-permute-start(bf16[256,512]{1,0:T(8,128)(2,1)S(1)} %slice.109), channel_id=1, source_target_pairs={{0,4},{1,5},{2,6},{3,7},{4,8},{5,9},{6,10},{7,11},{8,12},{9,13},{1... | collective-permute-start | bytes 786440 | tf_op jit(solution)/shard_map/ppermute | solution.py:34
  39.0 7.1 %collective-permute-start.10 = (bf16[256,512]{1,0:T(8,128)(2,1)S(1)}, bf16[256,512]{1,0:T(8,128)(2,1)S(1)}, u32[]{:S(2)}, u32[]{:S(2)}) collective-permute-start(bf16[256,512]{1,0:T(8,128)(2,1)S(1)} %slice.110), channel_id=1, source_target_pairs={{0,12},{1,13},{2,14},{3,15},{4,0},{5,1},{6,2},{7,3},{8,4},{9,5},{1... | collective-permute-start | bytes 786440 | tf_op jit(solution)/shard_map/ppermute | solution.py:34
  43.2 7.3 %collective-permute-start.11 = (bf16[512,512]{1,0:T(8,128)(2,1)S(1)}, bf16[512,512]{1,0:T(8,128)(2,1)S(1)}, u32[]{:S(2)}, u32[]{:S(2)}) collective-permute-start(bf16[512,512]{1,0:T(8,128)(2,1)S(1)} %collective-permute-done.1.first_ref), channel_id=1, source_target_pairs={{0,1},{1,0},{2,3},{3,2},{4,5},{5,4},{6,7},{7,6},{8,9},{9,8},{10,11... | collective-permute-start | bytes 1572872 | tf_op jit(solution)/shard_map/ppermute | solution.py:29
  47.9 17.0 %collective-permute-start.14 = (bf16[512,256]{1,0:T(8,128)(2,1)S(1)}, bf16[512,256]{1,0:T(8,128)(2,1)S(1)}, u32[]{:S(2)}, u32[]{:S(2)}) collective-permute-start(bf16[512,256]{1,0:T(8,128)(2,1)S(1)} %collective-permute-done.6.refs_7_), channel_id=1, source_target_pairs={{0,16},{16,32},{32,48},{48,64},{64,80},{80,96},{96,112},{112,0},{1... | collective-permute-start | bytes 786440 | tf_op jit(solution)/shard_map/ppermute | solution.py:21
  50.6 14.3 %collective-permute-start.15 = (bf16[512,256]{1,0:T(8,128)(2,1)S(1)}, bf16[512,256]{1,0:T(8,128)(2,1)S(1)}, u32[]{:S(2)}, u32[]{:S(2)}) collective-permute-start(bf16[512,256]{1,0:T(8,128)(2,1)S(1)} %collective-permute-done.7.refs_2_), channel_id=1, source_target_pairs={{0,112},{16,0},{32,16},{48,32},{64,48},{80,64},{96,80},{112,96},{1... | collective-permute-start | bytes 786440 | tf_op jit(solution)/shard_map/ppermute | solution.py:21
  63.6 7.4 %collective-permute-start.23 = (bf16[256,512]{1,0:T(8,128)(2,1)S(1)}, bf16[256,512]{1,0:T(8,128)(2,1)S(1)}, u32[]{:S(2)}, u32[]{:S(2)}) collective-permute-start(bf16[256,512]{1,0:T(8,128)(2,1)S(1)} %pad_maximum_fusion.3), channel_id=1, source_target_pairs={{0,112},{16,0},{32,16},{48,32},{64,48},{80,64},{96,80},{112,96},{1... | collective-permute-start | bytes 786440 | tf_op jit(solution)/shard_map/ppermute | solution.py:21
  64.9 7.8 %collective-permute-start.16 = (bf16[512,128]{1,0:T(8,128)(2,1)S(1)}, bf16[512,128]{1,0:T(8,128)(2,1)S(1)}, u32[]{:S(2)}, u32[]{:S(2)}) collective-permute-start(bf16[512,128]{1,0:T(8,128)(2,1)S(1)} %slice.111), channel_id=1, source_target_pairs={{0,16},{16,32},{32,48},{48,64},{64,80},{80,96},{96,112},{112,0},{1... | collective-permute-start | bytes 393224 | tf_op jit(solution)/shard_map/ppermute | solution.py:21
  66.5 7.3 %collective-permute-start.17 = (bf16[512,128]{1,0:T(8,128)(2,1)S(1)}, bf16[512,128]{1,0:T(8,128)(2,1)S(1)}, u32[]{:S(2)}, u32[]{:S(2)}) collective-permute-start(bf16[512,128]{1,0:T(8,128)(2,1)S(1)} %slice.112), channel_id=1, source_target_pairs={{0,112},{16,0},{32,16},{48,32},{64,48},{80,64},{96,80},{112,96},{1... | collective-permute-start | bytes 393224 | tf_op jit(solution)/shard_map/ppermute | solution.py:21
  71.2 7.9 %collective-permute-start.24 = (bf16[256,512]{1,0:T(8,128)(2,1)S(1)}, bf16[256,512]{1,0:T(8,128)(2,1)S(1)}, u32[]{:S(2)}, u32[]{:S(2)}) collective-permute-start(bf16[256,512]{1,0:T(8,128)(2,1)S(1)} %get-tuple-element.128), channel_id=1, source_target_pairs={{0,16},{16,32},{32,48},{48,64},{64,80},{80,96},{96,112},{112,0},{1... | collective-permute-start | bytes 786440 | tf_op jit(solution)/shard_map/ppermute | solution.py:21
  71.5 7.6 %collective-permute-start.25 = (bf16[256,512]{1,0:T(8,128)(2,1)S(1)}, bf16[256,512]{1,0:T(8,128)(2,1)S(1)}, u32[]{:S(2)}, u32[]{:S(2)}) collective-permute-start(bf16[256,512]{1,0:T(8,128)(2,1)S(1)} %get-tuple-element.127), channel_id=1, source_target_pairs={{0,112},{16,0},{32,16},{48,32},{64,48},{80,64},{96,80},{112,96},{1... | collective-permute-start | bytes 786440 | tf_op jit(solution)/shard_map/ppermute | solution.py:21
  79.3 13.3 %collective-permute-start.26 = (bf16[256,512]{1,0:T(8,128)(2,1)S(1)}, bf16[256,512]{1,0:T(8,128)(2,1)S(1)}, u32[]{:S(2)}, u32[]{:S(2)}) collective-permute-start(bf16[256,512]{1,0:T(8,128)(2,1)S(1)} %get-tuple-element.126), channel_id=1, source_target_pairs={{0,16},{16,32},{32,48},{48,64},{64,80},{80,96},{96,112},{112,0},{1... | collective-permute-start | bytes 786440 | tf_op jit(solution)/shard_map/ppermute | solution.py:21
  79.7 12.9 %collective-permute-start.27 = (bf16[256,512]{1,0:T(8,128)(2,1)S(1)}, bf16[256,512]{1,0:T(8,128)(2,1)S(1)}, u32[]{:S(2)}, u32[]{:S(2)}) collective-permute-start(bf16[256,512]{1,0:T(8,128)(2,1)S(1)} %get-tuple-element.125), channel_id=1, source_target_pairs={{0,112},{16,0},{32,16},{48,32},{64,48},{80,64},{96,80},{112,96},{1... | collective-permute-start | bytes 786440 | tf_op jit(solution)/shard_map/ppermute | solution.py:21
  83.4 12.5 %collective-permute-start.19 = (bf16[512,256]{1,0:T(8,128)(2,1)S(1)}, bf16[512,256]{1,0:T(8,128)(2,1)S(1)}, u32[]{:S(2)}, u32[]{:S(2)}) collective-permute-start(bf16[512,256]{1,0:T(8,128)(2,1)S(1)} %shard_map.134.refs_1_), channel_id=1, source_target_pairs={{0,1},{1,2},{2,3},{3,4},{4,5},{5,6},{6,7},{7,8},{8,9},{9,10},{10,1... | collective-permute-start | bytes 786440 | tf_op jit(solution)/shard_map/ppermute | solution.py:39
  98.5 11.8 %collective-permute-start.28 = (bf16[512,256]{1,0:T(8,128)(2,1)S(1)}, bf16[512,256]{1,0:T(8,128)(2,1)S(1)}, u32[]{:S(2)}, u32[]{:S(2)}) collective-permute-start(bf16[512,256]{1,0:T(8,128)(2,1)S(1)} %get-tuple-element.90), channel_id=1, source_target_pairs={{1,0},{2,1},{3,2},{4,3},{5,4},{6,5},{7,6},{8,7},{9,8},{10,9},{11,1... | collective-permute-start | bytes 786440 | tf_op jit(solution)/shard_map/ppermute | solution.py:39
  100.5 9.8 %collective-permute-start.29 = (bf16[512,256]{1,0:T(8,128)(2,1)S(1)}, bf16[512,256]{1,0:T(8,128)(2,1)S(1)}, u32[]{:S(2)}, u32[]{:S(2)}) collective-permute-start(bf16[512,256]{1,0:T(8,128)(2,1)S(1)} %convert_element_type.90), channel_id=1, source_target_pairs={{0,128},{16,144},{32,160},{48,176},{64,192},{80,208},{96,224},{112... | collective-permute-start | bytes 786440 | tf_op jit(solution)/shard_map/ppermute | solution.py:25
  101.0 11.1 %collective-permute-start.30 = (bf16[512,256]{1,0:T(8,128)(2,1)S(1)}, bf16[512,256]{1,0:T(8,128)(2,1)S(1)}, u32[]{:S(2)}, u32[]{:S(2)}) collective-permute-start(bf16[512,256]{1,0:T(8,128)(2,1)S(1)} %get-tuple-element.90), channel_id=1, source_target_pairs={{129,0},{130,1},{131,2},{132,3},{133,4},{134,5},{135,6},{136,7},{1... | collective-permute-start | bytes 786440 | tf_op jit(solution)/shard_map/ppermute | solution.py:438
  124.4 6.8 %collective-permute-start.33 = (bf16[256,512]{1,0:T(8,128)(2,1)S(1)}, bf16[256,512]{1,0:T(8,128)(2,1)S(1)}, u32[]{:S(2)}, u32[]{:S(2)}) collective-permute-start(bf16[256,512]{1,0:T(8,128)(2,1)S(1)} %pad_maximum_fusion.4), channel_id=1, source_target_pairs={{0,16},{16,32},{32,48},{48,64},{64,80},{80,96},{96,112},{112,0},{1... | collective-permute-start | bytes 786440 | tf_op jit(solution)/shard_map/ppermute | solution.py:21
  124.8 8.0 %collective-permute-start.34 = (bf16[256,512]{1,0:T(8,128)(2,1)S(1)}, bf16[256,512]{1,0:T(8,128)(2,1)S(1)}, u32[]{:S(2)}, u32[]{:S(2)}) collective-permute-start(bf16[256,512]{1,0:T(8,128)(2,1)S(1)} %pad_maximum_fusion.5), channel_id=1, source_target_pairs={{0,112},{16,0},{32,16},{48,32},{64,48},{80,64},{96,80},{112,96},{1... | collective-permute-start | bytes 786440 | tf_op jit(solution)/shard_map/ppermute | solution.py:21
  133.3 7.1 %collective-permute-start.36 = (bf16[256,512]{1,0:T(8,128)(2,1)S(1)}, bf16[256,512]{1,0:T(8,128)(2,1)S(1)}, u32[]{:S(2)}, u32[]{:S(2)}) collective-permute-start(bf16[256,512]{1,0:T(8,128)(2,1)S(1)} %get-tuple-element.121), channel_id=1, source_target_pairs={{0,112},{16,0},{32,16},{48,32},{64,48},{80,64},{96,80},{112,96},{1... | collective-permute-start | bytes 786440 | tf_op jit(solution)/shard_map/ppermute | solution.py:21
  173.5 16.4 %all-to-all-start.1 = ((bf16[16,96,128]{2,1,0:T(8,128)(2,1)}), bf16[16,96,128]{2,1,0:T(8,128)(2,1)S(1)}, u32[]{:S(2)}, u32[]{:S(2)}) async-start(bf16[16,96,128]{2,1,0:T(8,128)(2,1)} %broadcast_in_dim.10), calls=%async_computation.1 | async-start | bytes 786432 | tf_op jit(solution)/shard_map/all_to_all | solution.py:427
  178.6 16.9 %collective-permute-start.39 = (bf16[512,256]{1,0:T(8,128)(2,1)S(1)}, bf16[512,256]{1,0:T(8,128)(2,1)S(1)}, u32[]{:S(2)}, u32[]{:S(2)}) collective-permute-start(bf16[512,256]{1,0:T(8,128)(2,1)S(1)} %get-tuple-element.107), channel_id=1, source_target_pairs={{1,0},{2,1},{3,2},{4,3},{5,4},{6,5},{7,6},{8,7},{9,8},{10,9},{11,1... | collective-permute-start | bytes 786440 | tf_op jit(solution)/shard_map/ppermute | solution.py:39
  190.7 15.0 %all-to-all-start.2 = ((bf16[16,96,128]{2,1,0:T(8,128)(2,1)}), bf16[16,96,128]{2,1,0:T(8,128)(2,1)S(1)}, u32[]{:S(2)}, u32[]{:S(2)}) async-start(bf16[16,96,128]{2,1,0:T(8,128)(2,1)} %broadcast_in_dim.11), calls=%async_computation.2 | async-start | bytes 786432 | tf_op jit(solution)/shard_map/all_to_all | solution.py:427
  (18 other events, 159.8 us)

commit v3 on v2

--- a/solution.py
+++ b/solution.py
@@ -430,7 +430,29 @@
 def sum_everywhere(chunks):
     mine = jnp.sum(exchanged(chunks, "tm"), axis=0).astype(BF)
     mine = jnp.sum(exchanged(jnp.broadcast_to(mine, (FIRMS,) + mine.shape), "firm"), axis=0).astype(BF)
-    return exchanged(jnp.broadcast_to(mine, chunks.shape), "tm")
+    return lax.all_to_all(jnp.broadcast_to(mine, chunks.shape), "tm", 0, 0)
+
+
+def unpack_kernel(factor, sums_ref, prev_ref, cur_ref, self_ref, nbr_ref):
+    for layer in range(L):
+
+        def rows(k):
+            return sums_ref[layer, 128 * k : 128 * (k + 1), :].astype(F32) * factor
+
+        self_ref[layer] = rows(0)
+        nbr_ref[layer] = rows(1)
+        for t in range(2):
+            cur_ref[layer, :, 128 * t : 128 * (t + 1)] = rows(2 + t)
+            prev_ref[layer, :, 128 * t : 128 * (t + 1)] = rows(4 + t)
+
+
+def unpack(sums, factor):
+    wide, narrow = (L, 128, 256), (L, 128, 128)
+    return whole_call(
+        lambda *refs: unpack_kernel(factor, *refs),
+        [(wide, F32), (wide, F32), (narrow, F32), (narrow, F32)],
+        [(sums, VMEM_WHOLE)],
+    )
 
 
 def from_pair_later(array):
@@ -449,10 +471,10 @@
     cot = cotangent.reshape(rows, days * width)
     lent = firm_xor(piece, NZ)
     prior = along_tm(behind(state, piece), 1)
+    prior, first = lax.optimization_barrier((prior, lent))
     gated = gate(dilations, state, prior, w_prev, w_cur)
 
     half = width
-    first = behind(lent, gated)
     before, after = along_x(first, 1), along_x(first, -1)
     other_first = tm_xor(first, 1)
     f1, b1 = along_z(gated, 1), along_z(gated, -1)
@@ -464,7 +486,8 @@
     f2, b2 = along_z(f1, 1), along_z(b1, -1)
     sides = jnp.concatenate([after, before], axis=0)
     other_sides = tm_xor(sides, 1)
-    f2, b2, cot_pair, far[0], far[1] = lax.optimization_barrier((f2, b2, cot_pair, far[0], far[1]))
+    far = list(lax.optimization_barrier(tuple(far)))
+    f2, b2 = lax.optimization_barrier((f2, b2))
     other_far = tm_xor(jnp.concatenate(far, axis=0), 1)
     f3, b3 = along_z(f2, 1), along_z(b2, -1)
     peer = gather_pieces(pos, [first, sides] + far + [other_first, other_sides, other_far])
@@ -488,12 +511,8 @@
     gx, back, sent = layer_back(0, dilations, [state, prior, gz, last, f, b] + weights, upper)
     grad = jnp.stack(joined(dilations[0] == 1, gx, along_tm(back, -1)), axis=1)
 
-    factor = 1.0 / jnp.sqrt(jnp.float32(rows * FIRMS * days * TMS))
-    sums = sum_everywhere(sent).reshape(L, 768, width) * factor
-    g_self, g_nbr = sums[:, 0:128], sums[:, 128:256]
-    g_cur = jnp.concatenate([sums[:, 256:384], sums[:, 384:512]], axis=2)
-    g_prev = jnp.concatenate([sums[:, 512:640], sums[:, 640:768]], axis=2)
-    return grad, g_prev, g_cur, g_self, g_nbr
+    factor = (rows * FIRMS * days * TMS) ** -0.5
+    return (grad,) + tuple(unpack(sum_everywhere(sent).reshape(L, 768, width), factor))
 
 
 def solution(mesh):

time: 211 us -> 220 us (1.043)
  waiting for transfers between devices: 84 us -> 95.4 us
    all_to_all x2 -> x1, waiting for transfers between devices: 17.2 us -> 8.34 us  [exchanged(): return lax.all_to_all(chunks, axis, 0, 0).astype(F32)]
    all_to_all x0 -> x1, waiting for transfers between devices: none -> 8.85 us  [sum_everywhere(): return lax.all_to_all(jnp.broadcast_to(mine, chunks.shape), 'tm', 0, 0)]
    ppermute x4, waiting for transfers between devices: 0.01 us -> 5.81 us  [along_x(): return lax.ppermute(array, 'tm', pairs)]
    all_to_all x2 -> x1, starting transfers between devices: 9.98 us -> 5.17 us  [exchanged(): return lax.all_to_all(chunks, axis, 0, 0).astype(F32)]
    all_to_all x0 -> x1, starting transfers between devices: none -> 4.8 us  [sum_everywhere(): return lax.all_to_all(jnp.broadcast_to(mine, chunks.shape), 'tm', 0, 0)]
    ppermute x24, waiting for transfers between devices: 43.3 us -> 47 us  [along_z(): return lax.ppermute(array, 'firm', pairs)]
    pallas_call x13 -> x14, Pallas kernels: 25.5 us -> 26.3 us  [whole_call(): pl.pallas_call(kernel, in_specs=[spec for _, spec in ins], out_specs=[VME...]
  transfers between devices with their start and end apart: 42 -> 42, of which waited for: 24 -> 28; matrix products, arithmetic and copies ran while one was open for 2% -> 1% of each run, Pallas kernels for 7% -> 6%
where the time goes in v3:
time: 220 us; the launch traced here: 217 us
  waiting for transfers between devices  95.4 us (43%)
  starting transfers between devices  65.6 us (30%)
  Pallas kernels  26.3 us (12%)
  blocking collectives  22.7 us (10%)
  local copies, waits for them, and re-layouts  3.78 us (2%)
    ppermute x24, waiting for transfers between devices, along_z(): return lax.ppermute(array, 'firm', pairs)  47 us
    pallas_call x14, Pallas kernels, whole_call(): pl.pallas_call(kernel, in_specs=[spec for _, spec in ins], out_specs=[VME...  26.3 us
    all_to_all x1, blocking collectives, exchanged(): return lax.all_to_all(chunks, axis, 0, 0).astype(F32)  22.7 us
    ppermute x24, starting transfers between devices, along_z(): return lax.ppermute(array, 'firm', pairs)  21.7 us
    ppermute x4, starting transfers between devices, along_tm(): return lax.ppermute(array, 'tm', pairs)  21.1 us
    ppermute x4, waiting for transfers between devices, along_tm(): return lax.ppermute(array, 'tm', pairs)  19.6 us
    all_to_all x1, waiting for transfers between devices, sum_everywhere(): return lax.all_to_all(jnp.broadcast_to(mine, chunks.shape), 'tm', 0, 0)  8.85 us
    all_to_all x1, waiting for transfers between devices, exchanged(): return lax.all_to_all(chunks, axis, 0, 0).astype(F32)  8.34 us
  transfers between devices with their start and end apart: 42, of which 28 were waited for; matrix products, arithmetic and copies ran while one was open for 1% of the time, Pallas kernels for 6%

profile of v3, /device:TPU:97, one launch (start us, length us, event | category | flops | bytes accessed | tf_op | source)
XLA Modules:
  0.0 216.5 jit_solution(18068546763259750921)
XLA Ops:
  4.6 5.4 %collective-permute-start = (bf16[512,256]{1,0:T(8,128)(2,1)S(1)}, bf16[512,256]{1,0:T(8,128)(2,1)S(1)}, u32[]{:S(2)}, u32[]{:S(2)}) collective-permute-start(bf16[512,256]{1,0:T(8,128)(2,1)S(1)} %bitcast.72), channel_id=1, source_target_pairs={{0,1},{1,2},{2,3},{3,4},{4,5},{5,6},{6,7},{7,8},{8,9},{9,10},{10,1... | collective-permute-start | bytes 786440 | tf_op jit(solution)/shard_map/ppermute | solution.py:39
  10.0 9.1 %collective-permute-done.prior_ref.refs_2_ = bf16[512,256]{1,0:T(8,128)(2,1)S(1)} collective-permute-done((bf16[512,256]{1,0:T(8,128)(2,1)S(1)}, bf16[512,256]{1,0:T(8,128)(2,1)S(1)}, u32[]{:S(2)}, u32[]{:S(2)}) %collective-permute-start) | collective-permute-done | bytes 262176 | tf_op jit(solution)/shard_map/ppermute | solution.py:39
  23.0 2.9 %collective-permute-start.4 = (bf16[512,256]{1,0:T(8,128)(2,1)S(1)}, bf16[512,256]{1,0:T(8,128)(2,1)S(1)}, u32[]{:S(2)}, u32[]{:S(2)}) collective-permute-start(bf16[512,256]{1,0:T(8,128)(2,1)S(1)} %shard_map.129.refs_0_.gated_ref), channel_id=1, source_target_pairs={{0,16},{16,32},{32,48},{48,64},{64,80},{80,96},{96,112},{112,0},{1... | collective-permute-start | bytes 786440 | tf_op jit(solution)/shard_map/ppermute | solution.py:21
  25.9 4.1 %shard_map.130 = (bf16[8,512,512]{2,1,0:T(8,128)(2,1)S(1)}, bf16[256,512]{1,0:T(8,128)(2,1)S(1)}) custom-call(s32[1]{0:T(128)} %bitcast.pos_ref, s32[4,64]{1,0:T(4,128)S(1)} %copy-done.4, bf16[512,256]{1,0:T(8,128)(2,1)S(1)} %bitcast.76, bf16[4,64,128,128]{3,2,1,0:T(8,128)(2,1)} %tiles_ref.3), custom_call_target="tpu_custom_call" | custom-call | bytes 9437184 | tf_op jit(solution)/shard_map/pallas_call | solution.py:51
  31.4 3.1 %collective-permute-done.5.refs_1_ = bf16[512,256]{1,0:T(8,128)(2,1)S(1)} collective-permute-done((bf16[512,256]{1,0:T(8,128)(2,1)S(1)}, bf16[512,256]{1,0:T(8,128)(2,1)S(1)}, u32[]{:S(2)}, u32[]{:S(2)}) %collective-permute-start.5) | collective-permute-done | bytes 262176 | tf_op jit(solution)/shard_map/ppermute | solution.py:21
  36.2 2.6 %collective-permute-start.7 = (bf16[256,512]{1,0:T(8,128)(2,1)S(1)}, bf16[256,512]{1,0:T(8,128)(2,1)S(1)}, u32[]{:S(2)}, u32[]{:S(2)}) collective-permute-start(bf16[256,512]{1,0:T(8,128)(2,1)S(1)} %slice.92), channel_id=1, source_target_pairs={{0,12},{1,13},{2,14},{3,15},{4,0},{5,1},{6,2},{7,3},{8,4},{9,5},{1... | collective-permute-start | bytes 786440 | tf_op jit(solution)/shard_map/ppermute | solution.py:34
  39.4 5.8 %collective-permute-done.6.far0_ref = bf16[256,512]{1,0:T(8,128)(2,1)S(1)} collective-permute-done((bf16[256,512]{1,0:T(8,128)(2,1)S(1)}, bf16[256,512]{1,0:T(8,128)(2,1)S(1)}, u32[]{:S(2)}, u32[]{:S(2)}) %collective-permute-start.6) | collective-permute-done | bytes 262176 | tf_op jit(solution)/shard_map/ppermute | solution.py:34
  47.9 6.1 %collective-permute-done.12.refs_7_ = bf16[512,256]{1,0:T(8,128)(2,1)S(1)} collective-permute-done((bf16[512,256]{1,0:T(8,128)(2,1)S(1)}, bf16[512,256]{1,0:T(8,128)(2,1)S(1)}, u32[]{:S(2)}, u32[]{:S(2)}) %collective-permute-start.12) | collective-permute-done | bytes 262176 | tf_op jit(solution)/shard_map/ppermute | solution.py:21
  54.1 2.5 %collective-permute-done.13.refs_2_ = bf16[512,256]{1,0:T(8,128)(2,1)S(1)} collective-permute-done((bf16[512,256]{1,0:T(8,128)(2,1)S(1)}, bf16[512,256]{1,0:T(8,128)(2,1)S(1)}, u32[]{:S(2)}, u32[]{:S(2)}) %collective-permute-start.13) | collective-permute-done | bytes 262176 | tf_op jit(solution)/shard_map/ppermute | solution.py:21
  58.4 2.5 %collective-permute-done.11.theirs_ref = bf16[256,512]{1,0:T(8,128)(2,1)S(1)} collective-permute-done((bf16[256,512]{1,0:T(8,128)(2,1)S(1)}, bf16[256,512]{1,0:T(8,128)(2,1)S(1)}, u32[]{:S(2)}, u32[]{:S(2)}) %collective-permute-start.11) | collective-permute-done | bytes 262176 | tf_op jit(solution)/shard_map/ppermute | solution.py:25
  61.4 3.5 %shard_map.135 = (f32[6,256,512]{2,1,0:T(8,128)S(1)}, f32[256,512]{1,0:T(8,128)S(1)}) custom-call(s32[1]{0:T(128)} %bitcast.pos_ref, bf16[8,512,512]{2,1,0:T(8,128)(2,1)S(1)} %get-tuple-element.66.own_ref, bf16[8,512,512]{2,1,0:T(8,128)(2,1)S(1)} %shard_map.131.peer_ref, bf16[256,512]{1,0:T(8,128)(2,1)S(1)} %get-tuple-element.71.mine_ref, ...), custom_call_target="tpu_custom_call" | custom-call | flops 1879048192 | bytes 1048576 | tf_op jit(solution)/shard_map/pallas_call | solution.py:51
  65.0 3.0 %collective-permute-start.20 = (bf16[128,512]{1,0:T(8,128)(2,1)S(1)}, bf16[128,512]{1,0:T(8,128)(2,1)S(1)}, u32[]{:S(2)}, u32[]{:S(2)}) collective-permute-start(bf16[128,512]{1,0:T(8,128)(2,1)S(1)} %get-tuple-element.148), channel_id=1, source_target_pairs={{0,16},{16,32},{32,48},{48,64},{64,80},{80,96},{96,112},{112,0},{1... | collective-permute-start | bytes 393224 | tf_op jit(solution)/shard_map/ppermute | solution.py:21
  70.0 3.1 %collective-permute-done.21 = bf16[128,512]{1,0:T(8,128)(2,1)S(1)} collective-permute-done((bf16[128,512]{1,0:T(8,128)(2,1)S(1)}, bf16[128,512]{1,0:T(8,128)(2,1)S(1)}, u32[]{:S(2)}, u32[]{:S(2)}) %collective-permute-start.21) | collective-permute-done | bytes 131104 | tf_op jit(solution)/shard_map/ppermute | solution.py:21
  76.5 2.0 collective-permute-done.22
  82.1 3.8 %shard_map.133 = (f32[512,256]{1,0:T(8,128)S(1)}, bf16[512,256]{1,0:T(8,128)(2,1)S(1)}) custom-call(s32[1]{0:T(128)} %bitcast.pos_ref, bf16[8,512,512]{2,1,0:T(8,128)(2,1)S(1)} %get-tuple-element.66.own_ref, bf16[8,512,512]{2,1,0:T(8,128)(2,1)S(1)} %shard_map.131.peer_ref, bf16[512,256]{1,0:T(8,128)(2,1)S(1)} %shard_map.129.refs_0_.gated_ref, ...), custom_call_target="tpu_custom_call" | custom-call | flops 2147483648 | bytes 1048576 | tf_op jit(solution)/shard_map/pallas_call | solution.py:51
  92.0 11.0 %collective-permute-start.19 = (bf16[512,256]{1,0:T(8,128)(2,1)S(1)}, bf16[512,256]{1,0:T(8,128)(2,1)S(1)}, u32[]{:S(2)}, u32[]{:S(2)}) collective-permute-start(bf16[512,256]{1,0:T(8,128)(2,1)S(1)} %shard_map.134.refs_1_), channel_id=1, source_target_pairs={{0,1},{1,2},{2,3},{3,4},{4,5},{5,6},{6,7},{7,8},{8,9},{9,10},{10,1... | collective-permute-start | bytes 786440 | tf_op jit(solution)/shard_map/ppermute | solution.py:39
  103.0 3.3 %collective-permute-done.19.refs_2_ = bf16[512,256]{1,0:T(8,128)(2,1)S(1)} collective-permute-done((bf16[512,256]{1,0:T(8,128)(2,1)S(1)}, bf16[512,256]{1,0:T(8,128)(2,1)S(1)}, u32[]{:S(2)}, u32[]{:S(2)}) %collective-permute-start.19) | collective-permute-done | bytes 262176 | tf_op jit(solution)/shard_map/ppermute | solution.py:39
  106.3 2.6 %shard_map.136 = (f32[512,256]{1,0:T(8,128)S(1)}, bf16[512,256]{1,0:T(8,128)(2,1)S(1)}, f32[768,128]{1,0:T(8,128)S(1)}) custom-call(s32[2]{0:T(128)S(1)} %copy-done.5, bf16[512,256]{1,0:T(8,128)(2,1)S(1)} %shard_map.134.refs_1_, bf16[512,256]{1,0:T(8,128)(2,1)S(1)} %collective-permute-done.19.refs_2_, bf16[512,256]{1,0:T(8,128)(2,1)S(1)} %bitcast.77, ...), custom_call_target="tpu_custom_call" | custom-call | flops 536870912 | bytes 4194304 | tf_op jit(solution)/shard_map/pallas_call | solution.py:51
  111.4 2.1 collective-permute-start.30
  113.5 7.2 %collective-permute-done.28.later_ref = bf16[512,256]{1,0:T(8,128)(2,1)S(1)} collective-permute-done((bf16[512,256]{1,0:T(8,128)(2,1)S(1)}, bf16[512,256]{1,0:T(8,128)(2,1)S(1)}, u32[]{:S(2)}, u32[]{:S(2)}) %collective-permute-start.28) | collective-permute-done | bytes 262176 | tf_op jit(solution)/shard_map/ppermute | solution.py:39
  123.8 3.5 %shard_map.139 = (f32[6,256,512]{2,1,0:T(8,128)S(1)}, f32[256,512]{1,0:T(8,128)S(1)}) custom-call(s32[1]{0:T(128)} %bitcast.pos_ref, bf16[8,512,512]{2,1,0:T(8,128)(2,1)S(1)} %get-tuple-element.66.own_ref, bf16[8,512,512]{2,1,0:T(8,128)(2,1)S(1)} %shard_map.131.peer_ref, bf16[256,512]{1,0:T(8,128)(2,1)S(1)} %get-tuple-element.96.mine_ref, ...), custom_call_target="tpu_custom_call" | custom-call | flops 1879048192 | bytes 1048576 | tf_op jit(solution)/shard_map/pallas_call | solution.py:51
  129.1 3.6 %collective-permute-done.31 = bf16[128,512]{1,0:T(8,128)(2,1)S(1)} collective-permute-done((bf16[128,512]{1,0:T(8,128)(2,1)S(1)}, bf16[128,512]{1,0:T(8,128)(2,1)S(1)}, u32[]{:S(2)}, u32[]{:S(2)}) %collective-permute-start.31) | collective-permute-done | bytes 131104 | tf_op jit(solution)/shard_map/ppermute | solution.py:21
  136.0 5.1 %collective-permute-done.33 = bf16[256,512]{1,0:T(8,128)(2,1)S(1)} collective-permute-done((bf16[256,512]{1,0:T(8,128)(2,1)S(1)}, bf16[256,512]{1,0:T(8,128)(2,1)S(1)}, u32[]{:S(2)}, u32[]{:S(2)}) %collective-permute-start.33) | collective-permute-done | bytes 262176 | tf_op jit(solution)/shard_map/ppermute | solution.py:21
  144.4 4.4 %collective-permute-done.35 = bf16[256,512]{1,0:T(8,128)(2,1)S(1)} collective-permute-done((bf16[256,512]{1,0:T(8,128)(2,1)S(1)}, bf16[256,512]{1,0:T(8,128)(2,1)S(1)}, u32[]{:S(2)}, u32[]{:S(2)}) %collective-permute-start.35) | collective-permute-done | bytes 262176 | tf_op jit(solution)/shard_map/ppermute | solution.py:21
  152.0 3.8 %collective-permute-done.37.refs_5_ = bf16[256,512]{1,0:T(8,128)(2,1)S(1)} collective-permute-done((bf16[256,512]{1,0:T(8,128)(2,1)S(1)}, bf16[256,512]{1,0:T(8,128)(2,1)S(1)}, u32[]{:S(2)}, u32[]{:S(2)}) %collective-permute-start.37) | collective-permute-done | bytes 262176 | tf_op jit(solution)/shard_map/ppermute | solution.py:21
  157.2 2.6 %shard_map.140 = (f32[512,256]{1,0:T(8,128)S(1)}, bf16[512,256]{1,0:T(8,128)(2,1)S(1)}, bf16[16,96,128]{2,1,0:T(8,128)(2,1)S(1)}) custom-call(s32[2]{0:T(128)S(1)} %copy-done.5, bf16[512,256]{1,0:T(8,128)(2,1)S(1)} %bitcast.75, bf16[512,256]{1,0:T(8,128)(2,1)S(1)} %collective-permute-done.prior_ref.refs_2_, f32[512,256]{1,0:T(8,128)S(1)} %get-tuple-element.95.refs_3_, ...), custom_call_target="tpu_custom_call" | custom-call | flops 536870912 | bytes 4194304 | tf_op jit(solution)/shard_map/pallas_call | solution.py:51
  159.8 22.7 %all_to_all.15 = bf16[16,96,128]{2,1,0:T(8,128)(2,1)S(1)} all-to-all(bf16[16,96,128]{2,1,0:T(8,128)(2,1)S(1)} %get-tuple-element.112), channel_id=1, replica_groups=mesh['firm'=16,'tm'=16] {'tm'}, dimensions={0} | all-to-all | bytes 786432 | tf_op jit(solution)/shard_map/all_to_all | solution.py:427
  183.4 5.2 %all-to-all-start.1 = ((bf16[16,96,128]{2,1,0:T(8,128)(2,1)}), bf16[16,96,128]{2,1,0:T(8,128)(2,1)S(1)}, u32[]{:S(2)}, u32[]{:S(2)}) async-start(bf16[16,96,128]{2,1,0:T(8,128)(2,1)} %broadcast_in_dim.10), calls=%async_computation.1 | async-start | bytes 786432 | tf_op jit(solution)/shard_map/all_to_all | solution.py:427
  188.6 2.8 %collective-permute-start.39 = (bf16[512,256]{1,0:T(8,128)(2,1)S(1)}, bf16[512,256]{1,0:T(8,128)(2,1)S(1)}, u32[]{:S(2)}, u32[]{:S(2)}) collective-permute-start(bf16[512,256]{1,0:T(8,128)(2,1)S(1)} %get-tuple-element.111), channel_id=1, source_target_pairs={{1,0},{2,1},{3,2},{4,3},{5,4},{6,5},{7,6},{8,7},{9,8},{10,9},{11,1... | collective-permute-start | bytes 786440 | tf_op jit(solution)/shard_map/ppermute | solution.py:39
  191.5 8.3 %all-to-all-done.1 = bf16[16,96,128]{2,1,0:T(8,128)(2,1)S(1)} async-done(((bf16[16,96,128]{2,1,0:T(8,128)(2,1)}), bf16[16,96,128]{2,1,0:T(8,128)(2,1)S(1)}, u32[]{:S(2)}, u32[]{:S(2)}) %all-to-all-start.1) | async-done | bytes 393248 | tf_op jit(solution)/shard_map/all_to_all | solution.py:427
  200.7 4.8 %all-to-all-start.2 = ((bf16[16,96,128]{2,1,0:T(8,128)(2,1)}), bf16[16,96,128]{2,1,0:T(8,128)(2,1)S(1)}, u32[]{:S(2)}, u32[]{:S(2)}) async-start(bf16[16,96,128]{2,1,0:T(8,128)(2,1)} %broadcast_in_dim.11), calls=%async_computation.2 | async-start | bytes 786432 | tf_op jit(solution)/shard_map/all_to_all | solution.py:433
  206.8 8.9 %all-to-all-done.2 = bf16[16,96,128]{2,1,0:T(8,128)(2,1)S(1)} async-done(((bf16[16,96,128]{2,1,0:T(8,128)(2,1)}), bf16[16,96,128]{2,1,0:T(8,128)(2,1)S(1)}, u32[]{:S(2)}, u32[]{:S(2)}) %all-to-all-start.2) | async-done | bytes 393248 | tf_op jit(solution)/shard_map/all_to_all | solution.py:433
  (116 shorter events, 54.1 us)
Async XLA Ops:
  3.2 15.9 %collective-permute-start.1 = (bf16[512,512]{1,0:T(8,128)(2,1)S(1)}, bf16[512,512]{1,0:T(8,128)(2,1)S(1)}, u32[]{:S(2)}, u32[]{:S(2)}) collective-permute-start(bf16[512,512]{1,0:T(8,128)(2,1)S(1)} %shard_map.128), channel_id=1, source_target_pairs={{0,128},{16,144},{32,160},{48,176},{64,192},{80,208},{96,224},{112... | collective-permute-start | bytes 1572872 | tf_op jit(solution)/shard_map/ppermute | solution.py:25
  4.6 14.5 %collective-permute-start = (bf16[512,256]{1,0:T(8,128)(2,1)S(1)}, bf16[512,256]{1,0:T(8,128)(2,1)S(1)}, u32[]{:S(2)}, u32[]{:S(2)}) collective-permute-start(bf16[512,256]{1,0:T(8,128)(2,1)S(1)} %bitcast.72), channel_id=1, source_target_pairs={{0,1},{1,2},{2,3},{3,4},{4,5},{5,6},{6,7},{7,8},{8,9},{9,10},{10,1... | collective-permute-start | bytes 786440 | tf_op jit(solution)/shard_map/ppermute | solution.py:39
  19.1 15.4 %collective-permute-start.2 = (bf16[512,512]{1,0:T(8,128)(2,1)S(1)}, bf16[512,512]{1,0:T(8,128)(2,1)S(1)}, u32[]{:S(2)}, u32[]{:S(2)}) collective-permute-start(bf16[512,512]{1,0:T(8,128)(2,1)S(1)} %collective-permute-done.1.first_ref), channel_id=1, source_target_pairs={{0,4},{1,5},{2,6},{3,7},{4,8},{5,9},{6,10},{7,11},{8,12},{9,13},{1... | collective-permute-start | bytes 1572872 | tf_op jit(solution)/shard_map/ppermute | solution.py:34
  20.4 14.2 %collective-permute-start.3 = (bf16[512,512]{1,0:T(8,128)(2,1)S(1)}, bf16[512,512]{1,0:T(8,128)(2,1)S(1)}, u32[]{:S(2)}, u32[]{:S(2)}) collective-permute-start(bf16[512,512]{1,0:T(8,128)(2,1)S(1)} %collective-permute-done.1.first_ref), channel_id=1, source_target_pairs={{0,12},{1,13},{2,14},{3,15},{4,0},{5,1},{6,2},{7,3},{8,4},{9,5},{1... | collective-permute-start | bytes 1572872 | tf_op jit(solution)/shard_map/ppermute | solution.py:34
  23.0 8.4 %collective-permute-start.4 = (bf16[512,256]{1,0:T(8,128)(2,1)S(1)}, bf16[512,256]{1,0:T(8,128)(2,1)S(1)}, u32[]{:S(2)}, u32[]{:S(2)}) collective-permute-start(bf16[512,256]{1,0:T(8,128)(2,1)S(1)} %shard_map.129.refs_0_.gated_ref), channel_id=1, source_target_pairs={{0,16},{16,32},{32,48},{48,64},{64,80},{80,96},{96,112},{112,0},{1... | collective-permute-start | bytes 786440 | tf_op jit(solution)/shard_map/ppermute | solution.py:21
  25.9 8.6 %collective-permute-start.5 = (bf16[512,256]{1,0:T(8,128)(2,1)S(1)}, bf16[512,256]{1,0:T(8,128)(2,1)S(1)}, u32[]{:S(2)}, u32[]{:S(2)}) collective-permute-start(bf16[512,256]{1,0:T(8,128)(2,1)S(1)} %shard_map.129.refs_0_.gated_ref), channel_id=1, source_target_pairs={{0,112},{16,0},{32,16},{48,32},{64,48},{80,64},{96,80},{112,96},{1... | collective-permute-start | bytes 786440 | tf_op jit(solution)/shard_map/ppermute | solution.py:21
  34.6 23.5 %collective-permute-start.9 = (bf16[1024,512]{1,0:T(8,128)(2,1)S(1)}, bf16[1024,512]{1,0:T(8,128)(2,1)S(1)}, u32[]{:S(2)}, u32[]{:S(2)}) collective-permute-start(bf16[1024,512]{1,0:T(8,128)(2,1)S(1)} %constant_dynamic-update-slice_fusion.sides_ref), channel_id=1, source_target_pairs={{0,1},{1,0},{2,3},{3,2},{4,5},{5,4},{6,7},{7,6},{8,9},{9,8},{10,11... | collective-permute-start | bytes 3145736 | tf_op jit(solution)/shard_map/ppermute | solution.py:29
  36.1 9.1 %collective-permute-start.6 = (bf16[256,512]{1,0:T(8,128)(2,1)S(1)}, bf16[256,512]{1,0:T(8,128)(2,1)S(1)}, u32[]{:S(2)}, u32[]{:S(2)}) collective-permute-start(bf16[256,512]{1,0:T(8,128)(2,1)S(1)} %slice.91), channel_id=1, source_target_pairs={{0,4},{1,5},{2,6},{3,7},{4,8},{5,9},{6,10},{7,11},{8,12},{9,13},{1... | collective-permute-start | bytes 786440 | tf_op jit(solution)/shard_map/ppermute | solution.py:34
  36.2 9.0 %collective-permute-start.7 = (bf16[256,512]{1,0:T(8,128)(2,1)S(1)}, bf16[256,512]{1,0:T(8,128)(2,1)S(1)}, u32[]{:S(2)}, u32[]{:S(2)}) collective-permute-start(bf16[256,512]{1,0:T(8,128)(2,1)S(1)} %slice.92), channel_id=1, source_target_pairs={{0,12},{1,13},{2,14},{3,15},{4,0},{5,1},{6,2},{7,3},{8,4},{9,5},{1... | collective-permute-start | bytes 786440 | tf_op jit(solution)/shard_map/ppermute | solution.py:34
  38.8 18.3 %collective-permute-start.8 = (bf16[512,512]{1,0:T(8,128)(2,1)S(1)}, bf16[512,512]{1,0:T(8,128)(2,1)S(1)}, u32[]{:S(2)}, u32[]{:S(2)}) collective-permute-start(bf16[512,512]{1,0:T(8,128)(2,1)S(1)} %collective-permute-done.1.first_ref), channel_id=1, source_target_pairs={{0,1},{1,0},{2,3},{3,2},{4,5},{5,4},{6,7},{7,6},{8,9},{9,8},{10,11... | collective-permute-start | bytes 1572872 | tf_op jit(solution)/shard_map/ppermute | solution.py:29
  45.2 12.9 %collective-permute-start.10 = (bf16[512,512]{1,0:T(8,128)(2,1)S(1)}, bf16[512,512]{1,0:T(8,128)(2,1)S(1)}, u32[]{:S(2)}, u32[]{:S(2)}) collective-permute-start(bf16[512,512]{1,0:T(8,128)(2,1)S(1)} %pad_maximum_fusion), channel_id=1, source_target_pairs={{0,1},{1,0},{2,3},{3,2},{4,5},{5,4},{6,7},{7,6},{8,9},{9,8},{10,11... | collective-permute-start | bytes 1572872 | tf_op jit(solution)/shard_map/ppermute | solution.py:29
  46.2 7.8 %collective-permute-start.12 = (bf16[512,256]{1,0:T(8,128)(2,1)S(1)}, bf16[512,256]{1,0:T(8,128)(2,1)S(1)}, u32[]{:S(2)}, u32[]{:S(2)}) collective-permute-start(bf16[512,256]{1,0:T(8,128)(2,1)S(1)} %collective-permute-done.4.refs_8_), channel_id=1, source_target_pairs={{0,16},{16,32},{32,48},{48,64},{64,80},{80,96},{96,112},{112,0},{1... | collective-permute-start | bytes 786440 | tf_op jit(solution)/shard_map/ppermute | solution.py:21
  47.9 8.7 %collective-permute-start.13 = (bf16[512,256]{1,0:T(8,128)(2,1)S(1)}, bf16[512,256]{1,0:T(8,128)(2,1)S(1)}, u32[]{:S(2)}, u32[]{:S(2)}) collective-permute-start(bf16[512,256]{1,0:T(8,128)(2,1)S(1)} %collective-permute-done.5.refs_1_), channel_id=1, source_target_pairs={{0,112},{16,0},{32,16},{48,32},{64,48},{80,64},{96,80},{112,96},{1... | collective-permute-start | bytes 786440 | tf_op jit(solution)/shard_map/ppermute | solution.py:21
  54.0 6.9 %collective-permute-start.11 = (bf16[256,512]{1,0:T(8,128)(2,1)S(1)}, bf16[256,512]{1,0:T(8,128)(2,1)S(1)}, u32[]{:S(2)}, u32[]{:S(2)}) collective-permute-start(bf16[256,512]{1,0:T(8,128)(2,1)S(1)} %get-tuple-element.71.mine_ref), channel_id=1, source_target_pairs={{0,128},{16,144},{32,160},{48,176},{64,192},{80,208},{96,224},{112... | collective-permute-start | bytes 786440 | tf_op jit(solution)/shard_map/ppermute | solution.py:25
  56.6 18.2 %collective-permute-start.14 = (bf16[512,256]{1,0:T(8,128)(2,1)S(1)}, bf16[512,256]{1,0:T(8,128)(2,1)S(1)}, u32[]{:S(2)}, u32[]{:S(2)}) collective-permute-start(bf16[512,256]{1,0:T(8,128)(2,1)S(1)} %collective-permute-done.12.refs_7_), channel_id=1, source_target_pairs={{0,16},{16,32},{32,48},{48,64},{64,80},{80,96},{96,112},{112,0},{1... | collective-permute-start | bytes 786440 | tf_op jit(solution)/shard_map/ppermute | solution.py:21
  57.1 17.8 %collective-permute-start.15 = (bf16[512,256]{1,0:T(8,128)(2,1)S(1)}, bf16[512,256]{1,0:T(8,128)(2,1)S(1)}, u32[]{:S(2)}, u32[]{:S(2)}) collective-permute-start(bf16[512,256]{1,0:T(8,128)(2,1)S(1)} %collective-permute-done.13.refs_2_), channel_id=1, source_target_pairs={{0,112},{16,0},{32,16},{48,32},{64,48},{80,64},{96,80},{112,96},{1... | collective-permute-start | bytes 786440 | tf_op jit(solution)/shard_map/ppermute | solution.py:21
  73.3 6.5 %collective-permute-start.23 = (bf16[256,512]{1,0:T(8,128)(2,1)S(1)}, bf16[256,512]{1,0:T(8,128)(2,1)S(1)}, u32[]{:S(2)}, u32[]{:S(2)}) collective-permute-start(bf16[256,512]{1,0:T(8,128)(2,1)S(1)} %pad_maximum_fusion.3), channel_id=1, source_target_pairs={{0,112},{16,0},{32,16},{48,32},{64,48},{80,64},{96,80},{112,96},{1... | collective-permute-start | bytes 786440 | tf_op jit(solution)/shard_map/ppermute | solution.py:21
  74.8 6.7 %collective-permute-start.16 = (bf16[512,128]{1,0:T(8,128)(2,1)S(1)}, bf16[512,128]{1,0:T(8,128)(2,1)S(1)}, u32[]{:S(2)}, u32[]{:S(2)}) collective-permute-start(bf16[512,128]{1,0:T(8,128)(2,1)S(1)} %slice.93), channel_id=1, source_target_pairs={{0,16},{16,32},{32,48},{48,64},{64,80},{80,96},{96,112},{112,0},{1... | collective-permute-start | bytes 393224 | tf_op jit(solution)/shard_map/ppermute | solution.py:21
  80.0 7.2 %collective-permute-start.24 = (bf16[256,512]{1,0:T(8,128)(2,1)S(1)}, bf16[256,512]{1,0:T(8,128)(2,1)S(1)}, u32[]{:S(2)}, u32[]{:S(2)}) collective-permute-start(bf16[256,512]{1,0:T(8,128)(2,1)S(1)} %get-tuple-element.136), channel_id=1, source_target_pairs={{0,16},{16,32},{32,48},{48,64},{64,80},{80,96},{96,112},{112,0},{1... | collective-permute-start | bytes 786440 | tf_op jit(solution)/shard_map/ppermute | solution.py:21
  80.1 8.2 %collective-permute-start.25 = (bf16[256,512]{1,0:T(8,128)(2,1)S(1)}, bf16[256,512]{1,0:T(8,128)(2,1)S(1)}, u32[]{:S(2)}, u32[]{:S(2)}) collective-permute-start(bf16[256,512]{1,0:T(8,128)(2,1)S(1)} %get-tuple-element.135), channel_id=1, source_target_pairs={{0,112},{16,0},{32,16},{48,32},{64,48},{80,64},{96,80},{112,96},{1... | collective-permute-start | bytes 786440 | tf_op jit(solution)/shard_map/ppermute | solution.py:21
  88.5 14.5 %collective-permute-start.26 = (bf16[256,512]{1,0:T(8,128)(2,1)S(1)}, bf16[256,512]{1,0:T(8,128)(2,1)S(1)}, u32[]{:S(2)}, u32[]{:S(2)}) collective-permute-start(bf16[256,512]{1,0:T(8,128)(2,1)S(1)} %get-tuple-element.134), channel_id=1, source_target_pairs={{0,16},{16,32},{32,48},{48,64},{64,80},{80,96},{96,112},{112,0},{1... | collective-permute-start | bytes 786440 | tf_op jit(solution)/shard_map/ppermute | solution.py:21
  88.6 14.5 %collective-permute-start.27 = (bf16[256,512]{1,0:T(8,128)(2,1)S(1)}, bf16[256,512]{1,0:T(8,128)(2,1)S(1)}, u32[]{:S(2)}, u32[]{:S(2)}) collective-permute-start(bf16[256,512]{1,0:T(8,128)(2,1)S(1)} %get-tuple-element.133), channel_id=1, source_target_pairs={{0,112},{16,0},{32,16},{48,32},{64,48},{80,64},{96,80},{112,96},{1... | collective-permute-start | bytes 786440 | tf_op jit(solution)/shard_map/ppermute | solution.py:21
  92.0 14.3 %collective-permute-start.19 = (bf16[512,256]{1,0:T(8,128)(2,1)S(1)}, bf16[512,256]{1,0:T(8,128)(2,1)S(1)}, u32[]{:S(2)}, u32[]{:S(2)}) collective-permute-start(bf16[512,256]{1,0:T(8,128)(2,1)S(1)} %shard_map.134.refs_1_), channel_id=1, source_target_pairs={{0,1},{1,2},{2,3},{3,4},{4,5},{5,6},{6,7},{7,8},{8,9},{9,10},{10,1... | collective-permute-start | bytes 786440 | tf_op jit(solution)/shard_map/ppermute | solution.py:39
  108.9 11.8 %collective-permute-start.28 = (bf16[512,256]{1,0:T(8,128)(2,1)S(1)}, bf16[512,256]{1,0:T(8,128)(2,1)S(1)}, u32[]{:S(2)}, u32[]{:S(2)}) collective-permute-start(bf16[512,256]{1,0:T(8,128)(2,1)S(1)} %get-tuple-element.94), channel_id=1, source_target_pairs={{1,0},{2,1},{3,2},{4,3},{5,4},{6,5},{7,6},{8,7},{9,8},{10,9},{11,1... | collective-permute-start | bytes 786440 | tf_op jit(solution)/shard_map/ppermute | solution.py:39
  110.9 9.8 %collective-permute-start.29 = (bf16[512,256]{1,0:T(8,128)(2,1)S(1)}, bf16[512,256]{1,0:T(8,128)(2,1)S(1)}, u32[]{:S(2)}, u32[]{:S(2)}) collective-permute-start(bf16[512,256]{1,0:T(8,128)(2,1)S(1)} %convert_element_type.87), channel_id=1, source_target_pairs={{0,128},{16,144},{32,160},{48,176},{64,192},{80,208},{96,224},{112... | collective-permute-start | bytes 786440 | tf_op jit(solution)/shard_map/ppermute | solution.py:25
  111.4 11.1 %collective-permute-start.30 = (bf16[512,256]{1,0:T(8,128)(2,1)S(1)}, bf16[512,256]{1,0:T(8,128)(2,1)S(1)}, u32[]{:S(2)}, u32[]{:S(2)}) collective-permute-start(bf16[512,256]{1,0:T(8,128)(2,1)S(1)} %get-tuple-element.94), channel_id=1, source_target_pairs={{129,0},{130,1},{131,2},{132,3},{133,4},{134,5},{135,6},{136,7},{1... | collective-permute-start | bytes 786440 | tf_op jit(solution)/shard_map/ppermute | solution.py:460
  134.3 6.8 %collective-permute-start.33 = (bf16[256,512]{1,0:T(8,128)(2,1)S(1)}, bf16[256,512]{1,0:T(8,128)(2,1)S(1)}, u32[]{:S(2)}, u32[]{:S(2)}) collective-permute-start(bf16[256,512]{1,0:T(8,128)(2,1)S(1)} %pad_maximum_fusion.4), channel_id=1, source_target_pairs={{0,16},{16,32},{32,48},{48,64},{64,80},{80,96},{96,112},{112,0},{1... | collective-permute-start | bytes 786440 | tf_op jit(solution)/shard_map/ppermute | solution.py:21
  134.7 8.0 %collective-permute-start.34 = (bf16[256,512]{1,0:T(8,128)(2,1)S(1)}, bf16[256,512]{1,0:T(8,128)(2,1)S(1)}, u32[]{:S(2)}, u32[]{:S(2)}) collective-permute-start(bf16[256,512]{1,0:T(8,128)(2,1)S(1)} %pad_maximum_fusion.5), channel_id=1, source_target_pairs={{0,112},{16,0},{32,16},{48,32},{64,48},{80,64},{96,80},{112,96},{1... | collective-permute-start | bytes 786440 | tf_op jit(solution)/shard_map/ppermute | solution.py:21
  143.2 7.1 %collective-permute-start.36 = (bf16[256,512]{1,0:T(8,128)(2,1)S(1)}, bf16[256,512]{1,0:T(8,128)(2,1)S(1)}, u32[]{:S(2)}, u32[]{:S(2)}) collective-permute-start(bf16[256,512]{1,0:T(8,128)(2,1)S(1)} %get-tuple-element.129), channel_id=1, source_target_pairs={{0,112},{16,0},{32,16},{48,32},{64,48},{80,64},{96,80},{112,96},{1... | collective-permute-start | bytes 786440 | tf_op jit(solution)/shard_map/ppermute | solution.py:21
  183.4 16.4 %all-to-all-start.1 = ((bf16[16,96,128]{2,1,0:T(8,128)(2,1)}), bf16[16,96,128]{2,1,0:T(8,128)(2,1)S(1)}, u32[]{:S(2)}, u32[]{:S(2)}) async-start(bf16[16,96,128]{2,1,0:T(8,128)(2,1)} %broadcast_in_dim.10), calls=%async_computation.1 | async-start | bytes 786432 | tf_op jit(solution)/shard_map/all_to_all | solution.py:427
  188.6 16.9 %collective-permute-start.39 = (bf16[512,256]{1,0:T(8,128)(2,1)S(1)}, bf16[512,256]{1,0:T(8,128)(2,1)S(1)}, u32[]{:S(2)}, u32[]{:S(2)}) collective-permute-start(bf16[512,256]{1,0:T(8,128)(2,1)S(1)} %get-tuple-element.111), channel_id=1, source_target_pairs={{1,0},{2,1},{3,2},{4,3},{5,4},{6,5},{7,6},{8,7},{9,8},{10,9},{11,1... | collective-permute-start | bytes 786440 | tf_op jit(solution)/shard_map/ppermute | solution.py:39
  200.7 15.0 %all-to-all-start.2 = ((bf16[16,96,128]{2,1,0:T(8,128)(2,1)}), bf16[16,96,128]{2,1,0:T(8,128)(2,1)S(1)}, u32[]{:S(2)}, u32[]{:S(2)}) async-start(bf16[16,96,128]{2,1,0:T(8,128)(2,1)} %broadcast_in_dim.11), calls=%async_computation.2 | async-start | bytes 786432 | tf_op jit(solution)/shard_map/all_to_all | solution.py:433
  (18 other events, 168.5 us)

commit v4 on v3

--- a/solution.py
+++ b/solution.py
@@ -466,35 +466,35 @@
     pos = (firm * TMS + tm).astype(jnp.int32).reshape(1)
     weights = [w_prev, w_cur, w_self, w_nbr]
 
-    piece = lend(pos, mask, tiles)
     state = features.reshape(rows, days * width)
     cot = cotangent.reshape(rows, days * width)
-    lent = firm_xor(piece, NZ)
-    prior = along_tm(behind(state, piece), 1)
-    prior, first = lax.optimization_barrier((prior, lent))
+    prior = along_tm(state, 1)
+    lent = firm_xor(lend(pos, mask, tiles), NZ)
     gated = gate(dilations, state, prior, w_prev, w_cur)
 
     half = width
-    before, after = along_x(first, 1), along_x(first, -1)
-    other_first = tm_xor(first, 1)
     f1, b1 = along_z(gated, 1), along_z(gated, -1)
     pos_then = behind(pos, gated)
     own, cot_turned = prepare(pos_then, mask, tiles, cot)
+    first = behind(lent, own)
+    before, after = along_x(first, 1), along_x(first, -1)
+    other_first = tm_xor(first, 1)
+    f1, b1 = lax.optimization_barrier((f1, b1))
+    f2, b2 = along_z(f1, 1), along_z(b1, -1)
     cot_pair = firm_xor(cot_turned, NZ)
-    before, after, own, f1, b1 = lax.optimization_barrier((before, after, own, f1, b1))
+    before, after = lax.optimization_barrier((before, after))
     far = [along_x(before[:256], 1), along_x(after[256:], -1)]
-    f2, b2 = along_z(f1, 1), along_z(b1, -1)
     sides = jnp.concatenate([after, before], axis=0)
     other_sides = tm_xor(sides, 1)
+    f2, b2 = lax.optimization_barrier((f2, b2))
+    f3, b3 = along_z(f2, 1), along_z(b2, -1)
     far = list(lax.optimization_barrier(tuple(far)))
-    f2, b2 = lax.optimization_barrier((f2, b2))
     other_far = tm_xor(jnp.concatenate(far, axis=0), 1)
-    f3, b3 = along_z(f2, 1), along_z(b2, -1)
-    peer = gather_pieces(pos, [first, sides] + far + [other_first, other_sides, other_far])
-    send, parts, last = spread_backward(pos, own, peer, cot_turned, cot_pair)
     f3, b3 = lax.optimization_barrier((f3, b3))
     f4, b4 = along_z(f3[:, :half], 1), along_z(b3[:, half:], -1)
     f4, b4 = lax.optimization_barrier((f4, b4))
+    peer = gather_pieces(pos, [first, sides] + far + [other_first, other_sides, other_far])
+    send, parts, last = spread_backward(pos, own, peer, cot_turned, cot_pair)
     pieces = [gated, b1, b2, b3, f4, b4, f3, f2, f1]
 
     pos_then = behind(pos, send)
@@ -504,8 +504,10 @@
     f, b = ring_sum(send, parts)
     gx, back, upper = layer_back(1, dilations, [next_state, next_prior, cot, last, f, b] + weights)
 
+    later = along_tm(back, -1)
+    later_pair = from_pair_later(back)
     gx_pair = firm_xor(gx.astype(BF), NZ)
-    gz, gz_turned, gz_pair = join(dilations, gx, along_tm(back, -1), gx_pair, from_pair_later(back))
+    gz, gz_turned, gz_pair = join(dilations, gx, later, gx_pair, later_pair)
     send, parts, last = spread_backward(pos, own, peer, gz_turned, gz_pair)
     f, b = ring_sum(send, parts)
     gx, back, sent = layer_back(0, dilations, [state, prior, gz, last, f, b] + weights, upper)

time: 220 us -> 221 us (level)
  starting transfers between devices: 65.6 us -> 74.2 us
  blocking collectives: 22.7 us -> 18.6 us
  waiting for transfers between devices: 95.4 us -> 91.9 us
    ppermute x24, starting transfers between devices: 21.7 us -> 29.7 us  [along_z(): return lax.ppermute(array, 'firm', pairs)]
    ppermute x24, waiting for transfers between devices: 47 us -> 39.6 us  [along_z(): return lax.ppermute(array, 'firm', pairs)]
    all_to_all x1, blocking collectives: 22.7 us -> 18.6 us  [exchanged(): return lax.all_to_all(chunks, axis, 0, 0).astype(F32)]
    ppermute x4, waiting for transfers between devices: 5.81 us -> 9.7 us  [along_x(): return lax.ppermute(array, 'tm', pairs)]
  transfers between devices with their start and end apart: 42 -> 42, of which waited for: 28 -> 26; matrix products, arithmetic and copies ran while one was open for 1% -> 2% of each run, Pallas kernels for 6% -> 8%
where the time goes in v4:
time: 221 us; the launch traced here: 218 us
  waiting for transfers between devices  91.9 us (42%)
  starting transfers between devices  74.2 us (34%)
  Pallas kernels  26.3 us (12%)
  blocking collectives  18.6 us (8%)
  local copies, waits for them, and re-layouts  3.79 us (2%)
    ppermute x24, waiting for transfers between devices, along_z(): return lax.ppermute(array, 'firm', pairs)  39.6 us
    ppermute x24, starting transfers between devices, along_z(): return lax.ppermute(array, 'firm', pairs)  29.7 us
    pallas_call x14, Pallas kernels, whole_call(): pl.pallas_call(kernel, in_specs=[spec for _, spec in ins], out_specs=[VME...  26.3 us
    ppermute x4, starting transfers between devices, along_tm(): return lax.ppermute(array, 'tm', pairs)  21.2 us
    ppermute x4, waiting for transfers between devices, along_tm(): return lax.ppermute(array, 'tm', pairs)  19.6 us
    all_to_all x1, blocking collectives, exchanged(): return lax.all_to_all(chunks, axis, 0, 0).astype(F32)  18.6 us
    ppermute x4, waiting for transfers between devices, along_x(): return lax.ppermute(array, 'tm', pairs)  9.7 us
    all_to_all x1, waiting for transfers between devices, sum_everywhere(): return lax.all_to_all(jnp.broadcast_to(mine, chunks.shape), 'tm', 0, 0)  8.79 us
  transfers between devices with their start and end apart: 42, of which 26 were waited for; matrix products, arithmetic and copies ran while one was open for 2% of the time, Pallas kernels for 8%

profile of v4, /device:TPU:97, one launch (start us, length us, event | category | flops | bytes accessed | tf_op | source)
XLA Modules:
  0.0 217.6 jit_solution(5362528101901717853)
XLA Ops:
  4.6 5.4 %collective-permute-start = (bf16[512,256]{1,0:T(8,128)(2,1)S(1)}, bf16[512,256]{1,0:T(8,128)(2,1)S(1)}, u32[]{:S(2)}, u32[]{:S(2)}) collective-permute-start(bf16[512,256]{1,0:T(8,128)(2,1)S(1)} %bitcast.72), channel_id=1, source_target_pairs={{0,1},{1,2},{2,3},{3,4},{4,5},{5,6},{6,7},{7,8},{8,9},{9,10},{10,1... | collective-permute-start | bytes 786440 | tf_op jit(solution)/shard_map/ppermute | solution.py:39
  10.1 9.1 %collective-permute-done.prior_ref.refs_2_ = bf16[512,256]{1,0:T(8,128)(2,1)S(1)} collective-permute-done((bf16[512,256]{1,0:T(8,128)(2,1)S(1)}, bf16[512,256]{1,0:T(8,128)(2,1)S(1)}, u32[]{:S(2)}, u32[]{:S(2)}) %collective-permute-start) | collective-permute-done | bytes 262176 | tf_op jit(solution)/shard_map/ppermute | solution.py:39
  20.3 4.1 %shard_map.129 = (bf16[8,512,512]{2,1,0:T(8,128)(2,1)S(1)}, bf16[256,512]{1,0:T(8,128)(2,1)S(1)}) custom-call(s32[1]{0:T(128)} %bitcast.pos_ref, s32[4,64]{1,0:T(4,128)S(1)} %copy-done.5, bf16[512,256]{1,0:T(8,128)(2,1)S(1)} %bitcast.76, bf16[4,64,128,128]{3,2,1,0:T(8,128)(2,1)} %tiles_ref.3), custom_call_target="tpu_custom_call" | custom-call | bytes 9437184 | tf_op jit(solution)/shard_map/pallas_call | solution.py:51
  27.1 8.8 %collective-permute-done.2 = bf16[512,512]{1,0:T(8,128)(2,1)S(1)} collective-permute-done((bf16[512,512]{1,0:T(8,128)(2,1)S(1)}, bf16[512,512]{1,0:T(8,128)(2,1)S(1)}, u32[]{:S(2)}, u32[]{:S(2)}) %collective-permute-start.2) | collective-permute-done | bytes 524320 | tf_op jit(solution)/shard_map/ppermute | solution.py:34
  36.9 2.9 %collective-permute-start.10 = (bf16[512,256]{1,0:T(8,128)(2,1)S(1)}, bf16[512,256]{1,0:T(8,128)(2,1)S(1)}, u32[]{:S(2)}, u32[]{:S(2)}) collective-permute-start(bf16[512,256]{1,0:T(8,128)(2,1)S(1)} %shard_map.128.refs_0_.gated_ref), channel_id=1, source_target_pairs={{0,16},{16,32},{32,48},{48,64},{64,80},{80,96},{96,112},{112,0},{1... | collective-permute-start | bytes 786440 | tf_op jit(solution)/shard_map/ppermute | solution.py:21
  50.0 2.7 %collective-permute-start.12 = (bf16[512,256]{1,0:T(8,128)(2,1)S(1)}, bf16[512,256]{1,0:T(8,128)(2,1)S(1)}, u32[]{:S(2)}, u32[]{:S(2)}) collective-permute-start(bf16[512,256]{1,0:T(8,128)(2,1)S(1)} %collective-permute-done.10.refs_8_), channel_id=1, source_target_pairs={{0,16},{16,32},{32,48},{48,64},{64,80},{80,96},{96,112},{112,0},{1... | collective-permute-start | bytes 786440 | tf_op jit(solution)/shard_map/ppermute | solution.py:21
  52.7 5.6 %collective-permute-done.12.refs_7_ = bf16[512,256]{1,0:T(8,128)(2,1)S(1)} collective-permute-done((bf16[512,256]{1,0:T(8,128)(2,1)S(1)}, bf16[512,256]{1,0:T(8,128)(2,1)S(1)}, u32[]{:S(2)}, u32[]{:S(2)}) %collective-permute-start.12) | collective-permute-done | bytes 262176 | tf_op jit(solution)/shard_map/ppermute | solution.py:21
  58.4 3.0 %collective-permute-done.13.refs_2_ = bf16[512,256]{1,0:T(8,128)(2,1)S(1)} collective-permute-done((bf16[512,256]{1,0:T(8,128)(2,1)S(1)}, bf16[512,256]{1,0:T(8,128)(2,1)S(1)}, u32[]{:S(2)}, u32[]{:S(2)}) %collective-permute-start.13) | collective-permute-done | bytes 262176 | tf_op jit(solution)/shard_map/ppermute | solution.py:21
  65.7 3.5 %collective-permute-start.20 = (bf16[128,512]{1,0:T(8,128)(2,1)S(1)}, bf16[128,512]{1,0:T(8,128)(2,1)S(1)}, u32[]{:S(2)}, u32[]{:S(2)}) collective-permute-start(bf16[128,512]{1,0:T(8,128)(2,1)S(1)} %get-tuple-element.142), channel_id=1, source_target_pairs={{0,16},{16,32},{32,48},{48,64},{64,80},{80,96},{96,112},{112,0},{1... | collective-permute-start | bytes 393224 | tf_op jit(solution)/shard_map/ppermute | solution.py:21
  69.1 3.4 %shard_map.135 = (f32[6,256,512]{2,1,0:T(8,128)S(1)}, f32[256,512]{1,0:T(8,128)S(1)}) custom-call(s32[1]{0:T(128)} %bitcast.pos_ref, bf16[8,512,512]{2,1,0:T(8,128)(2,1)S(1)} %get-tuple-element.59.own_ref, bf16[8,512,512]{2,1,0:T(8,128)(2,1)S(1)} %shard_map.131.peer_ref, bf16[256,512]{1,0:T(8,128)(2,1)S(1)} %get-tuple-element.65.mine_ref, ...), custom_call_target="tpu_custom_call" | custom-call | flops 1879048192 | bytes 1048576 | tf_op jit(solution)/shard_map/pallas_call | solution.py:51
  74.4 2.7 %collective-permute-start.22 = (bf16[256,512]{1,0:T(8,128)(2,1)S(1)}, bf16[256,512]{1,0:T(8,128)(2,1)S(1)}, u32[]{:S(2)}, u32[]{:S(2)}) collective-permute-start(bf16[256,512]{1,0:T(8,128)(2,1)S(1)} %pad_maximum_fusion.2), channel_id=1, source_target_pairs={{0,16},{16,32},{32,48},{48,64},{64,80},{80,96},{96,112},{112,0},{1... | collective-permute-start | bytes 786440 | tf_op jit(solution)/shard_map/ppermute | solution.py:21
  81.0 2.8 %collective-permute-start.24 = (bf16[256,512]{1,0:T(8,128)(2,1)S(1)}, bf16[256,512]{1,0:T(8,128)(2,1)S(1)}, u32[]{:S(2)}, u32[]{:S(2)}) collective-permute-start(bf16[256,512]{1,0:T(8,128)(2,1)S(1)} %get-tuple-element.130), channel_id=1, source_target_pairs={{0,16},{16,32},{32,48},{48,64},{64,80},{80,96},{96,112},{112,0},{1... | collective-permute-start | bytes 786440 | tf_op jit(solution)/shard_map/ppermute | solution.py:21
  83.9 3.8 %shard_map.133 = (f32[512,256]{1,0:T(8,128)S(1)}, bf16[512,256]{1,0:T(8,128)(2,1)S(1)}) custom-call(s32[1]{0:T(128)} %bitcast.pos_ref, bf16[8,512,512]{2,1,0:T(8,128)(2,1)S(1)} %get-tuple-element.59.own_ref, bf16[8,512,512]{2,1,0:T(8,128)(2,1)S(1)} %shard_map.131.peer_ref, bf16[512,256]{1,0:T(8,128)(2,1)S(1)} %shard_map.128.refs_0_.gated_ref, ...), custom_call_target="tpu_custom_call" | custom-call | flops 2147483648 | bytes 1048576 | tf_op jit(solution)/shard_map/pallas_call | solution.py:51
  93.4 10.9 %collective-permute-start.19 = (bf16[512,256]{1,0:T(8,128)(2,1)S(1)}, bf16[512,256]{1,0:T(8,128)(2,1)S(1)}, u32[]{:S(2)}, u32[]{:S(2)}) collective-permute-start(bf16[512,256]{1,0:T(8,128)(2,1)S(1)} %shard_map.134.refs_1_), channel_id=1, source_target_pairs={{0,1},{1,2},{2,3},{3,4},{4,5},{5,6},{6,7},{7,8},{8,9},{9,10},{10,1... | collective-permute-start | bytes 786440 | tf_op jit(solution)/shard_map/ppermute | solution.py:39
  104.3 3.3 %collective-permute-done.19.refs_2_ = bf16[512,256]{1,0:T(8,128)(2,1)S(1)} collective-permute-done((bf16[512,256]{1,0:T(8,128)(2,1)S(1)}, bf16[512,256]{1,0:T(8,128)(2,1)S(1)}, u32[]{:S(2)}, u32[]{:S(2)}) %collective-permute-start.19) | collective-permute-done | bytes 262176 | tf_op jit(solution)/shard_map/ppermute | solution.py:39
  107.6 2.6 %shard_map.136 = (f32[512,256]{1,0:T(8,128)S(1)}, bf16[512,256]{1,0:T(8,128)(2,1)S(1)}, f32[768,128]{1,0:T(8,128)S(1)}) custom-call(s32[2]{0:T(128)S(1)} %copy-done.6, bf16[512,256]{1,0:T(8,128)(2,1)S(1)} %shard_map.134.refs_1_, bf16[512,256]{1,0:T(8,128)(2,1)S(1)} %collective-permute-done.19.refs_2_, bf16[512,256]{1,0:T(8,128)(2,1)S(1)} %bitcast.77, ...), custom_call_target="tpu_custom_call" | custom-call | flops 536870912 | bytes 4194304 | tf_op jit(solution)/shard_map/pallas_call | solution.py:51
  116.4 7.2 %collective-permute-done.28.later_ref = bf16[512,256]{1,0:T(8,128)(2,1)S(1)} collective-permute-done((bf16[512,256]{1,0:T(8,128)(2,1)S(1)}, bf16[512,256]{1,0:T(8,128)(2,1)S(1)}, u32[]{:S(2)}, u32[]{:S(2)}) %collective-permute-start.28) | collective-permute-done | bytes 262176 | tf_op jit(solution)/shard_map/ppermute | solution.py:39
  126.4 3.1 %collective-permute-start.31 = (bf16[128,512]{1,0:T(8,128)(2,1)S(1)}, bf16[128,512]{1,0:T(8,128)(2,1)S(1)}, u32[]{:S(2)}, u32[]{:S(2)}) collective-permute-start(bf16[128,512]{1,0:T(8,128)(2,1)S(1)} %get-tuple-element.140), channel_id=1, source_target_pairs={{0,16},{16,32},{32,48},{48,64},{64,80},{80,96},{96,112},{112,0},{1... | collective-permute-start | bytes 393224 | tf_op jit(solution)/shard_map/ppermute | solution.py:21
  129.5 3.4 %shard_map.139 = (f32[6,256,512]{2,1,0:T(8,128)S(1)}, f32[256,512]{1,0:T(8,128)S(1)}) custom-call(s32[1]{0:T(128)} %bitcast.pos_ref, bf16[8,512,512]{2,1,0:T(8,128)(2,1)S(1)} %get-tuple-element.59.own_ref, bf16[8,512,512]{2,1,0:T(8,128)(2,1)S(1)} %shard_map.131.peer_ref, bf16[256,512]{1,0:T(8,128)(2,1)S(1)} %get-tuple-element.90.mine_ref, ...), custom_call_target="tpu_custom_call" | custom-call | flops 1879048192 | bytes 1048576 | tf_op jit(solution)/shard_map/pallas_call | solution.py:51
  135.7 2.7 %collective-permute-start.33 = (bf16[256,512]{1,0:T(8,128)(2,1)S(1)}, bf16[256,512]{1,0:T(8,128)(2,1)S(1)}, u32[]{:S(2)}, u32[]{:S(2)}) collective-permute-start(bf16[256,512]{1,0:T(8,128)(2,1)S(1)} %pad_maximum_fusion.4), channel_id=1, source_target_pairs={{0,16},{16,32},{32,48},{48,64},{64,80},{80,96},{96,112},{112,0},{1... | collective-permute-start | bytes 786440 | tf_op jit(solution)/shard_map/ppermute | solution.py:21
  138.4 6.1 %collective-permute-done.34 = bf16[256,512]{1,0:T(8,128)(2,1)S(1)} collective-permute-done((bf16[256,512]{1,0:T(8,128)(2,1)S(1)}, bf16[256,512]{1,0:T(8,128)(2,1)S(1)}, u32[]{:S(2)}, u32[]{:S(2)}) %collective-permute-start.34) | collective-permute-done | bytes 262176 | tf_op jit(solution)/shard_map/ppermute | solution.py:21
  144.7 2.6 %collective-permute-start.35 = (bf16[256,512]{1,0:T(8,128)(2,1)S(1)}, bf16[256,512]{1,0:T(8,128)(2,1)S(1)}, u32[]{:S(2)}, u32[]{:S(2)}) collective-permute-start(bf16[256,512]{1,0:T(8,128)(2,1)S(1)} %get-tuple-element.124), channel_id=1, source_target_pairs={{0,16},{16,32},{32,48},{48,64},{64,80},{80,96},{96,112},{112,0},{1... | collective-permute-start | bytes 786440 | tf_op jit(solution)/shard_map/ppermute | solution.py:21
  147.3 4.3 %collective-permute-done.35 = bf16[256,512]{1,0:T(8,128)(2,1)S(1)} collective-permute-done((bf16[256,512]{1,0:T(8,128)(2,1)S(1)}, bf16[256,512]{1,0:T(8,128)(2,1)S(1)}, u32[]{:S(2)}, u32[]{:S(2)}) %collective-permute-start.35) | collective-permute-done | bytes 262176 | tf_op jit(solution)/shard_map/ppermute | solution.py:21
  151.6 3.1 %collective-permute-done.36 = bf16[256,512]{1,0:T(8,128)(2,1)S(1)} collective-permute-done((bf16[256,512]{1,0:T(8,128)(2,1)S(1)}, bf16[256,512]{1,0:T(8,128)(2,1)S(1)}, u32[]{:S(2)}, u32[]{:S(2)}) %collective-permute-start.36) | collective-permute-done | bytes 262176 | tf_op jit(solution)/shard_map/ppermute | solution.py:21
  156.4 3.8 %collective-permute-done.37.refs_5_ = bf16[256,512]{1,0:T(8,128)(2,1)S(1)} collective-permute-done((bf16[256,512]{1,0:T(8,128)(2,1)S(1)}, bf16[256,512]{1,0:T(8,128)(2,1)S(1)}, u32[]{:S(2)}, u32[]{:S(2)}) %collective-permute-start.37) | collective-permute-done | bytes 262176 | tf_op jit(solution)/shard_map/ppermute | solution.py:21
  161.7 2.6 %shard_map.140 = (f32[512,256]{1,0:T(8,128)S(1)}, bf16[512,256]{1,0:T(8,128)(2,1)S(1)}, bf16[16,96,128]{2,1,0:T(8,128)(2,1)S(1)}) custom-call(s32[2]{0:T(128)S(1)} %copy-done.6, bf16[512,256]{1,0:T(8,128)(2,1)S(1)} %bitcast.75, bf16[512,256]{1,0:T(8,128)(2,1)S(1)} %collective-permute-done.prior_ref.refs_2_, f32[512,256]{1,0:T(8,128)S(1)} %get-tuple-element.89.refs_3_, ...), custom_call_target="tpu_custom_call" | custom-call | flops 536870912 | bytes 4194304 | tf_op jit(solution)/shard_map/pallas_call | solution.py:51
  164.3 18.6 %all_to_all.15 = bf16[16,96,128]{2,1,0:T(8,128)(2,1)S(1)} all-to-all(bf16[16,96,128]{2,1,0:T(8,128)(2,1)S(1)} %get-tuple-element.106), channel_id=1, replica_groups=mesh['firm'=16,'tm'=16] {'tm'}, dimensions={0} | all-to-all | bytes 786432 | tf_op jit(solution)/shard_map/all_to_all | solution.py:427
  183.7 5.7 %all-to-all-start.1 = ((bf16[16,96,128]{2,1,0:T(8,128)(2,1)}), bf16[16,96,128]{2,1,0:T(8,128)(2,1)S(1)}, u32[]{:S(2)}, u32[]{:S(2)}) async-start(bf16[16,96,128]{2,1,0:T(8,128)(2,1)} %broadcast_in_dim.10), calls=%async_computation.1 | async-start | bytes 786432 | tf_op jit(solution)/shard_map/all_to_all | solution.py:427
  189.5 3.0 %collective-permute-start.39 = (bf16[512,256]{1,0:T(8,128)(2,1)S(1)}, bf16[512,256]{1,0:T(8,128)(2,1)S(1)}, u32[]{:S(2)}, u32[]{:S(2)}) collective-permute-start(bf16[512,256]{1,0:T(8,128)(2,1)S(1)} %get-tuple-element.105), channel_id=1, source_target_pairs={{1,0},{2,1},{3,2},{4,3},{5,4},{6,5},{7,6},{8,7},{9,8},{10,9},{11,1... | collective-permute-start | bytes 786440 | tf_op jit(solution)/shard_map/ppermute | solution.py:39
  192.6 8.3 %all-to-all-done.1 = bf16[16,96,128]{2,1,0:T(8,128)(2,1)S(1)} async-done(((bf16[16,96,128]{2,1,0:T(8,128)(2,1)}), bf16[16,96,128]{2,1,0:T(8,128)(2,1)S(1)}, u32[]{:S(2)}, u32[]{:S(2)}) %all-to-all-start.1) | async-done | bytes 393248 | tf_op jit(solution)/shard_map/all_to_all | solution.py:427
  201.7 4.9 %all-to-all-start.2 = ((bf16[16,96,128]{2,1,0:T(8,128)(2,1)}), bf16[16,96,128]{2,1,0:T(8,128)(2,1)S(1)}, u32[]{:S(2)}, u32[]{:S(2)}) async-start(bf16[16,96,128]{2,1,0:T(8,128)(2,1)} %broadcast_in_dim.11), calls=%async_computation.2 | async-start | bytes 786432 | tf_op jit(solution)/shard_map/all_to_all | solution.py:433
  207.9 8.8 %all-to-all-done.2 = bf16[16,96,128]{2,1,0:T(8,128)(2,1)S(1)} async-done(((bf16[16,96,128]{2,1,0:T(8,128)(2,1)}), bf16[16,96,128]{2,1,0:T(8,128)(2,1)S(1)}, u32[]{:S(2)}, u32[]{:S(2)}) %all-to-all-start.2) | async-done | bytes 393248 | tf_op jit(solution)/shard_map/all_to_all | solution.py:433
  (118 shorter events, 53.7 us)
Async XLA Ops:
  3.2 21.2 %collective-permute-start.1 = (bf16[512,512]{1,0:T(8,128)(2,1)S(1)}, bf16[512,512]{1,0:T(8,128)(2,1)S(1)}, u32[]{:S(2)}, u32[]{:S(2)}) collective-permute-start(bf16[512,512]{1,0:T(8,128)(2,1)S(1)} %shard_map.130), channel_id=1, source_target_pairs={{0,128},{16,144},{32,160},{48,176},{64,192},{80,208},{96,224},{112... | collective-permute-start | bytes 1572872 | tf_op jit(solution)/shard_map/ppermute | solution.py:25
  4.6 14.5 %collective-permute-start = (bf16[512,256]{1,0:T(8,128)(2,1)S(1)}, bf16[512,256]{1,0:T(8,128)(2,1)S(1)}, u32[]{:S(2)}, u32[]{:S(2)}) collective-permute-start(bf16[512,256]{1,0:T(8,128)(2,1)S(1)} %bitcast.72), channel_id=1, source_target_pairs={{0,1},{1,2},{2,3},{3,4},{4,5},{5,6},{6,7},{7,8},{8,9},{9,10},{10,1... | collective-permute-start | bytes 786440 | tf_op jit(solution)/shard_map/ppermute | solution.py:39
  24.4 11.6 %collective-permute-start.2 = (bf16[512,512]{1,0:T(8,128)(2,1)S(1)}, bf16[512,512]{1,0:T(8,128)(2,1)S(1)}, u32[]{:S(2)}, u32[]{:S(2)}) collective-permute-start(bf16[512,512]{1,0:T(8,128)(2,1)S(1)} %collective-permute-done.1.first_ref), channel_id=1, source_target_pairs={{0,4},{1,5},{2,6},{3,7},{4,8},{5,9},{6,10},{7,11},{8,12},{9,13},{1... | collective-permute-start | bytes 1572872 | tf_op jit(solution)/shard_map/ppermute | solution.py:34
  25.7 11.0 %collective-permute-start.3 = (bf16[512,512]{1,0:T(8,128)(2,1)S(1)}, bf16[512,512]{1,0:T(8,128)(2,1)S(1)}, u32[]{:S(2)}, u32[]{:S(2)}) collective-permute-start(bf16[512,512]{1,0:T(8,128)(2,1)S(1)} %collective-permute-done.1.first_ref), channel_id=1, source_target_pairs={{0,12},{1,13},{2,14},{3,15},{4,0},{5,1},{6,2},{7,3},{8,4},{9,5},{1... | collective-permute-start | bytes 1572872 | tf_op jit(solution)/shard_map/ppermute | solution.py:34
  36.8 26.1 %collective-permute-start.7 = (bf16[1024,512]{1,0:T(8,128)(2,1)S(1)}, bf16[1024,512]{1,0:T(8,128)(2,1)S(1)}, u32[]{:S(2)}, u32[]{:S(2)}) collective-permute-start(bf16[1024,512]{1,0:T(8,128)(2,1)S(1)} %constant_dynamic-update-slice_fusion.sides_ref), channel_id=1, source_target_pairs={{0,1},{1,0},{2,3},{3,2},{4,5},{5,4},{6,7},{7,6},{8,9},{9,8},{10,11... | collective-permute-start | bytes 3145736 | tf_op jit(solution)/shard_map/ppermute | solution.py:29
  36.9 8.2 %collective-permute-start.10 = (bf16[512,256]{1,0:T(8,128)(2,1)S(1)}, bf16[512,256]{1,0:T(8,128)(2,1)S(1)}, u32[]{:S(2)}, u32[]{:S(2)}) collective-permute-start(bf16[512,256]{1,0:T(8,128)(2,1)S(1)} %shard_map.128.refs_0_.gated_ref), channel_id=1, source_target_pairs={{0,16},{16,32},{32,48},{48,64},{64,80},{80,96},{96,112},{112,0},{1... | collective-permute-start | bytes 786440 | tf_op jit(solution)/shard_map/ppermute | solution.py:21
  39.8 8.4 %collective-permute-start.11 = (bf16[512,256]{1,0:T(8,128)(2,1)S(1)}, bf16[512,256]{1,0:T(8,128)(2,1)S(1)}, u32[]{:S(2)}, u32[]{:S(2)}) collective-permute-start(bf16[512,256]{1,0:T(8,128)(2,1)S(1)} %shard_map.128.refs_0_.gated_ref), channel_id=1, source_target_pairs={{0,112},{16,0},{32,16},{48,32},{64,48},{80,64},{96,80},{112,96},{1... | collective-permute-start | bytes 786440 | tf_op jit(solution)/shard_map/ppermute | solution.py:21
  39.9 8.5 %collective-permute-start.4 = (bf16[256,512]{1,0:T(8,128)(2,1)S(1)}, bf16[256,512]{1,0:T(8,128)(2,1)S(1)}, u32[]{:S(2)}, u32[]{:S(2)}) collective-permute-start(bf16[256,512]{1,0:T(8,128)(2,1)S(1)} %slice.91), channel_id=1, source_target_pairs={{0,4},{1,5},{2,6},{3,7},{4,8},{5,9},{6,10},{7,11},{8,12},{9,13},{1... | collective-permute-start | bytes 786440 | tf_op jit(solution)/shard_map/ppermute | solution.py:34
  41.1 7.2 %collective-permute-start.5 = (bf16[256,512]{1,0:T(8,128)(2,1)S(1)}, bf16[256,512]{1,0:T(8,128)(2,1)S(1)}, u32[]{:S(2)}, u32[]{:S(2)}) collective-permute-start(bf16[256,512]{1,0:T(8,128)(2,1)S(1)} %slice.92), channel_id=1, source_target_pairs={{0,12},{1,13},{2,14},{3,15},{4,0},{5,1},{6,2},{7,3},{8,4},{9,5},{1... | collective-permute-start | bytes 786440 | tf_op jit(solution)/shard_map/ppermute | solution.py:34
  45.1 16.8 %collective-permute-start.6 = (bf16[512,512]{1,0:T(8,128)(2,1)S(1)}, bf16[512,512]{1,0:T(8,128)(2,1)S(1)}, u32[]{:S(2)}, u32[]{:S(2)}) collective-permute-start(bf16[512,512]{1,0:T(8,128)(2,1)S(1)} %collective-permute-done.1.first_ref), channel_id=1, source_target_pairs={{0,1},{1,0},{2,3},{3,2},{4,5},{5,4},{6,7},{7,6},{8,9},{9,8},{10,11... | collective-permute-start | bytes 1572872 | tf_op jit(solution)/shard_map/ppermute | solution.py:29
  48.4 14.5 %collective-permute-start.8 = (bf16[512,512]{1,0:T(8,128)(2,1)S(1)}, bf16[512,512]{1,0:T(8,128)(2,1)S(1)}, u32[]{:S(2)}, u32[]{:S(2)}) collective-permute-start(bf16[512,512]{1,0:T(8,128)(2,1)S(1)} %pad_maximum_fusion), channel_id=1, source_target_pairs={{0,1},{1,0},{2,3},{3,2},{4,5},{5,4},{6,7},{7,6},{8,9},{9,8},{10,11... | collective-permute-start | bytes 1572872 | tf_op jit(solution)/shard_map/ppermute | solution.py:29
  50.0 8.2 %collective-permute-start.12 = (bf16[512,256]{1,0:T(8,128)(2,1)S(1)}, bf16[512,256]{1,0:T(8,128)(2,1)S(1)}, u32[]{:S(2)}, u32[]{:S(2)}) collective-permute-start(bf16[512,256]{1,0:T(8,128)(2,1)S(1)} %collective-permute-done.10.refs_8_), channel_id=1, source_target_pairs={{0,16},{16,32},{32,48},{48,64},{64,80},{80,96},{96,112},{112,0},{1... | collective-permute-start | bytes 786440 | tf_op jit(solution)/shard_map/ppermute | solution.py:21
  52.7 8.7 %collective-permute-start.13 = (bf16[512,256]{1,0:T(8,128)(2,1)S(1)}, bf16[512,256]{1,0:T(8,128)(2,1)S(1)}, u32[]{:S(2)}, u32[]{:S(2)}) collective-permute-start(bf16[512,256]{1,0:T(8,128)(2,1)S(1)} %collective-permute-done.11.refs_1_), channel_id=1, source_target_pairs={{0,112},{16,0},{32,16},{48,32},{64,48},{80,64},{96,80},{112,96},{1... | collective-permute-start | bytes 786440 | tf_op jit(solution)/shard_map/ppermute | solution.py:21
  58.3 6.9 %collective-permute-start.9 = (bf16[256,512]{1,0:T(8,128)(2,1)S(1)}, bf16[256,512]{1,0:T(8,128)(2,1)S(1)}, u32[]{:S(2)}, u32[]{:S(2)}) collective-permute-start(bf16[256,512]{1,0:T(8,128)(2,1)S(1)} %get-tuple-element.65.mine_ref), channel_id=1, source_target_pairs={{0,128},{16,144},{32,160},{48,176},{64,192},{80,208},{96,224},{112... | collective-permute-start | bytes 786440 | tf_op jit(solution)/shard_map/ppermute | solution.py:25
  61.4 15.7 %collective-permute-start.14 = (bf16[512,256]{1,0:T(8,128)(2,1)S(1)}, bf16[512,256]{1,0:T(8,128)(2,1)S(1)}, u32[]{:S(2)}, u32[]{:S(2)}) collective-permute-start(bf16[512,256]{1,0:T(8,128)(2,1)S(1)} %collective-permute-done.12.refs_7_), channel_id=1, source_target_pairs={{0,16},{16,32},{32,48},{48,64},{64,80},{80,96},{96,112},{112,0},{1... | collective-permute-start | bytes 786440 | tf_op jit(solution)/shard_map/ppermute | solution.py:21
  61.9 15.3 %collective-permute-start.15 = (bf16[512,256]{1,0:T(8,128)(2,1)S(1)}, bf16[512,256]{1,0:T(8,128)(2,1)S(1)}, u32[]{:S(2)}, u32[]{:S(2)}) collective-permute-start(bf16[512,256]{1,0:T(8,128)(2,1)S(1)} %collective-permute-done.13.refs_2_), channel_id=1, source_target_pairs={{0,112},{16,0},{32,16},{48,32},{64,48},{80,64},{96,80},{112,96},{1... | collective-permute-start | bytes 786440 | tf_op jit(solution)/shard_map/ppermute | solution.py:21
  65.7 7.2 %collective-permute-start.20 = (bf16[128,512]{1,0:T(8,128)(2,1)S(1)}, bf16[128,512]{1,0:T(8,128)(2,1)S(1)}, u32[]{:S(2)}, u32[]{:S(2)}) collective-permute-start(bf16[128,512]{1,0:T(8,128)(2,1)S(1)} %get-tuple-element.142), channel_id=1, source_target_pairs={{0,16},{16,32},{32,48},{48,64},{64,80},{80,96},{96,112},{112,0},{1... | collective-permute-start | bytes 393224 | tf_op jit(solution)/shard_map/ppermute | solution.py:21
  77.2 6.7 %collective-permute-start.16 = (bf16[512,128]{1,0:T(8,128)(2,1)S(1)}, bf16[512,128]{1,0:T(8,128)(2,1)S(1)}, u32[]{:S(2)}, u32[]{:S(2)}) collective-permute-start(bf16[512,128]{1,0:T(8,128)(2,1)S(1)} %slice.93), channel_id=1, source_target_pairs={{0,16},{16,32},{32,48},{48,64},{64,80},{80,96},{96,112},{112,0},{1... | collective-permute-start | bytes 393224 | tf_op jit(solution)/shard_map/ppermute | solution.py:21
  81.0 7.9 %collective-permute-start.24 = (bf16[256,512]{1,0:T(8,128)(2,1)S(1)}, bf16[256,512]{1,0:T(8,128)(2,1)S(1)}, u32[]{:S(2)}, u32[]{:S(2)}) collective-permute-start(bf16[256,512]{1,0:T(8,128)(2,1)S(1)} %get-tuple-element.130), channel_id=1, source_target_pairs={{0,16},{16,32},{32,48},{48,64},{64,80},{80,96},{96,112},{112,0},{1... | collective-permute-start | bytes 786440 | tf_op jit(solution)/shard_map/ppermute | solution.py:21
  90.5 13.9 %collective-permute-start.26 = (bf16[256,512]{1,0:T(8,128)(2,1)S(1)}, bf16[256,512]{1,0:T(8,128)(2,1)S(1)}, u32[]{:S(2)}, u32[]{:S(2)}) collective-permute-start(bf16[256,512]{1,0:T(8,128)(2,1)S(1)} %get-tuple-element.128), channel_id=1, source_target_pairs={{0,16},{16,32},{32,48},{48,64},{64,80},{80,96},{96,112},{112,0},{1... | collective-permute-start | bytes 786440 | tf_op jit(solution)/shard_map/ppermute | solution.py:21
  92.3 12.1 %collective-permute-start.27 = (bf16[256,512]{1,0:T(8,128)(2,1)S(1)}, bf16[256,512]{1,0:T(8,128)(2,1)S(1)}, u32[]{:S(2)}, u32[]{:S(2)}) collective-permute-start(bf16[256,512]{1,0:T(8,128)(2,1)S(1)} %get-tuple-element.127), channel_id=1, source_target_pairs={{0,112},{16,0},{32,16},{48,32},{64,48},{80,64},{96,80},{112,96},{1... | collective-permute-start | bytes 786440 | tf_op jit(solution)/shard_map/ppermute | solution.py:21
  93.4 14.2 %collective-permute-start.19 = (bf16[512,256]{1,0:T(8,128)(2,1)S(1)}, bf16[512,256]{1,0:T(8,128)(2,1)S(1)}, u32[]{:S(2)}, u32[]{:S(2)}) collective-permute-start(bf16[512,256]{1,0:T(8,128)(2,1)S(1)} %shard_map.134.refs_1_), channel_id=1, source_target_pairs={{0,1},{1,2},{2,3},{3,4},{4,5},{5,6},{6,7},{7,8},{8,9},{9,10},{10,1... | collective-permute-start | bytes 786440 | tf_op jit(solution)/shard_map/ppermute | solution.py:39
  110.5 13.1 %collective-permute-start.28 = (bf16[512,256]{1,0:T(8,128)(2,1)S(1)}, bf16[512,256]{1,0:T(8,128)(2,1)S(1)}, u32[]{:S(2)}, u32[]{:S(2)}) collective-permute-start(bf16[512,256]{1,0:T(8,128)(2,1)S(1)} %get-tuple-element.88), channel_id=1, source_target_pairs={{1,0},{2,1},{3,2},{4,3},{5,4},{6,5},{7,6},{8,7},{9,8},{10,9},{11,1... | collective-permute-start | bytes 786440 | tf_op jit(solution)/shard_map/ppermute | solution.py:39
  112.4 12.6 %collective-permute-start.30 = (bf16[512,256]{1,0:T(8,128)(2,1)S(1)}, bf16[512,256]{1,0:T(8,128)(2,1)S(1)}, u32[]{:S(2)}, u32[]{:S(2)}) collective-permute-start(bf16[512,256]{1,0:T(8,128)(2,1)S(1)} %get-tuple-element.88), channel_id=1, source_target_pairs={{129,0},{130,1},{131,2},{132,3},{133,4},{134,5},{135,6},{136,7},{1... | collective-permute-start | bytes 786440 | tf_op jit(solution)/shard_map/ppermute | solution.py:460
  126.4 6.8 %collective-permute-start.31 = (bf16[128,512]{1,0:T(8,128)(2,1)S(1)}, bf16[128,512]{1,0:T(8,128)(2,1)S(1)}, u32[]{:S(2)}, u32[]{:S(2)}) collective-permute-start(bf16[128,512]{1,0:T(8,128)(2,1)S(1)} %get-tuple-element.140), channel_id=1, source_target_pairs={{0,16},{16,32},{32,48},{48,64},{64,80},{80,96},{96,112},{112,0},{1... | collective-permute-start | bytes 393224 | tf_op jit(solution)/shard_map/ppermute | solution.py:21
  135.6 8.9 %collective-permute-start.34 = (bf16[256,512]{1,0:T(8,128)(2,1)S(1)}, bf16[256,512]{1,0:T(8,128)(2,1)S(1)}, u32[]{:S(2)}, u32[]{:S(2)}) collective-permute-start(bf16[256,512]{1,0:T(8,128)(2,1)S(1)} %pad_maximum_fusion.5), channel_id=1, source_target_pairs={{0,112},{16,0},{32,16},{48,32},{64,48},{80,64},{96,80},{112,96},{1... | collective-permute-start | bytes 786440 | tf_op jit(solution)/shard_map/ppermute | solution.py:21
  135.7 8.8 %collective-permute-start.33 = (bf16[256,512]{1,0:T(8,128)(2,1)S(1)}, bf16[256,512]{1,0:T(8,128)(2,1)S(1)}, u32[]{:S(2)}, u32[]{:S(2)}) collective-permute-start(bf16[256,512]{1,0:T(8,128)(2,1)S(1)} %pad_maximum_fusion.4), channel_id=1, source_target_pairs={{0,16},{16,32},{32,48},{48,64},{64,80},{80,96},{96,112},{112,0},{1... | collective-permute-start | bytes 786440 | tf_op jit(solution)/shard_map/ppermute | solution.py:21
  144.7 6.9 %collective-permute-start.35 = (bf16[256,512]{1,0:T(8,128)(2,1)S(1)}, bf16[256,512]{1,0:T(8,128)(2,1)S(1)}, u32[]{:S(2)}, u32[]{:S(2)}) collective-permute-start(bf16[256,512]{1,0:T(8,128)(2,1)S(1)} %get-tuple-element.124), channel_id=1, source_target_pairs={{0,16},{16,32},{32,48},{48,64},{64,80},{80,96},{96,112},{112,0},{1... | collective-permute-start | bytes 786440 | tf_op jit(solution)/shard_map/ppermute | solution.py:21
  147.3 7.4 %collective-permute-start.36 = (bf16[256,512]{1,0:T(8,128)(2,1)S(1)}, bf16[256,512]{1,0:T(8,128)(2,1)S(1)}, u32[]{:S(2)}, u32[]{:S(2)}) collective-permute-start(bf16[256,512]{1,0:T(8,128)(2,1)S(1)} %get-tuple-element.123), channel_id=1, source_target_pairs={{0,112},{16,0},{32,16},{48,32},{64,48},{80,64},{96,80},{112,96},{1... | collective-permute-start | bytes 786440 | tf_op jit(solution)/shard_map/ppermute | solution.py:21
  183.7 17.1 %all-to-all-start.1 = ((bf16[16,96,128]{2,1,0:T(8,128)(2,1)}), bf16[16,96,128]{2,1,0:T(8,128)(2,1)S(1)}, u32[]{:S(2)}, u32[]{:S(2)}) async-start(bf16[16,96,128]{2,1,0:T(8,128)(2,1)} %broadcast_in_dim.10), calls=%async_computation.1 | async-start | bytes 786432 | tf_op jit(solution)/shard_map/all_to_all | solution.py:427
  189.5 17.1 %collective-permute-start.39 = (bf16[512,256]{1,0:T(8,128)(2,1)S(1)}, bf16[512,256]{1,0:T(8,128)(2,1)S(1)}, u32[]{:S(2)}, u32[]{:S(2)}) collective-permute-start(bf16[512,256]{1,0:T(8,128)(2,1)S(1)} %get-tuple-element.105), channel_id=1, source_target_pairs={{1,0},{2,1},{3,2},{4,3},{5,4},{6,5},{7,6},{8,7},{9,8},{10,9},{11,1... | collective-permute-start | bytes 786440 | tf_op jit(solution)/shard_map/ppermute | solution.py:39
  201.7 15.0 %all-to-all-start.2 = ((bf16[16,96,128]{2,1,0:T(8,128)(2,1)}), bf16[16,96,128]{2,1,0:T(8,128)(2,1)S(1)}, u32[]{:S(2)}, u32[]{:S(2)}) async-start(bf16[16,96,128]{2,1,0:T(8,128)(2,1)} %broadcast_in_dim.11), calls=%async_computation.2 | async-start | bytes 786432 | tf_op jit(solution)/shard_map/all_to_all | solution.py:433
  (19 other events, 163.4 us)
